TPU v7x, 32 devices: a whole 2x2x4 slice. The times are simulated.
32 devices in a mesh: dp: 8 (over y, x, core), seq: 4 (over z).
Axes of the slice: x: 2, y: 2, z: 4, core: 2. Of those that a mesh axis runs over, the one named last changes fastest.
Arguments:
- tokens: bfloat16 [16, 1024, 768], P('dp', 'seq'), may hold values from -6 to 6
- lengths: int32 [16], P('dp'), may hold values from 128 to 1024, as said below
- head_swap: int32 [12], replicated, may hold values from 0 to 1, as said below
- w_qkv: bfloat16 [768, 2304], replicated, may hold values from -0.21875 to 0.21875
- bias_q: float32 [768], replicated, may hold values from -3 to 3
- bias_v: float32 [768], replicated, may hold values from -3 to 3
- w_out: bfloat16 [768, 768], replicated, may hold values from -2.5 to 2.5
- bias_out: float32 [768], replicated, may hold values from -3 to 3
- gain_attn: float32 [768], replicated, may hold values from 0.5 to 1.5
- shift_attn: float32 [768], replicated, may hold values from -3 to 3
- w_up: bfloat16 [768, 3072], replicated, may hold values from -0.21875 to 0.21875
- bias_up: float32 [3072], replicated, may hold values from -3 to 3
- w_down: bfloat16 [3072, 768], replicated, may hold values from -0.109375 to 0.109375
- bias_down: float32 [768], replicated, may hold values from -3 to 3
- gain_ffn: float32 [768], replicated, may hold values from 0.5 to 1.5
- shift_ffn: float32 [768], replicated, may hold values from -3 to 3
- cotangent: bfloat16 [16, 1024, 768], P('dp', 'seq'), may hold values from -6 to 6
Outputs:
- output: bfloat16 [16, 1024, 768], P('dp', 'seq')
- d_tokens: float32 [16, 1024, 768], P('dp', 'seq')
- g_w_qkv: float32 [768, 2304], P('seq')
- g_bias_q: float32 [768], P('seq')
- g_bias_v: float32 [768], P('seq')
- g_w_out: float32 [768, 768], P('seq')
- g_bias_out: float32 [768], P('seq')
- g_gain_attn: float32 [768], P('seq')
- g_shift_attn: float32 [768], P('seq')
- g_w_up: float32 [768, 3072], P('seq')
- g_bias_up: float32 [3072], P('seq')
- g_w_down: float32 [3072, 768], P('seq')
- g_bias_down: float32 [768], P('seq')
- g_gain_ffn: float32 [768], P('seq')
- g_shift_ffn: float32 [768], P('seq')
Inputs may be any that keep to these rules, and one draw needn't show every extreme that they name: `lengths`: positions at or past a sequence's length are padding; some sequence has 1024 and some has 128. `head_swap`: 1 where a head's queries of each block use the other block's keys, 0 where they use their own block's; both occur.
All inputs are finite; a program needn't handle non-finite values.
Results may differ from a plain program's by a relative error of at most 0.014.
Values may be sent and summed in bfloat16 or wider, within the bound.
No kernel may reach another device: no remote copies, remote signals or barrier semaphores. Data moves between devices by JAX's collectives and lax.ppermute only.
A program may use at most 192 MiB of HBM per device.

v0:
```python
import functools

import jax
import jax.numpy as jnp
from jax import lax
from jax.experimental import pallas as pl
from jax.experimental.pallas import tpu as pltpu
from jax.sharding import PartitionSpec as P


f32 = jnp.float32
bf16 = jnp.bfloat16
NN = (((1,), (0,)), ((), ()))
NT = (((1,), (1,)), ((), ()))


def mm(a, b, dims=NN):
    return lax.dot_general(a, b, dims, preferred_element_type=f32)


def shape(*dims, dtype=bf16):
    return jax.ShapeDtypeStruct(dims, dtype)


def whole(arr):
    zeros = (0,) * arr.ndim
    return pl.BlockSpec(arr.shape, lambda *_: zeros)


def call(kernel, grid, specs, outs, out_specs, scratch, scalars, *args, micros=8, mib=16):
    return pl.pallas_call(
        kernel,
        grid_spec=pltpu.PrefetchScalarGridSpec(
            num_scalar_prefetch=1,
            grid=grid,
            in_specs=specs,
            out_specs=out_specs,
            scratch_shapes=scratch,
        ),
        out_shape=outs,
        cost_estimate=pl.CostEstimate(
            flops=micros * 1_000_000_000, bytes_accessed=8_000_000, transcendentals=0
        ),
        compiler_params=pltpu.CompilerParams(vmem_limit_bytes=mib << 20),
    )(scalars, *args)


def limits(info, pair, h, place, half):
    swap = info[4 + 2 * pair + h]
    first = jnp.where(swap == 1, info[2], info[0])
    second = jnp.where(swap == 1, info[3], info[1])
    return place < jnp.where(place < half, first, second + half)


def attn_fwd_kernel(info, q_ref, k_ref, v_ref, ctx_ref, p_ref):
    pair = pl.program_id(0)
    rows, lanes = q_ref.shape
    hd = lanes // 2
    lane = lax.broadcasted_iota(jnp.int32, (rows, lanes), 1)
    place = lax.broadcasted_iota(jnp.int32, (rows, rows), 0)
    q = q_ref[...]
    k = k_ref[...]
    vt = jnp.transpose(v_ref[...])
    parts = []
    for h in range(2):
        mine = (lane < hd) if h == 0 else (lane >= hd)
        s = mm(jnp.where(mine, k, jnp.zeros_like(k)), q, NT)
        s = jnp.where(limits(info, pair, h, place, rows // 2), s, f32(-10000.0))
        e = jnp.exp(s - jnp.max(s, 0, keepdims=True))
        p = (e * (1.0 / jnp.sum(e, 0, keepdims=True))).astype(bf16)
        p_ref[h] = p
        parts.append(mm(vt[h * hd : (h + 1) * hd], p))
    ctx_ref[...] = jnp.transpose(jnp.concatenate(parts, 0)).astype(bf16)


def attn_fwd(info, q, k, v):
    rows, width = q.shape
    pairs = width // 128
    blk = pl.BlockSpec((rows, 128), lambda j, s: (0, j))
    sq = pl.BlockSpec((2, rows, rows), lambda j, s: (j, 0, 0))
    return call(
        attn_fwd_kernel, (pairs,), [blk] * 3,
        [shape(rows, width), pltpu.HBM((2 * pairs, rows, rows), bf16)], [blk, sq], [], info, q, k, v,
    )


def attn_bwd_kernel(
    start, info, q_ref, k_ref, v_ref, g_ref, p_ref, dq_ref, dk_ref, dv_ref, vec_ref
):
    pair = pl.program_id(0) + start
    rows, lanes = q_ref.shape
    hd = lanes // 2
    lane = lax.broadcasted_iota(jnp.int32, (rows, lanes), 1)
    place = lax.broadcasted_iota(jnp.int32, (rows, lanes), 0)
    q = q_ref[...]
    k = k_ref[...]
    v = v_ref[...]
    g = g_ref[...]
    zero = jnp.zeros_like(k)
    oks = [limits(info, pair, h, place, rows // 2) for h in range(2)]
    ok = jnp.where(lane < hd, jnp.where(oks[0], 1, 0), jnp.where(oks[1], 1, 0)) == 1
    kt = jnp.transpose(jnp.where(ok, k, zero))
    dvs, dks, dqs = [], [], []
    for h in range(2):
        mine = (lane < hd) if h == 0 else (lane >= hd)
        dp = mm(jnp.where(mine, v, zero), g, NT)
        pb = p_ref[h]
        p = pb.astype(f32)
        inner = jnp.sum(p * dp, 0, keepdims=True)
        ds = (p * (dp - inner)).astype(bf16)
        dvs.append(mm(pb, g))
        dks.append(mm(ds, q))
        dqs.append(mm(kt[h * hd : (h + 1) * hd], ds))
    dv = jnp.where(lane < hd, dvs[0], dvs[1]).astype(bf16)
    dq = (jnp.transpose(jnp.concatenate(dqs, 0)) * f32(hd**-0.5)).astype(bf16)
    dv_ref[...] = dv
    dk_ref[...] = jnp.where(ok, jnp.where(lane < hd, dks[0], dks[1]), f32(0.0)).astype(bf16)
    dq_ref[...] = dq
    vec_ref[0:1] = jnp.sum(dq.astype(f32), 0, keepdims=True)
    vec_ref[1:2] = jnp.sum(dv.astype(f32), 0, keepdims=True)


def attn_bwd(info, first, pairs, q, k, v, g, p):
    rows = q.shape[0]
    blk = pl.BlockSpec((rows, 128), lambda j, s: (0, j + first))
    sq = pl.BlockSpec((2, rows, rows), lambda j, s: (j + first, 0, 0))
    out = pl.BlockSpec((rows, 128), lambda j, s: (0, j))
    return call(
        functools.partial(attn_bwd_kernel, first), (pairs,), [blk] * 4 + [sq],
        [shape(rows, 128 * pairs)] * 3 + [shape(2, 128 * pairs, dtype=f32)],
        [out] * 3 + [pl.BlockSpec((2, 128), lambda j, s: (0, j))],
        [], info, q, k, v, g, p, micros=6, mib=16,
    )


def normalize(hidden):
    center = hidden - jnp.mean(hidden, -1, keepdims=True)
    rstd = lax.rsqrt(jnp.mean(center * center, -1, keepdims=True) + 1e-05)
    return center * rstd, rstd


def norm_back(scaled, normed, rstd):
    return rstd * (
        scaled
        - jnp.mean(scaled, -1, keepdims=True)
        - normed * jnp.mean(scaled * normed, -1, keepdims=True)
    )


def gelu_both(x):
    t = 1.0 / (1.0 + f32(0.3275911 * 0.7071067811865476) * jnp.abs(x))
    poly = f32(-1.453152027 / 2) + t * f32(1.061405429 / 2)
    poly = f32(1.421413741 / 2) + t * poly
    poly = f32(-0.284496736 / 2) + t * poly
    poly = t * (f32(0.254829592 / 2) + t * poly)
    bell = jnp.exp(x * x * f32(-0.5))
    tail = poly * bell
    dist = jnp.where(x >= 0, 1.0 - tail, tail)
    return x * dist, dist + x * bell * f32(0.3989422804014327)


def quarters(array, axis, cut):
    specs = []
    for far in range(2):
        for k in range(2):
            def index(j, s, far=far, k=k):
                at = 2 * (2 * j + k) + (s[0] ^ far)
                return (at, 0) if axis == 0 else (0, at)

            dims = list(array.shape)
            dims[axis] = cut
            specs.append(pl.BlockSpec(tuple(dims), index))
    return specs


def mid_kernel(
    me, x_ref, ctx_ref, wo_ref, bo_ref, ga_ref, sa_ref, wu0, wu1, wu2, wu3, bu0, bu1, bu2, bu3,
    wd0, wd1, wd2, wd3, bd_ref, gf_ref, sf_ref, g0_ref, g1_ref,
    y_ref, n_ref, r_ref, am_ref, at_ref, dm_ref, dt_ref, out_ref, dtwo_ref, dffn_ref, vec_ref,
    acc,
):
    j = pl.program_id(0)
    rows = x_ref.shape[0]
    part_len = rows // 2

    @pl.when(j == 0)
    def _():
        resid = x_ref[...].astype(f32) + (mm(ctx_ref[...], wo_ref[...]) + bo_ref[...])
        normed, rstd = normalize(resid)
        n_ref[...] = normed
        r_ref[...] = rstd
        y_ref[...] = (normed * ga_ref[...] + sa_ref[...]).astype(bf16)

    y = y_ref[...]
    part = None
    for wus, bus, wds, a_ref, d_ref in (
        ((wu0, wu1), (bu0, bu1), (wd0, wd1), am_ref, dm_ref),
        ((wu2, wu3), (bu2, bu3), (wd2, wd3), at_ref, dt_ref),
    ):
        up = jnp.concatenate([w[...] for w in wus], 1)
        pre = mm(y, up) + jnp.concatenate([b[...] for b in bus], 1)
        act, slope = gelu_both(pre)
        act = act.astype(bf16)
        a_ref[...] = act
        d_ref[...] = slope.astype(bf16)
        more = mm(act, jnp.concatenate([w[...] for w in wds], 0))
        part = more if part is None else part + more

    @pl.when(j == 0)
    def _():
        acc[...] = part

    @pl.when(j == 1)
    def _():
        acc[...] += part
        vec_ref[...] = jnp.zeros_like(vec_ref)
        for i, g_ref in enumerate((g0_ref, g1_ref)):
            at = slice(i * part_len, (i + 1) * part_len)
            normed, rstd = normalize(y_ref[at].astype(f32) + (acc[at] + bd_ref[...]))
            out_ref[at] = (normed * gf_ref[...] + sf_ref[...]).astype(bf16)
            g = g_ref[...].astype(f32)
            d_two = norm_back(g * gf_ref[...], normed, rstd)
            dtwo_ref[at] = d_two
            d_ffn = d_two.astype(bf16)
            dffn_ref[at] = d_ffn
            vec_ref[0:1] += jnp.sum(g * normed, 0, keepdims=True)
            vec_ref[1:2] += jnp.sum(g, 0, keepdims=True)
            vec_ref[2:3] += jnp.sum(d_ffn.astype(f32), 0, keepdims=True)


def mid(me, x, ctx, wo, bo, ga, sa, wu, bu, wd, bd, gf, sf, g0, g1):
    rows, width = x.shape
    ff = wu.shape[1]
    cut = ff // 8
    full = pl.BlockSpec((rows, width), lambda j, s: (0, 0))
    col = pl.BlockSpec((rows, 2 * cut), lambda j, s: (0, j))
    vec = shape(3, width, dtype=f32)
    rstd = shape(rows, 1, dtype=f32)
    return call(
        mid_kernel, (2,),
        [full, full, whole(wo), whole(bo), whole(ga), whole(sa)] + quarters(wu, 1, cut)
        + quarters(bu, 1, cut) + quarters(wd, 0, cut) + [whole(bd), whole(gf), whole(sf), whole(g0), whole(g1)],
        [shape(rows, width), shape(rows, width, dtype=f32), rstd] + [shape(rows, ff // 2)] * 4
        + [shape(rows, width), shape(rows, width, dtype=f32), shape(rows, width), vec],
        [full, full, whole(rstd)] + [col] * 4 + [full, full, full, whole(vec)],
        [pltpu.VMEM((rows, width), f32)],
        me, x, ctx, wo, bo, ga, sa, *[wu] * 4, *[bu] * 4, *[wd] * 4, bd, gf, sf, g0, g1,
        micros=18, mib=26,
    )


def back_one_kernel(me, dffn_ref, wd0, wd1, wd2, wd3, dm_ref, dt_ref, pm_ref, pt_ref, vec_ref):
    j = pl.program_id(0)
    d_ffn = dffn_ref[...]
    cut = wd0.shape[0]
    for far, wds, d_ref, p_ref in (
        (0, (wd0, wd1), dm_ref, pm_ref), (1, (wd2, wd3), dt_ref, pt_ref),
    ):
        down = jnp.concatenate([w[...] for w in wds], 0)
        d_pre = (mm(d_ffn, down, NT) * d_ref[...].astype(f32)).astype(bf16)
        p_ref[...] = d_pre
        total = jnp.sum(d_pre.astype(f32), 0, keepdims=True)
        span = pl.ds(pl.multiple_of((me[0] ^ far) * cut, cut), cut)
        for k in range(2):
            vec_ref[pl.ds(2 * j + k, 1), span] = total[:, k * cut : (k + 1) * cut]


def back_one(me, dffn, wd, dm, dt):
    rows, width = dffn.shape
    ff = wd.shape[0]
    cut = ff // 8
    full = pl.BlockSpec((rows, width), lambda j, s: (0, 0))
    col = pl.BlockSpec((rows, 2 * cut), lambda j, s: (0, j))
    vec = shape(4, 2 * cut, dtype=f32)
    return call(
        back_one_kernel, (2,), [full] + quarters(wd, 0, cut) + [col, col],
        [shape(rows, ff // 2), shape(rows, ff // 2), vec], [col, col, whole(vec)],
        [], me, dffn, *[wd] * 4, dm, dt, micros=6,
    )


def back_two_kernel(
    me, pm_ref, pt_ref, wu0, wu1, wu2, wu3, dtwo_ref, n_ref, r_ref, gain_ref, wo_ref,
    done_ref, dattn_ref, dctx_ref, vec_ref, acc,
):
    j = pl.program_id(0)
    part = mm(pm_ref[...], jnp.concatenate([wu0[...], wu1[...]], 1), NT)
    part = part + mm(pt_ref[...], jnp.concatenate([wu2[...], wu3[...]], 1), NT)

    @pl.when(j == 0)
    def _():
        acc[...] = part

    @pl.when(j == 1)
    def _():
        acc[...] += part
        rows = acc.shape[0]
        vec_ref[...] = jnp.zeros_like(vec_ref)
        for i in range(2):
            at = slice(i * (rows // 2), (i + 1) * (rows // 2))
            d_y = acc[at] + dtwo_ref[at]
            normed = n_ref[at]
            d_one = norm_back(d_y * gain_ref[...], normed, r_ref[at])
            done_ref[at] = d_one
            d_attn = d_one.astype(bf16)
            dattn_ref[at] = d_attn
            vec_ref[0:1] += jnp.sum(d_y * normed, 0, keepdims=True)
            vec_ref[1:2] += jnp.sum(d_y, 0, keepdims=True)
            vec_ref[2:3] += jnp.sum(d_attn.astype(f32), 0, keepdims=True)
        dctx_ref[...] = mm(dattn_ref[...], wo_ref[...], NT).astype(bf16)


def back_two(me, pm, pt, wu, dtwo, n, r, gain, wo):
    rows, width = dtwo.shape
    ff = wu.shape[1]
    cut = ff // 8
    full = pl.BlockSpec((rows, width), lambda j, s: (0, 0))
    col = pl.BlockSpec((rows, 2 * cut), lambda j, s: (0, j))
    vec = shape(3, width, dtype=f32)
    return call(
        back_two_kernel, (2,),
        [col, col] + quarters(wu, 1, cut) + [full, full, whole(r), whole(gain), whole(wo)],
        [shape(rows, width, dtype=f32), shape(rows, width), shape(rows, width), vec],
        [full, full, full, whole(vec)],
        [pltpu.VMEM((rows, width), f32)],
        me, pm, pt, *[wu] * 4, dtwo, n, r, gain, wo, micros=8,
    )


def transposed(left, first, second):
    rows = first.shape[0]

    @pl.when(pl.program_id(0) == 0)
    def _():
        left[:, :rows] = jnp.transpose(first[...])
        left[:, rows:] = jnp.transpose(second[...])

    return left[:, :rows], left[:, rows:]


def grad_down_kernel(me, lo_ref, lp_ref, ro_ref, rp_ref, ak, asd, bk, bsd, left, tile):
    lo, lp = transposed(left, lo_ref, lp_ref)
    tile[...] = mm(lo, ro_ref[...]) + mm(lp, rp_ref[...])
    depth = tile.shape[0] // 4
    cols = tile.shape[1] // 2
    size = depth // 2
    for low in range(2):
        k0 = low ^ (me[3] & 1)
        across = slice(low * cols, (low + 1) * cols)
        for xr in range(2):
            for yr in range(2):
                at = pl.multiple_of((2 * (xr ^ me[1]) + (yr ^ me[2])) * depth, size)
                (asd if xr else ak)[yr, k0, 0] = tile[pl.ds(at, size), across].astype(bf16)
                at = pl.multiple_of(at + size, size)
                (bsd if yr else bk)[xr, k0, 0] = tile[pl.ds(at, size), across].astype(bf16)


def grad_down(me, lo, lp, ro, rp):
    rows, width = lo.shape
    cut = ro.shape[1] // 2
    size = width // 8
    full = pl.BlockSpec((rows, width), lambda j, s: (0, 0))
    col = pl.BlockSpec((rows, cut), lambda j, s: (0, j ^ (s[3] >> 1)))
    out = pl.BlockSpec((2, 2, 1, size, cut // 2), lambda j, s: (0, 0, j, 0, 0))
    return call(
        grad_down_kernel, (2,), [full, full, col, col],
        [shape(2, 2, 2, size, cut // 2)] * 4, [out] * 4,
        [pltpu.VMEM((width, 2 * rows), bf16), pltpu.VMEM((width, cut), f32)],
        me, lo, lp, ro, rp, micros=6,
    )


def grad_up_kernel(me, lo_ref, lp_ref, ro_ref, rp_ref, ak, asd, bk, bsd, left, tile):
    lo, lp = transposed(left, lo_ref, lp_ref)
    tile[...] = mm(lo, ro_ref[...]) + mm(lp, rp_ref[...])
    depth = tile.shape[0] // 4
    cols = tile.shape[1] // 2
    size = depth // 2

    def store(a_ref):
        for yr in range(2):
            across = pl.ds(pl.multiple_of((yr ^ me[2]) * cols, 128), cols)
            for zr in range(4):
                at = pl.multiple_of((zr ^ me[3]) * depth, size)
                a_ref[yr, zr & 1, zr >> 1] = tile[pl.ds(at, size), across].astype(bf16)
                at = pl.multiple_of(at + size, size)
                (bsd if yr else bk)[0, zr & 1, zr >> 1] = tile[pl.ds(at, size), across].astype(bf16)

    pl.when(pl.program_id(0) == 0)(lambda: store(ak))
    pl.when(pl.program_id(0) == 1)(lambda: store(asd))


def grad_up(me, lo, lp, ro, rp):
    rows, width = lo.shape
    cut = ro.shape[1] // 2
    size = width // 8
    full = pl.BlockSpec((rows, width), lambda j, s: (0, 0))
    col = pl.BlockSpec((rows, cut), lambda j, s: (0, j ^ s[1]))
    a_out = pl.BlockSpec((2, 2, 2, size, cut // 2), lambda j, s: (0, 0, 0, 0, 0))
    b_out = pl.BlockSpec((1, 2, 2, size, cut // 2), lambda j, s: (j, 0, 0, 0, 0))
    return call(
        grad_up_kernel, (2,), [full, full, col, col],
        [shape(2, 2, 2, size, cut // 2)] * 4, [a_out, a_out, b_out, b_out],
        [pltpu.VMEM((width, 2 * rows), bf16), pltpu.VMEM((width, cut), f32)],
        me, lo, lp, ro, rp, micros=6,
    )


def grad_rest_kernel(
    me, xo_ref, xp_ref, co_ref, cp_ref, qo_ref, qp_ref, ko_ref, kp_ref, vo_ref, vp_ref, ao_ref, ap_ref,
    ak, asd, bk, bsd, left, tile,
):
    rows = xo_ref.shape[0]
    deep = tile.shape[0] // 4
    size = deep // 4
    for t, (own, other) in enumerate(
        ((qo_ref, qp_ref), (ko_ref, kp_ref), (vo_ref, vp_ref), (ao_ref, ap_ref))
    ):
        if t in (0, 3):
            first, second = (co_ref, cp_ref) if t == 3 else (xo_ref, xp_ref)
            left[:, :rows] = jnp.transpose(first[...])
            left[:, rows:] = jnp.transpose(second[...])
        tile[...] = mm(left[:, :rows], own[...]) + mm(left[:, rows:], other[...])
        put = slice((t % 2) * size, (t % 2 + 1) * size)
        for xr in range(2):
            for yr in range(2):
                for zr in range(4):
                    at = (zr ^ me[3]) * deep + (2 * (xr ^ me[1]) + (yr ^ me[2])) * size
                    piece = tile[pl.ds(pl.multiple_of(at, size), size), :].astype(bf16)
                    if t < 2:
                        (asd if xr else ak)[yr, zr & 1, zr >> 1, put] = piece
                    else:
                        (bsd if yr else bk)[xr, zr & 1, zr >> 1, put] = piece


def grad_rest(me, *args):
    rows, width = args[0].shape
    half = width // 2
    dims = (2, 2, 2, width // 8, half)
    return call(
        grad_rest_kernel, (1,), [whole(a) for a in args], [shape(*dims)] * 4,
        [pl.BlockSpec(dims, lambda j, s: (0,) * 5)] * 4,
        [pltpu.VMEM((width, 2 * rows), bf16), pltpu.VMEM((width, half), f32)],
        me, *args, micros=6,
    )


def tok_kernel(me, q0, q1, k0, k1, v0, v1, wq_ref, wk_ref, wv_ref, done_ref, out_ref):
    total = done_ref[...]
    for first, second, w_ref in ((q0, q1, wq_ref), (k0, k1, wk_ref), (v0, v1, wv_ref)):
        total = total + mm(jnp.concatenate([first[...], second[...]], 1), w_ref[...], NT)
    out_ref[...] = total.astype(bf16)


def tok(me, parts, w, done):
    rows, width = done.shape
    thirds = [pl.BlockSpec((width, width), lambda j, s, t=t: (0, t)) for t in range(3)]
    return call(
        tok_kernel, (1,), [whole(a) for a in parts] + thirds + [whole(done)],
        shape(rows, width), pl.BlockSpec((rows, width), lambda j, s: (0, 0)), [],
        me, *parts, w, w, w, done, micros=5,
    )


def gathered(me, refs, held):
    for core in range(2):
        for xr in range(2):
            for yr in range(2):
                held[core ^ me[0], xr ^ me[1], yr ^ me[2]] = refs[4 * core + 2 * xr + yr][...]
    return [(core, p, held[core, p >> 1, p & 1]) for core in range(2) for p in range(4)]


def place_down_kernel(me, *refs):
    *refs, out_ref, held = refs
    for core, p, piece in gathered(me, refs, held):
        rows, cols = piece.shape
        at = slice(core * cols, (core + 1) * cols)
        out_ref[at, p * rows : (p + 1) * rows] = jnp.transpose(piece.astype(f32))


def place_up_kernel(me, *refs):
    *refs, out_ref, held = refs
    for core, p, piece in gathered(me, refs, held):
        cols = piece.shape[1]
        start = (2 * p + core) * cols
        out_ref[:, start : start + cols] = piece.astype(f32)


def place_rest_kernel(me, *refs):
    *refs, qkv_ref, out_ref, held = refs
    for core, p, piece in gathered(me, refs, held):
        cols = piece.shape[1]
        size = piece.shape[0] // 4
        at = slice(p * size, (p + 1) * size)
        for t in range(4):
            start = core * cols + (2 * t * cols if t < 3 else 0)
            part = piece[t * size : (t + 1) * size].astype(f32)
            (qkv_ref if t < 3 else out_ref)[at, start : start + cols] = part


def place_vec_kernel(me, a_ref, b_ref, c_ref, d_ref, *outs):
    total = (a_ref[...] + b_ref[...]) + (c_ref[...] + d_ref[...])
    cut = total.shape[1] // 4
    for z in range(4):
        @pl.when(me[3] == z)
        def _():
            for i in range(8):
                outs[i][...] = total[i : i + 1, z * cut : (z + 1) * cut]
            outs[8][...] = total[8 + z : 9 + z]


def place_vec(me, parts):
    width = parts[0].shape[1]
    outs = [shape(1, width // 4, dtype=f32)] * 8 + [shape(1, width, dtype=f32)]
    return call(
        place_vec_kernel, (1,), [whole(a) for a in parts], outs,
        [whole(o) for o in outs], [], me, *parts, micros=1, mib=16,
    )


def place(me, kernel, outs, parts):
    outs = [shape(*dims, dtype=f32) for dims in outs]
    rows, cols = parts[0].shape
    return call(
        kernel, (1,), [whole(a) for a in parts], outs, [whole(o) for o in outs],
        [pltpu.VMEM((2, 2, 2, rows, cols), bf16)], me, *parts, micros=3, mib=16,
    )


def local(
    dp, seq, tokens, lengths, head_swap, w_qkv, bias_q, bias_v, w_out, bias_out, gain_attn,
    shift_attn, w_up, bias_up, w_down, bias_down, gain_ffn, shift_ffn, cotangent,
):
    seqs_here, part_len, width = tokens.shape
    heads = head_swap.shape[0]
    head_dim = width // heads
    rows = seqs_here * part_len
    assert seqs_here == 2 and seq == 4 and dp % 8 == 0
    spot = lax.axis_index("dp")
    z = lax.axis_index("seq")
    core = spot & 1
    odd = z & 1
    me = jnp.stack([core, (spot >> 1) & 1, (spot >> 2) & 1, z]).astype(jnp.int32)

    def over_dp(arr, bit):
        return lax.ppermute(arr, "dp", [(i, i ^ bit) for i in range(dp)])

    def over_seq(arr, bit):
        return lax.ppermute(arr, "seq", [(i, i ^ bit) for i in range(seq)])

    def other(arr):
        return over_dp(arr, 1)

    def tie(value, *others):
        return lax.optimization_barrier((value, others))[0]

    def there(i, r):
        d, k = divmod(i, seq)
        return ((d & ~1) | (k >> 1)) * seq + 2 * (d & 1) + (r ^ (k & 1))

    ways = [[(i, there(i, r)) for i in range(dp * seq)] for r in range(2)]

    def send_block(parts):
        out = []
        for r, part in enumerate(parts):
            out.append(lax.ppermute(part, ("dp", "seq"), ways[r]))
        return out

    def gather_block(arr):
        return send_block([lax.dynamic_index_in_dim(arr, r ^ odd, 0, False) for r in range(2)])

    def return_block(arr):
        back = []
        for r in range(2):
            part = arr[r * part_len : (r + 1) * part_len]
            back.append(lax.ppermute(part, ("dp", "seq"), [(b, a) for a, b in ways[r]]))
        return back

    def in_order(back):
        return jnp.where(odd_z, jnp.stack(back[::-1]), jnp.stack(back))

    near = gather_block(tokens)
    length = lax.ppermute(lax.dynamic_slice_in_dim(lengths, odd, 1, 0), ("dp", "seq"), ways[0])[0]

    def limit(block, half):
        return length - (block * rows + (half ^ odd) * part_len)

    info = jnp.concatenate(
        [
            jnp.stack([limit(core, 0), limit(core, 1), limit(1 - core, 0), limit(1 - core, 1)]),
            head_swap,
        ]
    ).astype(jnp.int32)
    far = jnp.repeat(head_swap, head_dim)[None, :] == 1
    given = [lax.dynamic_index_in_dim(cotangent, r ^ odd, 0, False) for r in range(2)]
    near, info, far, me, second, odd_z, given = tie(
        (near, info, far, me, core == 1, odd == 1, given)
    )
    x = jnp.concatenate(near, 0)
    x_far = other(x)
    grad = send_block(tie(given, x))

    q = (mm(x, w_qkv[:, :width]) + bias_q).astype(bf16) * bf16(head_dim**-0.5)
    w_k, w_v = w_qkv[:, width : 2 * width], w_qkv[:, 2 * width :]
    k = jnp.where(far, mm(x_far, w_k), mm(x, w_k)).astype(bf16)
    v = (jnp.where(far, mm(x_far, w_v), mm(x, w_v)) + bias_v).astype(bf16)
    ctx, probs = attn_fwd(info, q, k, v)
    ctx_far = other(ctx)
    y, normed, rstd, act_m, act_t, slope_m, slope_t, out, d_two, d_ffn, vec_two = mid(
        me, x, ctx, w_out, bias_out[None], gain_attn[None], shift_attn[None], w_up, bias_up[None],
        w_down, bias_down[None], gain_ffn[None], shift_ffn[None], *grad,
    )

    def add(a, b):
        return (a.astype(f32) + b.astype(f32)).astype(bf16)

    def halve_first(stored):
        a_keep, a_send, b_keep, b_send = stored
        return (add(a_keep, over_dp(a_send, 2)), add(b_keep, over_dp(b_send, 4)))

    def halve_second(pair):
        a, b = pair
        return (add(a[0], over_dp(a[1], 4)), add(b[0], over_dp(b[1], 2)))

    def halve_seq_first(c):
        return add(c[0], over_seq(c[1], 1))

    def halve_seq_second(c):
        c = add(c[0], over_seq(c[1], 2))
        bit = 8
        while bit < dp:
            c = add(c, over_dp(c, bit))
            bit *= 2
        return c

    def collect(c, *others):
        c = c.reshape(-1, c.shape[-1])
        own = [c] + [over_dp(c, bit) for bit in (4, 2, 6)]
        if others:
            own = tie(own, *others)
        return own + [other(o) for o in own]

    half = width // 2
    d_ffn_far = other(d_ffn)
    act_far = other(act_t)
    y_far = other(y)
    pre_m, pre_t, vec_up = back_one(me, d_ffn, w_down, slope_m, slope_t)
    pre_far = other(pre_t)
    output = return_block(tie(out, pre_m))
    down = grad_down(me, d_ffn, d_ffn_far, act_m, act_far)
    pre_m, down = tie((pre_m, down))
    down = halve_first(down)
    d_one, d_attn, d_ctx, vec_one = back_two(
        me, pre_m, pre_t, w_up, d_two, normed, rstd, gain_attn[None], w_out
    )

    def mine(pair):
        return jnp.where(second, pair[1], pair[0])

    heads_far = [far[:, :half], far[:, half:]]
    pairs = heads // 4
    qs, ks, vs, k_gots, v_gots, vecs = [], [], [], [], [], []
    for i in range(2):
        d_q, d_k, d_v, vec = attn_bwd(info, i * pairs, pairs, q, k, v, d_ctx, probs)
        qs.append(d_q)
        ks.append(d_k)
        vs.append(d_v)
        vecs.append(vec)
        k_gots.append(other(d_k))
        v_gots.append(other(d_v))
        if i == 0:
            attn_far = other(jnp.where(second, d_attn[:, :half], d_attn[:, half:]))
            d_ctx, down, d_q = tie((d_ctx, down, d_q))
            down = halve_second(down)
    q_far = other(jnp.where(second, qs[0], qs[1]))
    down, qs = tie((down, qs))
    down = halve_seq_first(jnp.stack(down, 2))
    up = grad_up(me, y, y_far, pre_m, pre_far)
    down, up = tie((down, up))
    down = halve_seq_second(down)
    up = halve_first(up)
    k_own = [jnp.where(f, g, u) for f, g, u in zip(heads_far, k_gots, ks)]
    k_oth = [jnp.where(f, u, g) for f, g, u in zip(heads_far, k_gots, ks)]
    v_own = [jnp.where(f, g, u) for f, g, u in zip(heads_far, v_gots, vs)]
    v_oth = [jnp.where(f, u, g) for f, g, u in zip(heads_far, v_gots, vs)]

    rest = grad_rest(
        me, x, x_far, ctx, ctx_far, mine(qs), q_far, mine(k_own), mine(k_oth), mine(v_own),
        mine(v_oth), mine((d_attn[:, :half], d_attn[:, half:])), attn_far,
    )
    rest, qs, vecs = tie((rest, qs, vecs))
    rest = halve_first(rest)
    d_tok = tok(me, qs + k_own + v_own, w_qkv, d_one)
    d_tok = return_block(d_tok)
    up = halve_second(up)
    vec = jnp.concatenate(
        [jnp.concatenate(vecs, 1), vec_one, vec_two, vec_up], 0
    )
    vec = vec + other(vec)
    bit = 8
    while bit < dp:
        vec = vec + over_dp(vec, bit)
        bit *= 2
    v_y, v_x, v_d = tie([over_dp(vec, bit) for bit in (4, 2, 6)], rest)
    (s_down,) = place(me, place_down_kernel, [(width, width)], collect(down))
    up = halve_seq_first(jnp.stack(up, 2))
    rest = halve_second(rest)
    vec = (vec + v_y) + (v_x + v_d)
    vec_z = [vec] + [over_seq(vec, bit) for bit in (1, 2, 3)]
    rest = halve_seq_first(jnp.stack(rest, 2))
    up = halve_seq_second(up)
    (s_up,) = place(me, place_up_kernel, [(width // seq, w_up.shape[1])], collect(up))
    rest = tie(halve_seq_second(rest), s_down)
    rest = collect(rest, s_up)
    s_qkv, s_out = place(
        me, place_rest_kernel, [(width // seq, 3 * width), (width // seq, width)], rest
    )
    output = in_order(output)
    d_tokens = in_order(d_tok).astype(f32)

    s_bq, s_bv, s_ga, s_sa, s_bo, s_gf, s_sf, s_bd, s_b_up = (
        v.reshape(-1) for v in place_vec(me, vec_z)
    )
    return (
        output, d_tokens, s_qkv, s_bq, s_bv, s_out, s_bo, s_ga, s_sa, s_up, s_b_up, s_down, s_bd,
        s_gf, s_sf,
    )


def solution(mesh):
    dp, seq = mesh.shape["dp"], mesh.shape["seq"]
    rows = P("dp", "seq", None)
    placed = (rows, P("dp")) + (P(),) * 14 + (rows,)
    cut, line = P("seq", None), P("seq")

    def body(*args):
        return local(dp, seq, *args)

    return jax.shard_map(
        body,
        mesh=mesh,
        in_specs=placed,
        out_specs=(
            rows, rows, cut, line, line, cut, line, line, line, cut, line, cut, line, line, line,
        ),
        check_vma=False,
    )
```

profile of v0, /device:TPU:0, one launch (start us, length us, event | category | flops | bytes accessed | tf_op | source)
XLA Modules:
  0.0 256.9 jit_solution(17559966086838915545)
XLA Ops:
  2.1 1.9 collective-permute-start.2
  5.8 3.1 %collective-permute-start.1 = (bf16[256,768]{1,0:T(8,128)(2,1)S(1)}, bf16[256,768]{1,0:T(8,128)(2,1)S(1)}, u32[]{:S(2)}, u32[]{:S(2)}) collective-permute-start(bf16[256,768]{1,0:T(8,128)(2,1)S(1)} %get-tuple-element.225), channel_id=1, source_target_pairs={{0,1},{1,0},{2,5},{3,4},{4,3},{5,2},{6,7},{7,6},{8,9},{9,8},{10,13... | collective-permute-start | bytes 1179656 | tf_op jit(solution)/shard_map/ppermute | solution.py:566
  12.2 4.6 %collective-permute-done.1 = bf16[256,768]{1,0:T(8,128)(2,1)S(1)} collective-permute-done((bf16[256,768]{1,0:T(8,128)(2,1)S(1)}, bf16[256,768]{1,0:T(8,128)(2,1)S(1)}, u32[]{:S(2)}, u32[]{:S(2)}) %collective-permute-start.1) | collective-permute-done | bytes 393248 | tf_op jit(solution)/shard_map/ppermute | solution.py:566
  16.9 11.0 %collective-permute-start.3 = (bf16[512,768]{1,0:T(8,128)(2,1)S(1)}, bf16[512,768]{1,0:T(8,128)(2,1)S(1)}, u32[]{:S(2)}, u32[]{:S(2)}) collective-permute-start(bf16[512,768]{1,0:T(8,128)(2,1)S(1)} %constant_dynamic-update-slice_fusion.x_ref.xo_ref), channel_id=1, source_target_pairs={{0,4},{4,0},{8,12},{12,8},{16,20},{20,16},{24,28},{28,24},{1,5},{5... | collective-permute-start | bytes 2359304 | tf_op jit(solution)/shard_map/ppermute | solution.py:546
  28.6 4.8 %collective-permute-start.5 = (bf16[256,768]{1,0:T(8,128)(2,1)S(1)}, bf16[256,768]{1,0:T(8,128)(2,1)S(1)}, u32[]{:S(2)}, u32[]{:S(2)}) collective-permute-start(bf16[256,768]{1,0:T(8,128)(2,1)S(1)} %get-tuple-element.121), channel_id=1, source_target_pairs={{0,1},{1,0},{2,5},{3,4},{4,3},{5,2},{6,7},{7,6},{8,9},{9,8},{10,13... | collective-permute-start | bytes 1179656 | tf_op jit(solution)/shard_map/ppermute | solution.py:566
  33.4 2.2 fusion.5
  39.1 11.0 %shard_map.280 = (bf16[512,768]{1,0:T(8,128)(2,1)S(1)}, bf16[12,512,512]{2,1,0:T(8,128)(2,1)}) custom-call(s32[16]{0:T(128)S(1)} %concatenate.12.info, bf16[512,768]{1,0:T(8,128)(2,1)S(1)} %fusion.q_ref, bf16[512,768]{1,0:T(8,128)(2,1)S(1)} %select_convert_fusion.k_ref, bf16[512,768]{1,0:T(8,128)(2,1)S(1)} %add_convert_fusion.v_ref), custom_call_target="tpu_custom_call" | custom-call | flops 8000000000 | bytes 8000000 | tf_op jit(solution)/shard_map/pallas_call | solution.py:31
  50.2 13.7 %shard_map.281 = (bf16[512,768]{1,0:T(8,128)(2,1)S(1)}, f32[512,768]{1,0:T(8,128)S(1)}, f32[512,1]{1,0:T(8,128)S(1)}, bf16[512,1536]{1,0:T(8,128)(2,1)S(1)}, bf1...) custom-call(s32[4]{0:T(128)S(1)} %pad_add_fusion.me, ...), custom_call_target="tpu_custom_call" | custom-call | flops 17999998976 | bytes 8000000 | tf_op jit(solution)/shard_map/pallas_call | solution.py:31
  63.9 3.4 %collective-permute-start.10 = (bf16[512,1536]{1,0:T(8,128)(2,1)S(1)}, bf16[512,1536]{1,0:T(8,128)(2,1)S(1)}, u32[]{:S(2)}, u32[]{:S(2)}) collective-permute-start(bf16[512,1536]{1,0:T(8,128)(2,1)S(1)} %get-tuple-element.130), channel_id=1, source_target_pairs={{0,4},{4,0},{8,12},{12,8},{16,20},{20,16},{24,28},{28,24},{1,5},{5... | collective-permute-start | bytes 4718600 | tf_op jit(solution)/shard_map/ppermute | solution.py:546
  67.4 4.0 %shard_map.282 = (bf16[512,1536]{1,0:T(8,128)(2,1)S(1)}, bf16[512,1536]{1,0:T(8,128)(2,1)S(1)}, f32[4,768]{1,0:T(4,128)S(1)}) custom-call(s32[4]{0:T(128)S(1)} %pad_add_fusion.me, bf16[512,768]{1,0:T(8,128)(2,1)S(1)} %get-tuple-element.123.dffn_ref.lo_ref, bf16[3072,768]{1,0:T(8,128)(2,1)S(1)} %bitcast.139, bf16[3072,768]{1,0:T(8,128)(2,1)S(1)} %bitcast.139, ...), custom_call_target="tpu_custom_call" | custom-call | flops 6000000000 | bytes 8000000 | tf_op jit(solution)/shard_map/pallas_call | solution.py:31
  72.3 2.7 %collective-permute-start.8 = (bf16[512,768]{1,0:T(8,128)(2,1)S(1)}, bf16[512,768]{1,0:T(8,128)(2,1)S(1)}, u32[]{:S(2)}, u32[]{:S(2)}) collective-permute-start(bf16[512,768]{1,0:T(8,128)(2,1)S(1)} %get-tuple-element.117.ctx_ref.co_ref), channel_id=1, source_target_pairs={{0,4},{4,0},{8,12},{12,8},{16,20},{20,16},{24,28},{28,24},{1,5},{5... | collective-permute-start | bytes 2359304 | tf_op jit(solution)/shard_map/ppermute | solution.py:546
  75.0 9.1 %collective-permute-done.6 = bf16[256,768]{1,0:T(8,128)(2,1)S(1)} collective-permute-done((bf16[256,768]{1,0:T(8,128)(2,1)S(1)}, bf16[256,768]{1,0:T(8,128)(2,1)S(1)}, u32[]{:S(2)}, u32[]{:S(2)}) %collective-permute-start.6) | collective-permute-done | bytes 393248 | tf_op jit(solution)/shard_map/ppermute | solution.py:576
  84.1 6.5 %collective-permute-start.30 = (bf16[512,768]{1,0:T(8,128)(2,1)S(1)}, bf16[512,768]{1,0:T(8,128)(2,1)S(1)}, u32[]{:S(2)}, u32[]{:S(2)}) collective-permute-start(bf16[512,768]{1,0:T(8,128)(2,1)S(1)} %get-tuple-element.173.lo_ref), channel_id=1, source_target_pairs={{0,4},{4,0},{8,12},{12,8},{16,20},{20,16},{24,28},{28,24},{1,5},{5... | collective-permute-start | bytes 2359304 | tf_op jit(solution)/shard_map/ppermute | solution.py:546
  91.7 4.8 %shard_map.283 = (bf16[2,2,2,96,384]{4,3,2,1,0:T(8,128)(2,1)S(1)}, bf16[2,2,2,96,384]{4,3,2,1,0:T(8,128)(2,1)S(1)}, bf16[2,2,2,96,384]{4,3,2,1,0:T(8,128)(2,1)S(1)}, bf16[2,2,2,96,384]{4,3,2,1,0:T(8,128)(2,1)S(1)}) custom-call(s32[4]{0:T(128)S(1)} %pad_add_fusion.me, bf16[512,768]{1,0:T(8,128)(2,1)S(1)} %get-tuple-element.123.dffn_ref.lo_ref, ...), custom_call_target="tpu_custom_call" | custom-call | flops 6000000000 | bytes 8000000 | tf_op jit(solution)/shard_map/pallas_call | solution.py:31
  96.4 1.6 collective-permute-start.12
  98.0 1.5 collective-permute-start.11
  99.5 6.2 %shard_map.284 = (f32[512,768]{1,0:T(8,128)S(1)}, bf16[512,768]{1,0:T(8,128)(2,1)S(1)}, bf16[512,768]{1,0:T(8,128)(2,1)S(1)}, f32[3,768]{1,0:T(4,128)S(1)}) custom-call(s32[4]{0:T(128)S(1)} %pad_add_fusion.me, bf16[512,1536]{1,0:T(8,128)(2,1)S(1)} %get-tuple-element.135.pm_ref.ro_ref, bf16[512,1536]{1,0:T(8,128)(2,1)S(1)} %get-tuple-element.136.pt_ref, ...), custom_call_target="tpu_custom_call" | custom-call | flops 8000000000 | bytes 8000000 | tf_op jit(solution)/shard_map/pallas_call | solution.py:31
  105.7 5.8 %shard_map.285 = (bf16[512,384]{1,0:T(8,128)(2,1)S(1)}, bf16[512,384]{1,0:T(8,128)(2,1)S(1)}, bf16[512,384]{1,0:T(8,128)(2,1)S(1)}, f32[2,384]{1,0:T(2,128)S(1)}) custom-call(s32[16]{0:T(128)S(1)} %concatenate.12.info, bf16[512,768]{1,0:T(8,128)(2,1)S(1)} %fusion.q_ref, bf16[512,768]{1,0:T(8,128)(2,1)S(1)} %select_convert_fusion.k_ref, ...), custom_call_target="tpu_custom_call" | custom-call | flops 6000000000 | bytes 8000000 | tf_op jit(solution)/shard_map/pallas_call | solution.py:31
  112.1 4.4 %shard_map.289 = (bf16[2,2,2,96,384]{4,3,2,1,0:T(8,128)(2,1)S(1)}, bf16[2,2,2,96,384]{4,3,2,1,0:T(8,128)(2,1)S(1)}, bf16[2,2,2,96,384]{4,3,2,1,0:T(8,128)(2,1)S(1)}, bf16[2,2,2,96,384]{4,3,2,1,0:T(8,128)(2,1)S(1)}) custom-call(s32[4]{0:T(128)S(1)} %pad_add_fusion.me, bf16[512,768]{1,0:T(8,128)(2,1)S(1)} %get-tuple-element.173.lo_ref, ...), custom_call_target="tpu_custom_call" | custom-call | flops 6000000000 | bytes 8000000 | tf_op jit(solution)/shard_map/pallas_call | solution.py:31
  116.9 6.0 %shard_map.286 = (bf16[512,384]{1,0:T(8,128)(2,1)S(1)}, bf16[512,384]{1,0:T(8,128)(2,1)S(1)}, bf16[512,384]{1,0:T(8,128)(2,1)S(1)}, f32[2,384]{1,0:T(2,128)S(1)}) custom-call(s32[16]{0:T(128)S(1)} %concatenate.12.info, bf16[512,768]{1,0:T(8,128)(2,1)S(1)} %fusion.q_ref, bf16[512,768]{1,0:T(8,128)(2,1)S(1)} %select_convert_fusion.k_ref, ...), custom_call_target="tpu_custom_call" | custom-call | flops 6000000000 | bytes 8000000 | tf_op jit(solution)/shard_map/pallas_call | solution.py:31
  124.2 7.8 %collective-permute-done.14 = bf16[2,2,96,384]{3,2,1,0:T(8,128)(2,1)S(1)} collective-permute-done((bf16[2,2,96,384]{3,2,1,0:T(8,128)(2,1)S(1)}, bf16[2,2,96,384]{3,2,1,0:T(8,128)(2,1)S(1)}, u32[]{:S(2)}, u32[]{:S(2)}) %collective-permute-start.14) | collective-permute-done | bytes 294944 | tf_op jit(solution)/shard_map/ppermute | solution.py:546
  135.4 4.1 %shard_map.287 = (bf16[2,2,2,96,384]{4,3,2,1,0:T(8,128)(2,1)S(1)}, bf16[2,2,2,96,384]{4,3,2,1,0:T(8,128)(2,1)S(1)}, bf16[2,2,2,96,384]{4,3,2,1,0:T(8,128)(2,1)S(1)}, bf16[2,2,2,96,384]{4,3,2,1,0:T(8,128)(2,1)S(1)}) custom-call(s32[4]{0:T(128)S(1)} %pad_add_fusion.me, bf16[512,768]{1,0:T(8,128)(2,1)S(1)} %constant_dynamic-update-slice_fusion.x_ref.xo_ref, ...), custom_call_target="tpu_custom_call" | custom-call | flops 6000000000 | bytes 8000000 | tf_op jit(solution)/shard_map/pallas_call | solution.py:31
  141.6 2.6 %shard_map.288 = bf16[512,768]{1,0:T(8,128)(2,1)S(1)} custom-call(s32[4]{0:T(128)S(1)} %pad_add_fusion.me, bf16[512,384]{1,0:T(8,128)(2,1)S(1)} %get-tuple-element.164.q0, bf16[512,384]{1,0:T(8,128)(2,1)S(1)} %get-tuple-element.165.q1, bf16[512,384]{1,0:T(8,128)(2,1)S(1)} %get-tuple-element.229.k0, bf16[512,384]{1,0:T(8,128)(2,1)S(1)} %get-tuple-element.230.k1, ...), custom_call_target="tpu_custom_call" | custom-call | flops 5000000000 | bytes 8000000 | tf_op jit(solution)/shard_map/pallas_call | solution.py:31
  144.3 1.5 collective-permute-start.32
  146.8 7.1 %collective-permute-done.32 = bf16[2,96,384]{2,1,0:T(8,128)(2,1)S(1)} collective-permute-done((bf16[2,96,384]{2,1,0:T(8,128)(2,1)S(1)}, bf16[2,96,384]{2,1,0:T(8,128)(2,1)S(1)}, u32[]{:S(2)}, u32[]{:S(2)}) %collective-permute-start.32) | collective-permute-done | bytes 147488 | tf_op jit(solution)/shard_map/ppermute | solution.py:549
  154.0 1.6 collective-permute-start.33
  158.0 1.8 collective-permute-done.33.refs_1_
  159.8 1.5 collective-permute-start.45
  161.3 10.4 %collective-permute-done.34.refs_2_ = bf16[192,384]{1,0:T(8,128)(2,1)S(1)} collective-permute-done((bf16[192,384]{1,0:T(8,128)(2,1)S(1)}, bf16[192,384]{1,0:T(8,128)(2,1)S(1)}, u32[]{:S(2)}, u32[]{:S(2)}) %collective-permute-start.34) | collective-permute-done | bytes 147488 | tf_op jit(solution)/shard_map/ppermute | solution.py:546
  171.8 2.6 %collective-permute-done.35.refs_3_ = bf16[192,384]{1,0:T(8,128)(2,1)S(1)} collective-permute-done((bf16[192,384]{1,0:T(8,128)(2,1)S(1)}, bf16[192,384]{1,0:T(8,128)(2,1)S(1)}, u32[]{:S(2)}, u32[]{:S(2)}) %collective-permute-start.35) | collective-permute-done | bytes 147488 | tf_op jit(solution)/shard_map/ppermute | solution.py:546
  174.9 1.6 collective-permute-start.61
  178.7 2.7 %shard_map.290 = f32[768,768]{1,0:T(8,128)} custom-call(s32[4]{0:T(128)S(1)} %pad_add_fusion.me, bf16[192,384]{1,0:T(8,128)(2,1)S(1)} %bitcast.154, bf16[192,384]{1,0:T(8,128)(2,1)S(1)} %collective-permute-done.33.refs_1_, bf16[192,384]{1,0:T(8,128)(2,1)S(1)} %collective-permute-done.34.refs_2_, bf16[192,384]{1,0:T(8,128)(2,1)S(1)} %collective-permute-done.35.refs_3_, ...), custom_call_target="tpu_custom_call" | custom-call | flops 3000000000 | bytes 8000000 | tf_op jit(solution)/shard_map/pallas_call | solution.py:31
  184.5 5.5 %collective-permute-done.24 = bf16[2,2,96,384]{3,2,1,0:T(8,128)(2,1)S(1)} collective-permute-done((bf16[2,2,96,384]{3,2,1,0:T(8,128)(2,1)S(1)}, bf16[2,2,96,384]{3,2,1,0:T(8,128)(2,1)S(1)}, u32[]{:S(2)}, u32[]{:S(2)}) %collective-permute-start.24) | collective-permute-done | bytes 294944 | tf_op jit(solution)/shard_map/ppermute | solution.py:546
  190.9 1.3 collective-permute-start.46
  192.4 5.2 %collective-permute-done.44 = bf16[2,2,96,384]{3,2,1,0:T(8,128)(2,1)S(1)} collective-permute-done((bf16[2,2,96,384]{3,2,1,0:T(8,128)(2,1)S(1)}, bf16[2,2,96,384]{3,2,1,0:T(8,128)(2,1)S(1)}, u32[]{:S(2)}, u32[]{:S(2)}) %collective-permute-start.44) | collective-permute-done | bytes 294944 | tf_op jit(solution)/shard_map/ppermute | solution.py:546
  199.9 9.1 %collective-permute-done.27 = bf16[2,2,96,384]{3,2,0,1:T(8,128)(2,1)S(1)} collective-permute-done((bf16[2,2,96,384]{3,2,0,1:T(8,128)(2,1)S(1)}, bf16[2,2,96,384]{3,2,0,1:T(8,128)(2,1)S(1)}, u32[]{:S(2)}, u32[]{:S(2)}) %collective-permute-start.27) | collective-permute-done | bytes 294944 | tf_op jit(solution)/shard_map/ppermute | solution.py:549
  209.7 2.6 %collective-permute-done.47 = bf16[2,2,96,384]{3,2,0,1:T(8,128)(2,1)S(1)} collective-permute-done((bf16[2,2,96,384]{3,2,0,1:T(8,128)(2,1)S(1)}, bf16[2,2,96,384]{3,2,0,1:T(8,128)(2,1)S(1)}, u32[]{:S(2)}, u32[]{:S(2)}) %collective-permute-start.47) | collective-permute-done | bytes 294944 | tf_op jit(solution)/shard_map/ppermute | solution.py:549
  212.4 2.4 collective-permute-start.48
  214.8 5.9 %collective-permute-done.28 = bf16[2,96,384]{2,1,0:T(8,128)(2,1)S(1)} collective-permute-done((bf16[2,96,384]{2,1,0:T(8,128)(2,1)S(1)}, bf16[2,96,384]{2,1,0:T(8,128)(2,1)S(1)}, u32[]{:S(2)}, u32[]{:S(2)}) %collective-permute-start.28) | collective-permute-done | bytes 147488 | tf_op jit(solution)/shard_map/ppermute | solution.py:549
  220.9 1.5 collective-permute-done.48
  225.0 2.2 collective-permute-start.51
  227.4 1.6 collective-permute-done.41.refs_2_
  231.0 2.2 collective-permute-start.53
  235.5 1.8 collective-permute-start.65
  238.3 2.2 shard_map.291
  240.5 3.4 %collective-permute-done.42.refs_3_ = bf16[192,384]{1,0:T(8,128)(2,1)S(1)} collective-permute-done((bf16[192,384]{1,0:T(8,128)(2,1)S(1)}, bf16[192,384]{1,0:T(8,128)(2,1)S(1)}, u32[]{:S(2)}, u32[]{:S(2)}) %collective-permute-start.42) | collective-permute-done | bytes 147488 | tf_op jit(solution)/shard_map/ppermute | solution.py:546
  245.1 5.6 %collective-permute-start.57 = (bf16[192,384]{1,0:T(8,128)(2,1)S(1)}, bf16[192,384]{1,0:T(8,128)(2,1)S(1)}, u32[]{:S(2)}, u32[]{:S(2)}) collective-permute-start(bf16[192,384]{1,0:T(8,128)(2,1)S(1)} %collective-permute-done.40.refs_1_), channel_id=1, source_target_pairs={{0,4},{4,0},{8,12},{12,8},{16,20},{20,16},{24,28},{28,24},{1,5},{5... | collective-permute-start | bytes 442376 | tf_op jit(solution)/shard_map/ppermute | solution.py:546
  254.5 2.2 shard_map.292
  (210 shorter events, 43.9 us)
Async XLA Ops:
  2.1 7.3 %collective-permute-start.2 = (s32[1]{0:T(128)}, s32[1]{0:T(128)}, u32[]{:S(2)}, u32[]{:S(2)}) collective-permute-start(s32[1]{0:T(128)} %dynamic_slice.18), channel_id=1, source_target_pairs={{0,0},{1,1},{2,4},{3,5},{4,2},{5,3},{6,6},{7,7},{8,8},{9,9},{10,12... | collective-permute-start | bytes 20 | tf_op jit(solution)/shard_map/ppermute | solution.py:583
  5.1 7.1 %collective-permute-start = (bf16[256,768]{1,0:T(8,128)(2,1)S(1)}, bf16[256,768]{1,0:T(8,128)(2,1)S(1)}, u32[]{:S(2)}, u32[]{:S(2)}) collective-permute-start(bf16[256,768]{1,0:T(8,128)(2,1)S(1)} %get-tuple-element.226), channel_id=1, source_target_pairs={{0,0},{1,1},{2,4},{3,5},{4,2},{5,3},{6,6},{7,7},{8,8},{9,9},{10,12... | collective-permute-start | bytes 1179656 | tf_op jit(solution)/shard_map/ppermute | solution.py:566
  5.8 11.0 %collective-permute-start.1 = (bf16[256,768]{1,0:T(8,128)(2,1)S(1)}, bf16[256,768]{1,0:T(8,128)(2,1)S(1)}, u32[]{:S(2)}, u32[]{:S(2)}) collective-permute-start(bf16[256,768]{1,0:T(8,128)(2,1)S(1)} %get-tuple-element.225), channel_id=1, source_target_pairs={{0,1},{1,0},{2,5},{3,4},{4,3},{5,2},{6,7},{7,6},{8,9},{9,8},{10,13... | collective-permute-start | bytes 1179656 | tf_op jit(solution)/shard_map/ppermute | solution.py:566
  16.9 20.5 %collective-permute-start.3 = (bf16[512,768]{1,0:T(8,128)(2,1)S(1)}, bf16[512,768]{1,0:T(8,128)(2,1)S(1)}, u32[]{:S(2)}, u32[]{:S(2)}) collective-permute-start(bf16[512,768]{1,0:T(8,128)(2,1)S(1)} %constant_dynamic-update-slice_fusion.x_ref.xo_ref), channel_id=1, source_target_pairs={{0,4},{4,0},{8,12},{12,8},{16,20},{20,16},{24,28},{28,24},{1,5},{5... | collective-permute-start | bytes 2359304 | tf_op jit(solution)/shard_map/ppermute | solution.py:546
  27.9 22.2 %collective-permute-start.4 = (bf16[256,768]{1,0:T(8,128)(2,1)S(1)}, bf16[256,768]{1,0:T(8,128)(2,1)S(1)}, u32[]{:S(2)}, u32[]{:S(2)}) collective-permute-start(bf16[256,768]{1,0:T(8,128)(2,1)S(1)} %get-tuple-element.120), channel_id=1, source_target_pairs={{0,0},{1,1},{2,4},{3,5},{4,2},{5,3},{6,6},{7,7},{8,8},{9,9},{10,12... | collective-permute-start | bytes 1179656 | tf_op jit(solution)/shard_map/ppermute | solution.py:566
  28.6 21.6 %collective-permute-start.5 = (bf16[256,768]{1,0:T(8,128)(2,1)S(1)}, bf16[256,768]{1,0:T(8,128)(2,1)S(1)}, u32[]{:S(2)}, u32[]{:S(2)}) collective-permute-start(bf16[256,768]{1,0:T(8,128)(2,1)S(1)} %get-tuple-element.121), channel_id=1, source_target_pairs={{0,1},{1,0},{2,5},{3,4},{4,3},{5,2},{6,7},{7,6},{8,9},{9,8},{10,13... | collective-permute-start | bytes 1179656 | tf_op jit(solution)/shard_map/ppermute | solution.py:566
  63.9 27.7 %collective-permute-start.10 = (bf16[512,1536]{1,0:T(8,128)(2,1)S(1)}, bf16[512,1536]{1,0:T(8,128)(2,1)S(1)}, u32[]{:S(2)}, u32[]{:S(2)}) collective-permute-start(bf16[512,1536]{1,0:T(8,128)(2,1)S(1)} %get-tuple-element.130), channel_id=1, source_target_pairs={{0,4},{4,0},{8,12},{12,8},{16,20},{20,16},{24,28},{28,24},{1,5},{5... | collective-permute-start | bytes 4718600 | tf_op jit(solution)/shard_map/ppermute | solution.py:546
  67.3 24.3 %collective-permute-start.9 = (bf16[512,768]{1,0:T(8,128)(2,1)S(1)}, bf16[512,768]{1,0:T(8,128)(2,1)S(1)}, u32[]{:S(2)}, u32[]{:S(2)}) collective-permute-start(bf16[512,768]{1,0:T(8,128)(2,1)S(1)} %get-tuple-element.123.dffn_ref.lo_ref), channel_id=1, source_target_pairs={{0,4},{4,0},{8,12},{12,8},{16,20},{20,16},{24,28},{28,24},{1,5},{5... | collective-permute-start | bytes 2359304 | tf_op jit(solution)/shard_map/ppermute | solution.py:546
  71.5 12.6 %collective-permute-start.6 = (bf16[256,768]{1,0:T(8,128)(2,1)S(1)}, bf16[256,768]{1,0:T(8,128)(2,1)S(1)}, u32[]{:S(2)}, u32[]{:S(2)}) collective-permute-start(bf16[256,768]{1,0:T(8,128)(2,1)S(1)} %get-tuple-element.221), channel_id=1, source_target_pairs={{1,0},{0,1},{5,2},{4,3},{3,4},{2,5},{7,6},{6,7},{9,8},{8,9},{13,10... | collective-permute-start | bytes 1179656 | tf_op jit(solution)/shard_map/ppermute | solution.py:576
  71.6 12.5 %collective-permute-start.7 = (bf16[256,768]{1,0:T(8,128)(2,1)S(1)}, bf16[256,768]{1,0:T(8,128)(2,1)S(1)}, u32[]{:S(2)}, u32[]{:S(2)}) collective-permute-start(bf16[256,768]{1,0:T(8,128)(2,1)S(1)} %get-tuple-element.222), channel_id=1, source_target_pairs={{0,0},{1,1},{4,2},{5,3},{2,4},{3,5},{6,6},{7,7},{8,8},{9,9},{12,10... | collective-permute-start | bytes 1179656 | tf_op jit(solution)/shard_map/ppermute | solution.py:576
  72.3 62.4 %collective-permute-start.8 = (bf16[512,768]{1,0:T(8,128)(2,1)S(1)}, bf16[512,768]{1,0:T(8,128)(2,1)S(1)}, u32[]{:S(2)}, u32[]{:S(2)}) collective-permute-start(bf16[512,768]{1,0:T(8,128)(2,1)S(1)} %get-tuple-element.117.ctx_ref.co_ref), channel_id=1, source_target_pairs={{0,4},{4,0},{8,12},{12,8},{16,20},{20,16},{24,28},{28,24},{1,5},{5... | collective-permute-start | bytes 2359304 | tf_op jit(solution)/shard_map/ppermute | solution.py:546
  84.1 27.5 %collective-permute-start.31 = (bf16[512,1536]{1,0:T(8,128)(2,1)S(1)}, bf16[512,1536]{1,0:T(8,128)(2,1)S(1)}, u32[]{:S(2)}, u32[]{:S(2)}) collective-permute-start(bf16[512,1536]{1,0:T(8,128)(2,1)S(1)} %get-tuple-element.136.pt_ref), channel_id=1, source_target_pairs={{0,4},{4,0},{8,12},{12,8},{16,20},{20,16},{24,28},{28,24},{1,5},{5... | collective-permute-start | bytes 4718600 | tf_op jit(solution)/shard_map/ppermute | solution.py:546
  84.1 27.4 %collective-permute-start.30 = (bf16[512,768]{1,0:T(8,128)(2,1)S(1)}, bf16[512,768]{1,0:T(8,128)(2,1)S(1)}, u32[]{:S(2)}, u32[]{:S(2)}) collective-permute-start(bf16[512,768]{1,0:T(8,128)(2,1)S(1)} %get-tuple-element.173.lo_ref), channel_id=1, source_target_pairs={{0,4},{4,0},{8,12},{12,8},{16,20},{20,16},{24,28},{28,24},{1,5},{5... | collective-permute-start | bytes 2359304 | tf_op jit(solution)/shard_map/ppermute | solution.py:546
  96.4 20.1 %collective-permute-start.12 = (bf16[2,2,2,96,384]{4,3,2,1,0:T(8,128)(2,1)S(1)}, bf16[2,2,2,96,384]{4,3,2,1,0:T(8,128)(2,1)S(1)}, u32[]{:S(2)}, u32[]{:S(2)}) collective-permute-start(bf16[2,2,2,96,384]{4,3,2,1,0:T(8,128)(2,1)S(1)} %get-tuple-element.144), channel_id=1, source_target_pairs={{0,16},{4,20},{8,24},{12,28},{16,0},{20,4},{24,8},{28,12},{1,17},{... | collective-permute-start | bytes 1769480 | tf_op jit(solution)/shard_map/ppermute | solution.py:546
  98.0 18.7 %collective-permute-start.11 = (bf16[2,2,2,96,384]{4,3,2,1,0:T(8,128)(2,1)S(1)}, bf16[2,2,2,96,384]{4,3,2,1,0:T(8,128)(2,1)S(1)}, u32[]{:S(2)}, u32[]{:S(2)}) collective-permute-start(bf16[2,2,2,96,384]{4,3,2,1,0:T(8,128)(2,1)S(1)} %get-tuple-element.142), channel_id=1, source_target_pairs={{0,8},{4,12},{8,0},{12,4},{16,24},{20,28},{24,16},{28,20},{1,9},{5... | collective-permute-start | bytes 1769480 | tf_op jit(solution)/shard_map/ppermute | solution.py:546
  111.5 21.3 %collective-permute-start.17 = (bf16[512,384]{1,0:T(8,128)(2,1)S(1)}, bf16[512,384]{1,0:T(8,128)(2,1)S(1)}, u32[]{:S(2)}, u32[]{:S(2)}) collective-permute-start(bf16[512,384]{1,0:T(8,128)(2,1)S(1)} %get-tuple-element.154), channel_id=1, source_target_pairs={{0,4},{4,0},{8,12},{12,8},{16,20},{20,16},{24,28},{28,24},{1,5},{5... | collective-permute-start | bytes 1179656 | tf_op jit(solution)/shard_map/ppermute | solution.py:546
  111.6 21.5 %collective-permute-start.19 = (bf16[512,384]{1,0:T(8,128)(2,1)S(1)}, bf16[512,384]{1,0:T(8,128)(2,1)S(1)}, u32[]{:S(2)}, u32[]{:S(2)}) collective-permute-start(bf16[512,384]{1,0:T(8,128)(2,1)S(1)} %get-tuple-element.156), channel_id=1, source_target_pairs={{0,4},{4,0},{8,12},{12,8},{16,20},{20,16},{24,28},{28,24},{1,5},{5... | collective-permute-start | bytes 1179656 | tf_op jit(solution)/shard_map/ppermute | solution.py:546
  122.9 9.1 %collective-permute-start.14 = (bf16[2,2,96,384]{3,2,1,0:T(8,128)(2,1)S(1)}, bf16[2,2,96,384]{3,2,1,0:T(8,128)(2,1)S(1)}, u32[]{:S(2)}, u32[]{:S(2)}) collective-permute-start(bf16[2,2,96,384]{3,2,1,0:T(8,128)(2,1)S(1)} %slice_bitcast_fusion.8), channel_id=1, source_target_pairs={{0,8},{4,12},{8,0},{12,4},{16,24},{20,28},{24,16},{28,20},{1,9},{5... | collective-permute-start | bytes 884744 | tf_op jit(solution)/shard_map/ppermute | solution.py:546
  123.6 8.8 %collective-permute-start.13 = (bf16[2,2,96,384]{3,2,1,0:T(8,128)(2,1)S(1)}, bf16[2,2,96,384]{3,2,1,0:T(8,128)(2,1)S(1)}, u32[]{:S(2)}, u32[]{:S(2)}) collective-permute-start(bf16[2,2,96,384]{3,2,1,0:T(8,128)(2,1)S(1)} %slice_bitcast_fusion.9), channel_id=1, source_target_pairs={{0,16},{4,20},{8,24},{12,28},{16,0},{20,4},{24,8},{28,12},{1,17},{... | collective-permute-start | bytes 884744 | tf_op jit(solution)/shard_map/ppermute | solution.py:546
  133.7 10.5 %collective-permute-start.29 = (bf16[2,2,96,384]{3,2,0,1:T(8,128)(2,1)S(1)}, bf16[2,2,96,384]{3,2,0,1:T(8,128)(2,1)S(1)}, u32[]{:S(2)}, u32[]{:S(2)}) collective-permute-start(bf16[2,2,96,384]{3,2,0,1:T(8,128)(2,1)S(1)} %fusion.29), channel_id=1, source_target_pairs={{0,1},{1,0},{2,3},{3,2},{4,5},{5,4},{6,7},{7,6},{8,9},{9,8},{10,11... | collective-permute-start | bytes 884744 | tf_op jit(solution)/shard_map/ppermute | solution.py:549
  139.8 16.6 %collective-permute-start.23 = (bf16[2,2,2,96,384]{4,3,2,1,0:T(8,128)(2,1)S(1)}, bf16[2,2,2,96,384]{4,3,2,1,0:T(8,128)(2,1)S(1)}, u32[]{:S(2)}, u32[]{:S(2)}) collective-permute-start(bf16[2,2,2,96,384]{4,3,2,1,0:T(8,128)(2,1)S(1)} %get-tuple-element.168), channel_id=1, source_target_pairs={{0,8},{4,12},{8,0},{12,4},{16,24},{20,28},{24,16},{28,20},{1,9},{5... | collective-permute-start | bytes 1769480 | tf_op jit(solution)/shard_map/ppermute | solution.py:546
  141.1 16.6 %collective-permute-start.25 = (bf16[2,2,2,96,384]{4,3,2,1,0:T(8,128)(2,1)S(1)}, bf16[2,2,2,96,384]{4,3,2,1,0:T(8,128)(2,1)S(1)}, u32[]{:S(2)}, u32[]{:S(2)}) collective-permute-start(bf16[2,2,2,96,384]{4,3,2,1,0:T(8,128)(2,1)S(1)} %get-tuple-element.170), channel_id=1, source_target_pairs={{0,16},{4,20},{8,24},{12,28},{16,0},{20,4},{24,8},{28,12},{1,17},{... | collective-permute-start | bytes 1769480 | tf_op jit(solution)/shard_map/ppermute | solution.py:546
  144.3 9.6 %collective-permute-start.32 = (bf16[2,96,384]{2,1,0:T(8,128)(2,1)S(1)}, bf16[2,96,384]{2,1,0:T(8,128)(2,1)S(1)}, u32[]{:S(2)}, u32[]{:S(2)}) collective-permute-start(bf16[2,96,384]{2,1,0:T(8,128)(2,1)S(1)} %slice_bitcast_fusion.15), channel_id=1, source_target_pairs={{0,2},{1,3},{2,0},{3,1},{4,6},{5,7},{6,4},{7,5},{8,10},{9,11},{10,... | collective-permute-start | bytes 442376 | tf_op jit(solution)/shard_map/ppermute | solution.py:549
  145.8 35.6 %collective-permute-start.43 = (bf16[2,2,2,96,384]{4,3,2,1,0:T(8,128)(2,1)S(1)}, bf16[2,2,2,96,384]{4,3,2,1,0:T(8,128)(2,1)S(1)}, u32[]{:S(2)}, u32[]{:S(2)}) collective-permute-start(bf16[2,2,2,96,384]{4,3,2,1,0:T(8,128)(2,1)S(1)} %get-tuple-element.181), channel_id=1, source_target_pairs={{0,8},{4,12},{8,0},{12,4},{16,24},{20,28},{24,16},{28,20},{1,9},{5... | collective-permute-start | bytes 1769480 | tf_op jit(solution)/shard_map/ppermute | solution.py:546
  155.6 16.2 %collective-permute-start.34 = (bf16[192,384]{1,0:T(8,128)(2,1)S(1)}, bf16[192,384]{1,0:T(8,128)(2,1)S(1)}, u32[]{:S(2)}, u32[]{:S(2)}) collective-permute-start(bf16[192,384]{1,0:T(8,128)(2,1)S(1)} %bitcast.151), channel_id=1, source_target_pairs={{0,8},{4,12},{8,0},{12,4},{16,24},{20,28},{24,16},{28,20},{1,9},{5... | collective-permute-start | bytes 442376 | tf_op jit(solution)/shard_map/ppermute | solution.py:546
  156.4 18.0 %collective-permute-start.35 = (bf16[192,384]{1,0:T(8,128)(2,1)S(1)}, bf16[192,384]{1,0:T(8,128)(2,1)S(1)}, u32[]{:S(2)}, u32[]{:S(2)}) collective-permute-start(bf16[192,384]{1,0:T(8,128)(2,1)S(1)} %bitcast.152), channel_id=1, source_target_pairs={{0,24},{4,28},{8,16},{12,20},{16,8},{20,12},{24,0},{28,4},{1,25},{... | collective-permute-start | bytes 442376 | tf_op jit(solution)/shard_map/ppermute | solution.py:546
  157.7 16.7 %collective-permute-start.36 = (bf16[192,384]{1,0:T(8,128)(2,1)S(1)}, bf16[192,384]{1,0:T(8,128)(2,1)S(1)}, u32[]{:S(2)}, u32[]{:S(2)}) collective-permute-start(bf16[192,384]{1,0:T(8,128)(2,1)S(1)} %bitcast.153), channel_id=1, source_target_pairs={{0,4},{4,0},{8,12},{12,8},{16,20},{20,16},{24,28},{28,24},{1,5},{5... | collective-permute-start | bytes 442376 | tf_op jit(solution)/shard_map/ppermute | solution.py:546
  159.8 23.1 %collective-permute-start.45 = (bf16[2,2,2,96,384]{4,3,2,1,0:T(8,128)(2,1)S(1)}, bf16[2,2,2,96,384]{4,3,2,1,0:T(8,128)(2,1)S(1)}, u32[]{:S(2)}, u32[]{:S(2)}) collective-permute-start(bf16[2,2,2,96,384]{4,3,2,1,0:T(8,128)(2,1)S(1)} %get-tuple-element.183), channel_id=1, source_target_pairs={{0,16},{4,20},{8,24},{12,28},{16,0},{20,4},{24,8},{28,12},{1,17},{... | collective-permute-start | bytes 1769480 | tf_op jit(solution)/shard_map/ppermute | solution.py:546
  174.9 48.7 %collective-permute-start.61 = (f32[12,768]{1,0:T(8,128)S(1)}, f32[12,768]{1,0:T(8,128)S(1)}, u32[]{:S(2)}, u32[]{:S(2)}) collective-permute-start(f32[12,768]{1,0:T(8,128)S(1)} %fusion.34), channel_id=1, source_target_pairs={{0,16},{4,20},{8,24},{12,28},{16,0},{20,4},{24,8},{28,12},{1,17},{... | collective-permute-start | bytes 110600 | tf_op jit(solution)/shard_map/ppermute | solution.py:546
  176.5 47.8 %collective-permute-start.62 = (f32[12,768]{1,0:T(8,128)S(1)}, f32[12,768]{1,0:T(8,128)S(1)}, u32[]{:S(2)}, u32[]{:S(2)}) collective-permute-start(f32[12,768]{1,0:T(8,128)S(1)} %fusion.34), channel_id=1, source_target_pairs={{0,8},{4,12},{8,0},{12,4},{16,24},{20,28},{24,16},{28,20},{1,9},{5... | collective-permute-start | bytes 110600 | tf_op jit(solution)/shard_map/ppermute | solution.py:546
  177.8 47.2 %collective-permute-start.63 = (f32[12,768]{1,0:T(8,128)S(1)}, f32[12,768]{1,0:T(8,128)S(1)}, u32[]{:S(2)}, u32[]{:S(2)}) collective-permute-start(f32[12,768]{1,0:T(8,128)S(1)} %fusion.34), channel_id=1, source_target_pairs={{0,24},{4,28},{8,16},{12,20},{16,8},{20,12},{24,0},{28,4},{1,25},{... | collective-permute-start | bytes 110600 | tf_op jit(solution)/shard_map/ppermute | solution.py:546
  181.5 8.5 %collective-permute-start.24 = (bf16[2,2,96,384]{3,2,1,0:T(8,128)(2,1)S(1)}, bf16[2,2,96,384]{3,2,1,0:T(8,128)(2,1)S(1)}, u32[]{:S(2)}, u32[]{:S(2)}) collective-permute-start(bf16[2,2,96,384]{3,2,1,0:T(8,128)(2,1)S(1)} %slice_bitcast_fusion.6), channel_id=1, source_target_pairs={{0,16},{4,20},{8,24},{12,28},{16,0},{20,4},{24,8},{28,12},{1,17},{... | collective-permute-start | bytes 884744 | tf_op jit(solution)/shard_map/ppermute | solution.py:546
  182.9 8.0 %collective-permute-start.26 = (bf16[2,2,96,384]{3,2,1,0:T(8,128)(2,1)S(1)}, bf16[2,2,96,384]{3,2,1,0:T(8,128)(2,1)S(1)}, u32[]{:S(2)}, u32[]{:S(2)}) collective-permute-start(bf16[2,2,96,384]{3,2,1,0:T(8,128)(2,1)S(1)} %slice_bitcast_fusion.4), channel_id=1, source_target_pairs={{0,8},{4,12},{8,0},{12,4},{16,24},{20,28},{24,16},{28,20},{1,9},{5... | collective-permute-start | bytes 884744 | tf_op jit(solution)/shard_map/ppermute | solution.py:546
  190.0 7.6 %collective-permute-start.44 = (bf16[2,2,96,384]{3,2,1,0:T(8,128)(2,1)S(1)}, bf16[2,2,96,384]{3,2,1,0:T(8,128)(2,1)S(1)}, u32[]{:S(2)}, u32[]{:S(2)}) collective-permute-start(bf16[2,2,96,384]{3,2,1,0:T(8,128)(2,1)S(1)} %slice_bitcast_fusion.2), channel_id=1, source_target_pairs={{0,16},{4,20},{8,24},{12,28},{16,0},{20,4},{24,8},{28,12},{1,17},{... | collective-permute-start | bytes 884744 | tf_op jit(solution)/shard_map/ppermute | solution.py:546
  190.9 7.5 %collective-permute-start.46 = (bf16[2,2,96,384]{3,2,1,0:T(8,128)(2,1)S(1)}, bf16[2,2,96,384]{3,2,1,0:T(8,128)(2,1)S(1)}, u32[]{:S(2)}, u32[]{:S(2)}) collective-permute-start(bf16[2,2,96,384]{3,2,1,0:T(8,128)(2,1)S(1)} %slice_bitcast_fusion), channel_id=1, source_target_pairs={{0,8},{4,12},{8,0},{12,4},{16,24},{20,28},{24,16},{28,20},{1,9},{5... | collective-permute-start | bytes 884744 | tf_op jit(solution)/shard_map/ppermute | solution.py:546
  197.6 11.5 %collective-permute-start.27 = (bf16[2,2,96,384]{3,2,0,1:T(8,128)(2,1)S(1)}, bf16[2,2,96,384]{3,2,0,1:T(8,128)(2,1)S(1)}, u32[]{:S(2)}, u32[]{:S(2)}) collective-permute-start(bf16[2,2,96,384]{3,2,0,1:T(8,128)(2,1)S(1)} %fusion.30), channel_id=1, source_target_pairs={{0,1},{1,0},{2,3},{3,2},{4,5},{5,4},{6,7},{7,6},{8,9},{9,8},{10,11... | collective-permute-start | bytes 884744 | tf_op jit(solution)/shard_map/ppermute | solution.py:549
  198.6 13.7 %collective-permute-start.47 = (bf16[2,2,96,384]{3,2,0,1:T(8,128)(2,1)S(1)}, bf16[2,2,96,384]{3,2,0,1:T(8,128)(2,1)S(1)}, u32[]{:S(2)}, u32[]{:S(2)}) collective-permute-start(bf16[2,2,96,384]{3,2,0,1:T(8,128)(2,1)S(1)} %fusion.28), channel_id=1, source_target_pairs={{0,1},{1,0},{2,3},{3,2},{4,5},{5,4},{6,7},{7,6},{8,9},{9,8},{10,11... | collective-permute-start | bytes 884744 | tf_op jit(solution)/shard_map/ppermute | solution.py:549
  209.2 11.6 %collective-permute-start.28 = (bf16[2,96,384]{2,1,0:T(8,128)(2,1)S(1)}, bf16[2,96,384]{2,1,0:T(8,128)(2,1)S(1)}, u32[]{:S(2)}, u32[]{:S(2)}) collective-permute-start(bf16[2,96,384]{2,1,0:T(8,128)(2,1)S(1)} %slice_bitcast_fusion.13), channel_id=1, source_target_pairs={{0,2},{1,3},{2,0},{3,1},{4,6},{5,7},{6,4},{7,5},{8,10},{9,11},{10,... | collective-permute-start | bytes 442376 | tf_op jit(solution)/shard_map/ppermute | solution.py:549
  212.4 9.9 %collective-permute-start.48 = (bf16[2,96,384]{2,1,0:T(8,128)(2,1)S(1)}, bf16[2,96,384]{2,1,0:T(8,128)(2,1)S(1)}, u32[]{:S(2)}, u32[]{:S(2)}) collective-permute-start(bf16[2,96,384]{2,1,0:T(8,128)(2,1)S(1)} %slice_bitcast_fusion.10), channel_id=1, source_target_pairs={{0,2},{1,3},{2,0},{3,1},{4,6},{5,7},{6,4},{7,5},{8,10},{9,11},{10,... | collective-permute-start | bytes 442376 | tf_op jit(solution)/shard_map/ppermute | solution.py:549
  222.3 6.7 %collective-permute-start.41 = (bf16[192,384]{1,0:T(8,128)(2,1)S(1)}, bf16[192,384]{1,0:T(8,128)(2,1)S(1)}, u32[]{:S(2)}, u32[]{:S(2)}) collective-permute-start(bf16[192,384]{1,0:T(8,128)(2,1)S(1)} %bitcast.141), channel_id=1, source_target_pairs={{0,8},{4,12},{8,0},{12,4},{16,24},{20,28},{24,16},{28,20},{1,9},{5... | collective-permute-start | bytes 442376 | tf_op jit(solution)/shard_map/ppermute | solution.py:546
  225.0 8.2 %collective-permute-start.51 = (bf16[192,384]{1,0:T(8,128)(2,1)S(1)}, bf16[192,384]{1,0:T(8,128)(2,1)S(1)}, u32[]{:S(2)}, u32[]{:S(2)}) collective-permute-start(bf16[192,384]{1,0:T(8,128)(2,1)S(1)} %bitcast.147), channel_id=1, source_target_pairs={{0,24},{4,28},{8,16},{12,20},{16,8},{20,12},{24,0},{28,4},{1,25},{... | collective-permute-start | bytes 442376 | tf_op jit(solution)/shard_map/ppermute | solution.py:546
  229.1 16.1 %collective-permute-start.21 = (bf16[256,768]{1,0:T(8,128)(2,1)S(1)}, bf16[256,768]{1,0:T(8,128)(2,1)S(1)}, u32[]{:S(2)}, u32[]{:S(2)}) collective-permute-start(bf16[256,768]{1,0:T(8,128)(2,1)S(1)} %get-tuple-element.217), channel_id=1, source_target_pairs={{1,0},{0,1},{5,2},{4,3},{3,4},{2,5},{7,6},{6,7},{9,8},{8,9},{13,10... | collective-permute-start | bytes 1179656 | tf_op jit(solution)/shard_map/ppermute | solution.py:576
  229.8 15.3 %collective-permute-start.22 = (bf16[256,768]{1,0:T(8,128)(2,1)S(1)}, bf16[256,768]{1,0:T(8,128)(2,1)S(1)}, u32[]{:S(2)}, u32[]{:S(2)}) collective-permute-start(bf16[256,768]{1,0:T(8,128)(2,1)S(1)} %get-tuple-element.218), channel_id=1, source_target_pairs={{0,0},{1,1},{4,2},{5,3},{2,4},{3,5},{6,6},{7,7},{8,8},{9,9},{12,10... | collective-permute-start | bytes 1179656 | tf_op jit(solution)/shard_map/ppermute | solution.py:576
  234.2 16.5 %collective-permute-start.64 = (f32[12,768]{1,0:T(8,128)S(1)}, f32[12,768]{1,0:T(8,128)S(1)}, u32[]{:S(2)}, u32[]{:S(2)}) collective-permute-start(f32[12,768]{1,0:T(8,128)S(1)} %add_add_fusion.a_ref), channel_id=1, source_target_pairs={{0,1},{1,0},{2,3},{3,2},{4,5},{5,4},{6,7},{7,6},{8,9},{9,8},{10,11... | collective-permute-start | bytes 110600 | tf_op jit(solution)/shard_map/ppermute | solution.py:549
  235.5 15.9 %collective-permute-start.65 = (f32[12,768]{1,0:T(8,128)S(1)}, f32[12,768]{1,0:T(8,128)S(1)}, u32[]{:S(2)}, u32[]{:S(2)}) collective-permute-start(f32[12,768]{1,0:T(8,128)S(1)} %add_add_fusion.a_ref), channel_id=1, source_target_pairs={{0,2},{1,3},{2,0},{3,1},{4,6},{5,7},{6,4},{7,5},{8,10},{9,11},{10,... | collective-permute-start | bytes 110600 | tf_op jit(solution)/shard_map/ppermute | solution.py:549
  243.9 8.8 %collective-permute-start.66 = (f32[12,768]{1,0:T(8,128)S(1)}, f32[12,768]{1,0:T(8,128)S(1)}, u32[]{:S(2)}, u32[]{:S(2)}) collective-permute-start(f32[12,768]{1,0:T(8,128)S(1)} %add_add_fusion.a_ref), channel_id=1, source_target_pairs={{0,3},{1,2},{2,1},{3,0},{4,7},{5,6},{6,5},{7,4},{8,11},{9,10},{10,... | collective-permute-start | bytes 110600 | tf_op jit(solution)/shard_map/ppermute | solution.py:549
  245.1 9.4 %collective-permute-start.56 = (bf16[192,384]{1,0:T(8,128)(2,1)S(1)}, bf16[192,384]{1,0:T(8,128)(2,1)S(1)}, u32[]{:S(2)}, u32[]{:S(2)}) collective-permute-start(bf16[192,384]{1,0:T(8,128)(2,1)S(1)} %bitcast.143), channel_id=1, source_target_pairs={{0,4},{4,0},{8,12},{12,8},{16,20},{20,16},{24,28},{28,24},{1,5},{5... | collective-permute-start | bytes 442376 | tf_op jit(solution)/shard_map/ppermute | solution.py:546
  245.1 9.4 %collective-permute-start.57 = (bf16[192,384]{1,0:T(8,128)(2,1)S(1)}, bf16[192,384]{1,0:T(8,128)(2,1)S(1)}, u32[]{:S(2)}, u32[]{:S(2)}) collective-permute-start(bf16[192,384]{1,0:T(8,128)(2,1)S(1)} %collective-permute-done.40.refs_1_), channel_id=1, source_target_pairs={{0,4},{4,0},{8,12},{12,8},{16,20},{20,16},{24,28},{28,24},{1,5},{5... | collective-permute-start | bytes 442376 | tf_op jit(solution)/shard_map/ppermute | solution.py:546
  (40 other events, 254.1 us)
where the time goes:
time: 261 us; the launch traced here: 257 us
  starting transfers between devices  84.3 us (32%)
  waiting for transfers between devices  82.9 us (32%)
  Pallas kernels  70.9 us (27%)
  other arithmetic  5.46 us (2%)
  matrix products  5.36 us (2%)
  between operations  4.55 us (2%)
  local copies, waits for them, and re-layouts  3.47 us (1%)
    pallas_call x14, Pallas kernels, call(): pl.pallas_call(kernel, grid_spec=pltpu.PrefetchScalarGridSpec(num_scalar_...  70.9 us
    ppermute x49, starting transfers between devices, over_dp(): return lax.ppermute(arr, 'dp', [(i, i ^ bit) for i in range(dp)])  60.9 us
    ppermute x49, waiting for transfers between devices, over_dp(): return lax.ppermute(arr, 'dp', [(i, i ^ bit) for i in range(dp)])  42.2 us
    ppermute x9, waiting for transfers between devices, over_seq(): return lax.ppermute(arr, 'seq', [(i, i ^ bit) for i in range(seq)])  26.9 us
    ppermute x9, starting transfers between devices, over_seq(): return lax.ppermute(arr, 'seq', [(i, i ^ bit) for i in range(seq)])  10.8 us
    ppermute x4, starting transfers between devices, send_block(): out.append(lax.ppermute(part, ('dp', 'seq'), ways[r]))  9.31 us
    ppermute x4, waiting for transfers between devices, return_block(): back.append(lax.ppermute(part, ('dp', 'seq'), [(b, a) for a, b in ways[r]]))  9.15 us
    dot_general x5, matrix products, mm(): return lax.dot_general(a, b, dims, preferred_element_type=f32)  5.36 us
  transfers between devices with their start and end apart: 67, of which 26 were waited for; matrix products, arithmetic and copies ran while one was open for 5% of the time, Pallas kernels for 21%

commit v1 on v0

--- a/solution.py
+++ b/solution.py
@@ -12,6 +12,9 @@
 bf16 = jnp.bfloat16
 NN = (((1,), (0,)), ((), ()))
 NT = (((1,), (1,)), ((), ()))
+TN = (((0,), (0,)), ((), ()))
+
+CHUNK = 256
 
 
 def mm(a, b, dims=NN):
@@ -52,40 +55,75 @@
     return place < jnp.where(place < half, first, second + half)
 
 
+def qkv_kernel(info, x_ref, xf_ref, w_ref, far_ref, bias_ref, q_ref, k_ref, v_ref, near):
+    t = pl.program_id(0)
+    near[...] = mm(x_ref[...], w_ref[...])
+
+    @pl.when(t == 0)
+    def _():
+        scale = bf16((q_ref.shape[1] // (info.shape[0] - 4)) ** -0.5)
+        q_ref[...] = (near[...] + bias_ref[0]).astype(bf16) * scale
+
+    @pl.when(t > 0)
+    def _():
+        picked = jnp.where(far_ref[...] == 1, mm(xf_ref[...], w_ref[...]), near[...])
+        picked = (picked + bias_ref[0]).astype(bf16)
+        for i, out_ref in ((1, k_ref), (2, v_ref)):
+            @pl.when(t == i)
+            def _():
+                out_ref[...] = picked
+
+
+def qkv(info, x, x_far, w, far, bias):
+    rows, width = x.shape
+    full = pl.BlockSpec((rows, width), lambda j, s: (0, 0))
+    return call(
+        qkv_kernel, (3,),
+        [full, full, pl.BlockSpec((width, width), lambda j, s: (0, j)), whole(far),
+         pl.BlockSpec((1, 1, width), lambda j, s: (j, 0, 0))],
+        [shape(rows, width)] * 3, [full] * 3, [pltpu.VMEM((rows, width), f32)],
+        info, x, x_far, w, far, bias, micros=5,
+    )
+
+
 def attn_fwd_kernel(info, q_ref, k_ref, v_ref, ctx_ref, p_ref):
-    pair = pl.program_id(0)
-    rows, lanes = q_ref.shape
+    rows = q_ref.shape[0]
+    lanes = 128
     hd = lanes // 2
     lane = lax.broadcasted_iota(jnp.int32, (rows, lanes), 1)
     place = lax.broadcasted_iota(jnp.int32, (rows, rows), 0)
-    q = q_ref[...]
-    k = k_ref[...]
-    vt = jnp.transpose(v_ref[...])
-    parts = []
-    for h in range(2):
-        mine = (lane < hd) if h == 0 else (lane >= hd)
-        s = mm(jnp.where(mine, k, jnp.zeros_like(k)), q, NT)
-        s = jnp.where(limits(info, pair, h, place, rows // 2), s, f32(-10000.0))
-        e = jnp.exp(s - jnp.max(s, 0, keepdims=True))
-        p = (e * (1.0 / jnp.sum(e, 0, keepdims=True))).astype(bf16)
-        p_ref[h] = p
-        parts.append(mm(vt[h * hd : (h + 1) * hd], p))
-    ctx_ref[...] = jnp.transpose(jnp.concatenate(parts, 0)).astype(bf16)
+    count = q_ref.shape[1] // lanes
+    for i in range(count):
+        cols = slice(i * lanes, (i + 1) * lanes)
+        q = q_ref[:, cols]
+        k = k_ref[:, cols]
+        v = v_ref[:, cols]
+        parts = []
+        for h in range(2):
+            mine = (lane < hd) if h == 0 else (lane >= hd)
+            s = mm(jnp.where(mine, k, jnp.zeros_like(k)), q, NT)
+            ok = limits(info, pl.program_id(0) * count + i, h, place, rows // 2)
+            s = jnp.where(ok, s, f32(-10000.0))
+            e = jnp.exp(s - jnp.max(s, 0, keepdims=True))
+            p = (e * (1.0 / jnp.sum(e, 0, keepdims=True))).astype(bf16)
+            p_ref[2 * i + h] = p
+            parts.append(mm(p, v, TN))
+        ctx_ref[:, cols] = jnp.where(lane < hd, parts[0], parts[1]).astype(bf16)
 
 
 def attn_fwd(info, q, k, v):
     rows, width = q.shape
     pairs = width // 128
-    blk = pl.BlockSpec((rows, 128), lambda j, s: (0, j))
-    sq = pl.BlockSpec((2, rows, rows), lambda j, s: (j, 0, 0))
-    return call(
-        attn_fwd_kernel, (pairs,), [blk] * 3,
+    blk = pl.BlockSpec((rows, 256), lambda j, s: (0, j))
+    sq = pl.BlockSpec((4, rows, rows), lambda j, s: (j, 0, 0))
+    return call(
+        attn_fwd_kernel, (pairs // 2,), [blk] * 3,
         [shape(rows, width), pltpu.HBM((2 * pairs, rows, rows), bf16)], [blk, sq], [], info, q, k, v,
     )
 
 
 def attn_bwd_kernel(
-    start, info, q_ref, k_ref, v_ref, g_ref, p_ref, dq_ref, dk_ref, dv_ref, vec_ref
+    start, info, q_ref, k_ref, v_ref, g_ref, c_ref, p_ref, dq_ref, dk_ref, dv_ref, vec_ref
 ):
     pair = pl.program_id(0) + start
     rows, lanes = q_ref.shape
@@ -101,12 +139,13 @@
     ok = jnp.where(lane < hd, jnp.where(oks[0], 1, 0), jnp.where(oks[1], 1, 0)) == 1
     kt = jnp.transpose(jnp.where(ok, k, zero))
     dvs, dks, dqs = [], [], []
+    prod = jnp.transpose(g.astype(f32) * c_ref[...].astype(f32))
     for h in range(2):
         mine = (lane < hd) if h == 0 else (lane >= hd)
         dp = mm(jnp.where(mine, v, zero), g, NT)
         pb = p_ref[h]
         p = pb.astype(f32)
-        inner = jnp.sum(p * dp, 0, keepdims=True)
+        inner = jnp.sum(prod[h * hd : (h + 1) * hd], 0, keepdims=True)
         ds = (p * (dp - inner)).astype(bf16)
         dvs.append(mm(pb, g))
         dks.append(mm(ds, q))
@@ -120,16 +159,16 @@
     vec_ref[1:2] = jnp.sum(dv.astype(f32), 0, keepdims=True)
 
 
-def attn_bwd(info, first, pairs, q, k, v, g, p):
+def attn_bwd(info, first, pairs, q, k, v, g, c, p):
     rows = q.shape[0]
     blk = pl.BlockSpec((rows, 128), lambda j, s: (0, j + first))
     sq = pl.BlockSpec((2, rows, rows), lambda j, s: (j + first, 0, 0))
     out = pl.BlockSpec((rows, 128), lambda j, s: (0, j))
     return call(
-        functools.partial(attn_bwd_kernel, first), (pairs,), [blk] * 4 + [sq],
+        functools.partial(attn_bwd_kernel, first), (pairs,), [blk] * 5 + [sq],
         [shape(rows, 128 * pairs)] * 3 + [shape(2, 128 * pairs, dtype=f32)],
         [out] * 3 + [pl.BlockSpec((2, 128), lambda j, s: (0, j))],
-        [], info, q, k, v, g, p, micros=6, mib=16,
+        [], info, q, k, v, g, c, p, micros=6, mib=16,
     )
 
 
@@ -145,6 +184,14 @@
         - jnp.mean(scaled, -1, keepdims=True)
         - normed * jnp.mean(scaled * normed, -1, keepdims=True)
     )
+
+
+def by_rows(rows, size, body):
+    def step(i, carry):
+        body(pl.ds(pl.multiple_of(i * size, size), size))
+        return carry
+
+    lax.fori_loop(0, rows // size, step, 0)
 
 
 def gelu_both(x):
@@ -177,7 +224,7 @@
     me, x_ref, ctx_ref, wo_ref, bo_ref, ga_ref, sa_ref, wu0, wu1, wu2, wu3, bu0, bu1, bu2, bu3,
     wd0, wd1, wd2, wd3, bd_ref, gf_ref, sf_ref, g0_ref, g1_ref,
     y_ref, n_ref, r_ref, am_ref, at_ref, dm_ref, dt_ref, out_ref, dtwo_ref, dffn_ref, vec_ref,
-    acc,
+    acc, grad,
 ):
     j = pl.program_id(0)
     rows = x_ref.shape[0]
@@ -185,11 +232,15 @@
 
     @pl.when(j == 0)
     def _():
-        resid = x_ref[...].astype(f32) + (mm(ctx_ref[...], wo_ref[...]) + bo_ref[...])
-        normed, rstd = normalize(resid)
-        n_ref[...] = normed
-        r_ref[...] = rstd
-        y_ref[...] = (normed * ga_ref[...] + sa_ref[...]).astype(bf16)
+        acc[...] = mm(ctx_ref[...], wo_ref[...])
+
+        def first(at):
+            normed, rstd = normalize(x_ref[at].astype(f32) + (acc[at] + bo_ref[...]))
+            n_ref[at] = normed
+            r_ref[at] = rstd
+            y_ref[at] = (normed * ga_ref[...] + sa_ref[...]).astype(bf16)
+
+        by_rows(rows, CHUNK // 2, first)
 
     y = y_ref[...]
     part = None
@@ -214,11 +265,13 @@
     def _():
         acc[...] += part
         vec_ref[...] = jnp.zeros_like(vec_ref)
-        for i, g_ref in enumerate((g0_ref, g1_ref)):
-            at = slice(i * part_len, (i + 1) * part_len)
+        grad[:part_len] = g0_ref[...]
+        grad[part_len:] = g1_ref[...]
+
+        def second(at):
             normed, rstd = normalize(y_ref[at].astype(f32) + (acc[at] + bd_ref[...]))
             out_ref[at] = (normed * gf_ref[...] + sf_ref[...]).astype(bf16)
-            g = g_ref[...].astype(f32)
+            g = grad[at].astype(f32)
             d_two = norm_back(g * gf_ref[...], normed, rstd)
             dtwo_ref[at] = d_two
             d_ffn = d_two.astype(bf16)
@@ -226,6 +279,8 @@
             vec_ref[0:1] += jnp.sum(g * normed, 0, keepdims=True)
             vec_ref[1:2] += jnp.sum(g, 0, keepdims=True)
             vec_ref[2:3] += jnp.sum(d_ffn.astype(f32), 0, keepdims=True)
+
+        by_rows(rows, CHUNK, second)
 
 
 def mid(me, x, ctx, wo, bo, ga, sa, wu, bu, wd, bd, gf, sf, g0, g1):
@@ -243,7 +298,7 @@
         [shape(rows, width), shape(rows, width, dtype=f32), rstd] + [shape(rows, ff // 2)] * 4
         + [shape(rows, width), shape(rows, width, dtype=f32), shape(rows, width), vec],
         [full, full, whole(rstd)] + [col] * 4 + [full, full, full, whole(vec)],
-        [pltpu.VMEM((rows, width), f32)],
+        [pltpu.VMEM((rows, width), f32), pltpu.VMEM((rows, width), bf16)],
         me, x, ctx, wo, bo, ga, sa, *[wu] * 4, *[bu] * 4, *[wd] * 4, bd, gf, sf, g0, g1,
         micros=18, mib=26,
     )
@@ -296,8 +351,8 @@
         acc[...] += part
         rows = acc.shape[0]
         vec_ref[...] = jnp.zeros_like(vec_ref)
-        for i in range(2):
-            at = slice(i * (rows // 2), (i + 1) * (rows // 2))
+
+        def last(at):
             d_y = acc[at] + dtwo_ref[at]
             normed = n_ref[at]
             d_one = norm_back(d_y * gain_ref[...], normed, r_ref[at])
@@ -307,6 +362,8 @@
             vec_ref[0:1] += jnp.sum(d_y * normed, 0, keepdims=True)
             vec_ref[1:2] += jnp.sum(d_y, 0, keepdims=True)
             vec_ref[2:3] += jnp.sum(d_attn.astype(f32), 0, keepdims=True)
+
+        by_rows(rows, CHUNK, last)
         dctx_ref[...] = mm(dattn_ref[...], wo_ref[...], NT).astype(bf16)
 
 
@@ -591,20 +648,21 @@
             head_swap,
         ]
     ).astype(jnp.int32)
-    far = jnp.repeat(head_swap, head_dim)[None, :] == 1
+    far_flag = jnp.repeat(head_swap, head_dim)[None, :]
+    biases = jnp.stack([bias_q, jnp.zeros_like(bias_q), bias_v])[:, None]
     given = [lax.dynamic_index_in_dim(cotangent, r ^ odd, 0, False) for r in range(2)]
-    near, info, far, me, second, odd_z, given = tie(
-        (near, info, far, me, core == 1, odd == 1, given)
-    )
+    near, info, far_flag, biases, me, second, odd_z, given = tie(
+        (near, info, far_flag, biases, me, core == 1, odd == 1, given)
+    )
+    far = far_flag == 1
     x = jnp.concatenate(near, 0)
     x_far = other(x)
     grad = send_block(tie(given, x))
 
-    q = (mm(x, w_qkv[:, :width]) + bias_q).astype(bf16) * bf16(head_dim**-0.5)
-    w_k, w_v = w_qkv[:, width : 2 * width], w_qkv[:, 2 * width :]
-    k = jnp.where(far, mm(x_far, w_k), mm(x, w_k)).astype(bf16)
-    v = (jnp.where(far, mm(x_far, w_v), mm(x, w_v)) + bias_v).astype(bf16)
+    w_hbm = pltpu.with_memory_space_constraint(w_qkv, pltpu.HBM)
+    q, k, v = qkv(info, x, x_far, w_hbm, far_flag, biases)
     ctx, probs = attn_fwd(info, q, k, v)
+    probs = pltpu.with_memory_space_constraint(probs, pltpu.HBM)
     ctx_far = other(ctx)
     y, normed, rstd, act_m, act_t, slope_m, slope_t, out, d_two, d_ffn, vec_two = mid(
         me, x, ctx, w_out, bias_out[None], gain_attn[None], shift_attn[None], w_up, bias_up[None],
@@ -616,17 +674,20 @@
 
     def halve_first(stored):
         a_keep, a_send, b_keep, b_send = stored
-        return (add(a_keep, over_dp(a_send, 2)), add(b_keep, over_dp(b_send, 4)))
+        a, b = over_dp(a_send, 2), over_dp(b_send, 4)
+        return add(a_keep, a), add(b_keep, b)
 
     def halve_second(pair):
         a, b = pair
-        return (add(a[0], over_dp(a[1], 4)), add(b[0], over_dp(b[1], 2)))
+        a_got, b_got = over_dp(a[1], 4), over_dp(b[1], 2)
+        return jnp.stack([add(a[0], a_got), add(b[0], b_got)], 2)
 
     def halve_seq_first(c):
-        return add(c[0], over_seq(c[1], 1))
-
-    def halve_seq_second(c):
-        c = add(c[0], over_seq(c[1], 2))
+        got = over_seq(c[1], 1)
+        return add(c[0], got)
+
+    def halve_seq_second(kept, got):
+        c = add(kept, got)
         bit = 8
         while bit < dp:
             c = add(c, over_dp(c, bit))
@@ -657,28 +718,24 @@
     def mine(pair):
         return jnp.where(second, pair[1], pair[0])
 
+    attn_far = other(jnp.where(second, d_attn[:, :half], d_attn[:, half:]))
+    y, d_ctx = tie((y, d_ctx))
+    up = grad_up(me, y, y_far, pre_m, pre_far)
+    d_ctx, up, down = tie((d_ctx, up, down))
+    up = halve_first(up)
+    down = halve_second(down)
     heads_far = [far[:, :half], far[:, half:]]
     pairs = heads // 4
     qs, ks, vs, k_gots, v_gots, vecs = [], [], [], [], [], []
     for i in range(2):
-        d_q, d_k, d_v, vec = attn_bwd(info, i * pairs, pairs, q, k, v, d_ctx, probs)
+        d_q, d_k, d_v, vec = attn_bwd(info, i * pairs, pairs, q, k, v, d_ctx, ctx, probs)
         qs.append(d_q)
         ks.append(d_k)
         vs.append(d_v)
         vecs.append(vec)
         k_gots.append(other(d_k))
         v_gots.append(other(d_v))
-        if i == 0:
-            attn_far = other(jnp.where(second, d_attn[:, :half], d_attn[:, half:]))
-            d_ctx, down, d_q = tie((d_ctx, down, d_q))
-            down = halve_second(down)
     q_far = other(jnp.where(second, qs[0], qs[1]))
-    down, qs = tie((down, qs))
-    down = halve_seq_first(jnp.stack(down, 2))
-    up = grad_up(me, y, y_far, pre_m, pre_far)
-    down, up = tie((down, up))
-    down = halve_seq_second(down)
-    up = halve_first(up)
     k_own = [jnp.where(f, g, u) for f, g, u in zip(heads_far, k_gots, ks)]
     k_oth = [jnp.where(f, u, g) for f, g, u in zip(heads_far, k_gots, ks)]
     v_own = [jnp.where(f, g, u) for f, g, u in zip(heads_far, v_gots, vs)]
@@ -688,11 +745,12 @@
         me, x, x_far, ctx, ctx_far, mine(qs), q_far, mine(k_own), mine(k_oth), mine(v_own),
         mine(v_oth), mine((d_attn[:, :half], d_attn[:, half:])), attn_far,
     )
-    rest, qs, vecs = tie((rest, qs, vecs))
+    rest, qs, vecs, down, up = tie((rest, qs, vecs, down, up))
     rest = halve_first(rest)
+    up = halve_second(up)
+    down = halve_seq_first(down)
     d_tok = tok(me, qs + k_own + v_own, w_qkv, d_one)
     d_tok = return_block(d_tok)
-    up = halve_second(up)
     vec = jnp.concatenate(
         [jnp.concatenate(vecs, 1), vec_one, vec_two, vec_up], 0
     )
@@ -701,25 +759,28 @@
     while bit < dp:
         vec = vec + over_dp(vec, bit)
         bit *= 2
-    v_y, v_x, v_d = tie([over_dp(vec, bit) for bit in (4, 2, 6)], rest)
+    v_got = [over_dp(vec, bit) for bit in (4, 2, 6)]
+    down_got = over_seq(down[1], 2)
+    up = halve_seq_first(up)
+    rest = halve_second(rest)
+    v_y, v_x, v_d = v_got
+    rest = halve_seq_first(rest)
+    up = halve_seq_second(up[0], over_seq(up[1], 2))
+    down = halve_seq_second(down[0], down_got)
     (s_down,) = place(me, place_down_kernel, [(width, width)], collect(down))
-    up = halve_seq_first(jnp.stack(up, 2))
-    rest = halve_second(rest)
     vec = (vec + v_y) + (v_x + v_d)
     vec_z = [vec] + [over_seq(vec, bit) for bit in (1, 2, 3)]
-    rest = halve_seq_first(jnp.stack(rest, 2))
-    up = halve_seq_second(up)
+    rest = halve_seq_second(rest[0], over_seq(rest[1], 2))
     (s_up,) = place(me, place_up_kernel, [(width // seq, w_up.shape[1])], collect(up))
-    rest = tie(halve_seq_second(rest), s_down)
-    rest = collect(rest, s_up)
+    d_tokens = in_order(d_tok).astype(f32)
+    vec = place_vec(me, vec_z)
+    rest = collect(rest)
     s_qkv, s_out = place(
         me, place_rest_kernel, [(width // seq, 3 * width), (width // seq, width)], rest
     )
     output = in_order(output)
-    d_tokens = in_order(d_tok).astype(f32)
-
     s_bq, s_bv, s_ga, s_sa, s_bo, s_gf, s_sf, s_bd, s_b_up = (
-        v.reshape(-1) for v in place_vec(me, vec_z)
+        v.reshape(-1) for v in vec
     )
     return (
         output, d_tokens, s_qkv, s_bq, s_bv, s_out, s_bo, s_ga, s_sa, s_up, s_b_up, s_down, s_bd,

time: 261 us -> 247 us (0.946); the launches traced: 257 us -> 246 us
  waiting for transfers between devices: 82.9 us -> 63.6 us
  Pallas kernels: 70.9 us -> 76.4 us
  matrix products: 5.36 us -> 0 us
  other arithmetic: 5.46 us -> 10.7 us
  local copies, waits for them, and re-layouts: 3.47 us -> 6.47 us
    ppermute x49, waiting for transfers between devices: 42.2 us -> 34.1 us  [over_dp(): return lax.ppermute(arr, 'dp', [(i, i ^ bit) for i in range(dp)])]
    ppermute x9, waiting for transfers between devices: 26.9 us -> 19 us  [over_seq(): return lax.ppermute(arr, 'seq', [(i, i ^ bit) for i in range(seq)])]
    pallas_call x14 -> x15, Pallas kernels: 70.9 us -> 76.4 us  [call(): pl.pallas_call(kernel, grid_spec=pltpu.PrefetchScalarGridSpec(num_scalar_...]
    dot_general x5 -> x0, matrix products: 5.36 us -> none  [mm(): return lax.dot_general(a, b, dims, preferred_element_type=f32)]
    ppermute x4, waiting for transfers between devices: 9.15 us -> 5.78 us  [return_block(): back.append(lax.ppermute(part, ('dp', 'seq'), [(b, a) for a, b in ways[r]]))]
    convert_element_type x14 -> x12, other arithmetic: 1.43 us -> 4.48 us  [add(): return (a.astype(f32) + b.astype(f32)).astype(bf16)]
  transfers between devices with their start and end apart: 67 -> 67, of which waited for: 26 -> 22; matrix products, arithmetic and copies ran while one was open for 5% -> 6% of each run, Pallas kernels for 21% -> 24%
where the time goes in v1:
time: 247 us; the launch traced here: 246 us
  starting transfers between devices  85.1 us (34%)
  Pallas kernels  76.4 us (31%)
  waiting for transfers between devices  63.6 us (26%)
  other arithmetic  10.7 us (4%)
  local copies, waits for them, and re-layouts  6.47 us (3%)
  between operations  4 us (2%)
    pallas_call x15, Pallas kernels, call(): pl.pallas_call(kernel, grid_spec=pltpu.PrefetchScalarGridSpec(num_scalar_...  76.4 us
    ppermute x49, starting transfers between devices, over_dp(): return lax.ppermute(arr, 'dp', [(i, i ^ bit) for i in range(dp)])  59.4 us
    ppermute x49, waiting for transfers between devices, over_dp(): return lax.ppermute(arr, 'dp', [(i, i ^ bit) for i in range(dp)])  34.1 us
    ppermute x9, waiting for transfers between devices, over_seq(): return lax.ppermute(arr, 'seq', [(i, i ^ bit) for i in range(seq)])  19 us
    ppermute x9, starting transfers between devices, over_seq(): return lax.ppermute(arr, 'seq', [(i, i ^ bit) for i in range(seq)])  10.8 us
    ppermute x4, starting transfers between devices, send_block(): out.append(lax.ppermute(part, ('dp', 'seq'), ways[r]))  9.33 us
    ppermute x4, waiting for transfers between devices, return_block(): back.append(lax.ppermute(part, ('dp', 'seq'), [(b, a) for a, b in ways[r]]))  5.78 us
  transfers between devices with their start and end apart: 67, of which 22 were waited for; matrix products, arithmetic and copies ran while one was open for 6% of the time, Pallas kernels for 24%

profile of v1, /device:TPU:0, one launch (start us, length us, event | category | flops | bytes accessed | tf_op | source)
XLA Modules:
  0.0 246.3 jit_solution(15826749184329719614)
XLA Ops:
  2.0 1.9 collective-permute-start.2
  5.7 3.1 %collective-permute-start.1 = (bf16[256,768]{1,0:T(8,128)(2,1)S(1)}, bf16[256,768]{1,0:T(8,128)(2,1)S(1)}, u32[]{:S(2)}, u32[]{:S(2)}) collective-permute-start(bf16[256,768]{1,0:T(8,128)(2,1)S(1)} %get-tuple-element.219), channel_id=1, source_target_pairs={{0,1},{1,0},{2,5},{3,4},{4,3},{5,2},{6,7},{7,6},{8,9},{9,8},{10,13... | collective-permute-start | bytes 1179656 | tf_op jit(solution)/shard_map/ppermute | solution.py:623
  12.0 4.7 %collective-permute-done.1 = bf16[256,768]{1,0:T(8,128)(2,1)S(1)} collective-permute-done((bf16[256,768]{1,0:T(8,128)(2,1)S(1)}, bf16[256,768]{1,0:T(8,128)(2,1)S(1)}, u32[]{:S(2)}, u32[]{:S(2)}) %collective-permute-start.1) | collective-permute-done | bytes 393248 | tf_op jit(solution)/shard_map/ppermute | solution.py:623
  16.8 11.0 %collective-permute-start.3 = (bf16[512,768]{1,0:T(8,128)(2,1)S(1)}, bf16[512,768]{1,0:T(8,128)(2,1)S(1)}, u32[]{:S(2)}, u32[]{:S(2)}) collective-permute-start(bf16[512,768]{1,0:T(8,128)(2,1)S(1)} %constant_dynamic-update-slice_fusion.x_ref.xo_ref), channel_id=1, source_target_pairs={{0,4},{4,0},{8,12},{12,8},{16,20},{20,16},{24,28},{28,24},{1,5},{5... | collective-permute-start | bytes 2359304 | tf_op jit(solution)/shard_map/ppermute | solution.py:603
  28.6 4.8 %collective-permute-start.5 = (bf16[256,768]{1,0:T(8,128)(2,1)S(1)}, bf16[256,768]{1,0:T(8,128)(2,1)S(1)}, u32[]{:S(2)}, u32[]{:S(2)}) collective-permute-start(bf16[256,768]{1,0:T(8,128)(2,1)S(1)} %get-tuple-element.121), channel_id=1, source_target_pairs={{0,1},{1,0},{2,5},{3,4},{4,3},{5,2},{6,7},{7,6},{8,9},{9,8},{10,13... | collective-permute-start | bytes 1179656 | tf_op jit(solution)/shard_map/ppermute | solution.py:623
  33.5 6.3 %shard_map.280 = (bf16[512,768]{1,0:T(8,128)(2,1)S(1)}, bf16[512,768]{1,0:T(8,128)(2,1)S(1)}, bf16[512,768]{1,0:T(8,128)(2,1)S(1)}) custom-call(s32[16]{0:T(128)S(1)} %concatenate.12.info, bf16[512,768]{1,0:T(8,128)(2,1)S(1)} %constant_dynamic-update-slice_fusion.x_ref.xo_ref, bf16[512,768]{1,0:T(8,128)(2,1)S(1)} %collective-permute-done.3.xf_ref.xp_ref, ...), custom_call_target="tpu_custom_call" | custom-call | flops 5000000000 | bytes 8000000 | tf_op jit(solution)/shard_map/pallas_call | solution.py:34
  39.9 9.0 %shard_map.281 = (bf16[512,768]{1,0:T(8,128)(2,1)S(1)}, bf16[12,512,512]{2,1,0:T(8,128)(2,1)}) custom-call(s32[16]{0:T(128)S(1)} %concatenate.12.info, bf16[512,768]{1,0:T(8,128)(2,1)S(1)} %get-tuple-element.114.q_ref, bf16[512,768]{1,0:T(8,128)(2,1)S(1)} %get-tuple-element.115.k_ref, bf16[512,768]{1,0:T(8,128)(2,1)S(1)} %get-tuple-element.116.v_ref), custom_call_target="tpu_custom_call" | custom-call | flops 8000000000 | bytes 8000000 | tf_op jit(solution)/shard_map/pallas_call | solution.py:34
  49.0 14.3 %shard_map.282 = (bf16[512,768]{1,0:T(8,128)(2,1)S(1)}, f32[512,768]{1,0:T(8,128)S(1)}, f32[512,1]{1,0:T(8,128)S(1)}, bf16[512,1536]{1,0:T(8,128)(2,1)S(1)}, bf1...) custom-call(s32[4]{0:T(128)S(1)} %pad_add_fusion.me, ...), custom_call_target="tpu_custom_call" | custom-call | flops 17999998976 | bytes 8000000 | tf_op jit(solution)/shard_map/pallas_call | solution.py:34
  63.3 3.4 %collective-permute-start.10 = (bf16[512,1536]{1,0:T(8,128)(2,1)S(1)}, bf16[512,1536]{1,0:T(8,128)(2,1)S(1)}, u32[]{:S(2)}, u32[]{:S(2)}) collective-permute-start(bf16[512,1536]{1,0:T(8,128)(2,1)S(1)} %get-tuple-element.131), channel_id=1, source_target_pairs={{0,4},{4,0},{8,12},{12,8},{16,20},{20,16},{24,28},{28,24},{1,5},{5... | collective-permute-start | bytes 4718600 | tf_op jit(solution)/shard_map/ppermute | solution.py:603
  66.8 4.0 %shard_map.283 = (bf16[512,1536]{1,0:T(8,128)(2,1)S(1)}, bf16[512,1536]{1,0:T(8,128)(2,1)S(1)}, f32[4,768]{1,0:T(4,128)S(1)}) custom-call(s32[4]{0:T(128)S(1)} %pad_add_fusion.me, bf16[512,768]{1,0:T(8,128)(2,1)S(1)} %get-tuple-element.123.dffn_ref.lo_ref, bf16[3072,768]{1,0:T(8,128)(2,1)S(1)} %bitcast.133, bf16[3072,768]{1,0:T(8,128)(2,1)S(1)} %bitcast.133, ...), custom_call_target="tpu_custom_call" | custom-call | flops 6000000000 | bytes 8000000 | tf_op jit(solution)/shard_map/pallas_call | solution.py:34
  72.4 2.9 %collective-permute-start.12 = (bf16[512,1536]{1,0:T(8,128)(2,1)S(1)}, bf16[512,1536]{1,0:T(8,128)(2,1)S(1)}, u32[]{:S(2)}, u32[]{:S(2)}) collective-permute-start(bf16[512,1536]{1,0:T(8,128)(2,1)S(1)} %get-tuple-element.137.pt_ref), channel_id=1, source_target_pairs={{0,4},{4,0},{8,12},{12,8},{16,20},{20,16},{24,28},{28,24},{1,5},{5... | collective-permute-start | bytes 4718600 | tf_op jit(solution)/shard_map/ppermute | solution.py:603
  75.3 5.8 %collective-permute-done.6 = bf16[256,768]{1,0:T(8,128)(2,1)S(1)} collective-permute-done((bf16[256,768]{1,0:T(8,128)(2,1)S(1)}, bf16[256,768]{1,0:T(8,128)(2,1)S(1)}, u32[]{:S(2)}, u32[]{:S(2)}) %collective-permute-start.6) | collective-permute-done | bytes 393248 | tf_op jit(solution)/shard_map/ppermute | solution.py:633
  81.1 2.3 collective-permute-start.8
  83.4 7.9 %collective-permute-start.11 = (bf16[512,768]{1,0:T(8,128)(2,1)S(1)}, bf16[512,768]{1,0:T(8,128)(2,1)S(1)}, u32[]{:S(2)}, u32[]{:S(2)}) collective-permute-start(bf16[512,768]{1,0:T(8,128)(2,1)S(1)} %get-tuple-element.143.lo_ref), channel_id=1, source_target_pairs={{0,4},{4,0},{8,12},{12,8},{16,20},{20,16},{24,28},{28,24},{1,5},{5... | collective-permute-start | bytes 2359304 | tf_op jit(solution)/shard_map/ppermute | solution.py:603
  92.3 4.6 %shard_map.284 = (bf16[2,2,2,96,384]{4,3,2,1,0:T(8,128)(2,1)S(1)}, bf16[2,2,2,96,384]{4,3,2,1,0:T(8,128)(2,1)S(1)}, bf16[2,2,2,96,384]{4,3,2,1,0:T(8,128)(2,1)S(1)}, bf16[2,2,2,96,384]{4,3,2,1,0:T(8,128)(2,1)S(1)}) custom-call(s32[4]{0:T(128)S(1)} %pad_add_fusion.me, bf16[512,768]{1,0:T(8,128)(2,1)S(1)} %get-tuple-element.123.dffn_ref.lo_ref, ...), custom_call_target="tpu_custom_call" | custom-call | flops 6000000000 | bytes 8000000 | tf_op jit(solution)/shard_map/pallas_call | solution.py:34
  96.9 1.6 collective-permute-start.14
  98.5 1.5 collective-permute-start.13
  100.0 6.4 %shard_map.285 = (f32[512,768]{1,0:T(8,128)S(1)}, bf16[512,768]{1,0:T(8,128)(2,1)S(1)}, bf16[512,768]{1,0:T(8,128)(2,1)S(1)}, f32[3,768]{1,0:T(4,128)S(1)}) custom-call(s32[4]{0:T(128)S(1)} %pad_add_fusion.me, bf16[512,1536]{1,0:T(8,128)(2,1)S(1)} %get-tuple-element.136.pm_ref.ro_ref, bf16[512,1536]{1,0:T(8,128)(2,1)S(1)} %get-tuple-element.137.pt_ref, ...), custom_call_target="tpu_custom_call" | custom-call | flops 8000000000 | bytes 8000000 | tf_op jit(solution)/shard_map/pallas_call | solution.py:34
  106.4 4.4 %shard_map.286 = (bf16[2,2,2,96,384]{4,3,2,1,0:T(8,128)(2,1)S(1)}, bf16[2,2,2,96,384]{4,3,2,1,0:T(8,128)(2,1)S(1)}, bf16[2,2,2,96,384]{4,3,2,1,0:T(8,128)(2,1)S(1)}, bf16[2,2,2,96,384]{4,3,2,1,0:T(8,128)(2,1)S(1)}) custom-call(s32[4]{0:T(128)S(1)} %pad_add_fusion.me, bf16[512,768]{1,0:T(8,128)(2,1)S(1)} %get-tuple-element.143.lo_ref, ...), custom_call_target="tpu_custom_call" | custom-call | flops 6000000000 | bytes 8000000 | tf_op jit(solution)/shard_map/pallas_call | solution.py:34
  114.2 1.6 collective-permute-start.22
  115.8 6.1 %shard_map.287 = (bf16[512,384]{1,0:T(8,128)(2,1)S(1)}, bf16[512,384]{1,0:T(8,128)(2,1)S(1)}, bf16[512,384]{1,0:T(8,128)(2,1)S(1)}, f32[2,384]{1,0:T(2,128)S(1)}) custom-call(s32[16]{0:T(128)S(1)} %concatenate.12.info, bf16[512,768]{1,0:T(8,128)(2,1)S(1)} %get-tuple-element.114.q_ref, bf16[512,768]{1,0:T(8,128)(2,1)S(1)} %get-tuple-element.115.k_ref, ...), custom_call_target="tpu_custom_call" | custom-call | flops 6000000000 | bytes 8000000 | tf_op jit(solution)/shard_map/pallas_call | solution.py:34
  121.9 6.3 %shard_map.288 = (bf16[512,384]{1,0:T(8,128)(2,1)S(1)}, bf16[512,384]{1,0:T(8,128)(2,1)S(1)}, bf16[512,384]{1,0:T(8,128)(2,1)S(1)}, f32[2,384]{1,0:T(2,128)S(1)}) custom-call(s32[16]{0:T(128)S(1)} %concatenate.12.info, bf16[512,768]{1,0:T(8,128)(2,1)S(1)} %get-tuple-element.114.q_ref, bf16[512,768]{1,0:T(8,128)(2,1)S(1)} %get-tuple-element.115.k_ref, ...), custom_call_target="tpu_custom_call" | custom-call | flops 6000000000 | bytes 8000000 | tf_op jit(solution)/shard_map/pallas_call | solution.py:34
  131.0 1.5 collective-permute-start.24
  133.5 4.1 %shard_map.289 = (bf16[2,2,2,96,384]{4,3,2,1,0:T(8,128)(2,1)S(1)}, bf16[2,2,2,96,384]{4,3,2,1,0:T(8,128)(2,1)S(1)}, bf16[2,2,2,96,384]{4,3,2,1,0:T(8,128)(2,1)S(1)}, bf16[2,2,2,96,384]{4,3,2,1,0:T(8,128)(2,1)S(1)}) custom-call(s32[4]{0:T(128)S(1)} %pad_add_fusion.me, bf16[512,768]{1,0:T(8,128)(2,1)S(1)} %constant_dynamic-update-slice_fusion.x_ref.xo_ref, ...), custom_call_target="tpu_custom_call" | custom-call | flops 6000000000 | bytes 8000000 | tf_op jit(solution)/shard_map/pallas_call | solution.py:34
  137.6 8.8 %collective-permute-done.24 = bf16[2,2,2,96,384]{4,3,2,1,0:T(8,128)(2,1)S(1)} collective-permute-done((bf16[2,2,2,96,384]{4,3,2,1,0:T(8,128)(2,1)S(1)}, bf16[2,2,2,96,384]{4,3,2,1,0:T(8,128)(2,1)S(1)}, u32[]{:S(2)}, u32[]{:S(2)}) %collective-permute-start.24) | collective-permute-done | bytes 589856 | tf_op jit(solution)/shard_map/ppermute | solution.py:603
  150.3 2.6 %shard_map.290 = bf16[512,768]{1,0:T(8,128)(2,1)S(1)} custom-call(s32[4]{0:T(128)S(1)} %pad_add_fusion.me, bf16[512,384]{1,0:T(8,128)(2,1)S(1)} %get-tuple-element.173.q0, bf16[512,384]{1,0:T(8,128)(2,1)S(1)} %get-tuple-element.174.q1, bf16[512,384]{1,0:T(8,128)(2,1)S(1)} %get-tuple-element.223.k0, bf16[512,384]{1,0:T(8,128)(2,1)S(1)} %get-tuple-element.224.k1, ...), custom_call_target="tpu_custom_call" | custom-call | flops 5000000000 | bytes 8000000 | tf_op jit(solution)/shard_map/pallas_call | solution.py:34
  154.7 1.8 collective-permute-start.43
  157.4 1.5 collective-permute-done.41
  159.7 2.1 collective-permute-start.44
  161.8 1.6 collective-permute-start.45
  165.5 1.5 collective-permute-start.48
  173.7 1.7 collective-permute-start.26
  176.4 4.6 %collective-permute-start.59 = (bf16[2,96,384]{2,1,0:T(8,128)(2,1)S(1)}, bf16[2,96,384]{2,1,0:T(8,128)(2,1)S(1)}, u32[]{:S(2)}, u32[]{:S(2)}) collective-permute-start(bf16[2,96,384]{2,1,0:T(8,128)(2,1)S(1)} %slice_bitcast_fusion.10), channel_id=1, source_target_pairs={{0,2},{1,3},{2,0},{3,1},{4,6},{5,7},{6,4},{7,5},{8,10},{9,11},{10,... | collective-permute-start | bytes 442376 | tf_op jit(solution)/shard_map/ppermute | solution.py:606
  182.2 3.8 %collective-permute-done.27 = bf16[2,2,2,96,384]{4,3,2,1,0:T(8,128)(2,1)} collective-permute-done((bf16[2,2,2,96,384]{4,3,2,1,0:T(8,128)(2,1)S(1)}, bf16[2,2,2,96,384]{4,3,2,1,0:T(8,128)(2,1)}, u32[]{:S(2)}, u32[]{:S(2)}) %collective-permute-start.27) | collective-permute-done | bytes 589856 | tf_op jit(solution)/shard_map/ppermute | solution.py:603
  189.9 10.1 %collective-permute-done.49 = bf16[2,2,96,384]{3,2,0,1:T(8,128)(2,1)S(1)} collective-permute-done((bf16[2,2,96,384]{3,2,0,1:T(8,128)(2,1)S(1)}, bf16[2,2,96,384]{3,2,0,1:T(8,128)(2,1)S(1)}, u32[]{:S(2)}, u32[]{:S(2)}) %collective-permute-start.49) | collective-permute-done | bytes 294944 | tf_op jit(solution)/shard_map/ppermute | solution.py:606
  201.0 5.8 %collective-permute-done.30 = bf16[2,2,96,384]{3,2,1,0:T(8,128)(2,1)S(1)} collective-permute-done((bf16[2,2,96,384]{3,2,1,0:T(8,128)(2,1)S(1)}, bf16[2,2,96,384]{3,2,1,0:T(8,128)(2,1)S(1)}, u32[]{:S(2)}, u32[]{:S(2)}) %collective-permute-start.30) | collective-permute-done | bytes 294944 | tf_op jit(solution)/shard_map/ppermute | solution.py:603
  208.7 1.5 collective-permute-start.61
  210.3 3.4 %collective-permute-done.31 = bf16[2,2,96,384]{3,2,0,1:T(8,128)(2,1)S(1)} collective-permute-done((bf16[2,2,96,384]{3,2,0,1:T(8,128)(2,1)S(1)}, bf16[2,2,96,384]{3,2,0,1:T(8,128)(2,1)S(1)}, u32[]{:S(2)}, u32[]{:S(2)}) %collective-permute-start.31) | collective-permute-done | bytes 294944 | tf_op jit(solution)/shard_map/ppermute | solution.py:606
  213.7 2.2 collective-permute-start.62
  217.8 2.0 collective-permute-done.62.refs_3_
  221.0 2.0 collective-permute-start.52
  223.9 3.8 %collective-permute-done.32 = bf16[2,96,384]{2,1,0:T(8,128)(2,1)S(1)} collective-permute-done((bf16[2,96,384]{2,1,0:T(8,128)(2,1)S(1)}, bf16[2,96,384]{2,1,0:T(8,128)(2,1)S(1)}, u32[]{:S(2)}, u32[]{:S(2)}) %collective-permute-start.32) | collective-permute-done | bytes 147488 | tf_op jit(solution)/shard_map/ppermute | solution.py:606
  228.3 2.9 %collective-permute-done.53.refs_3_ = bf16[192,384]{1,0:T(8,128)(2,1)S(1)} collective-permute-done((bf16[192,384]{1,0:T(8,128)(2,1)S(1)}, bf16[192,384]{1,0:T(8,128)(2,1)S(1)}, u32[]{:S(2)}, u32[]{:S(2)}) %collective-permute-start.53) | collective-permute-done | bytes 147488 | tf_op jit(solution)/shard_map/ppermute | solution.py:603
  232.1 1.7 collective-permute-start.34
  234.7 2.7 %shard_map.294 = f32[768,768]{1,0:T(8,128)} custom-call(s32[4]{0:T(128)S(1)} %pad_add_fusion.me, bf16[192,384]{1,0:T(8,128)(2,1)S(1)} %bitcast.143, bf16[192,384]{1,0:T(8,128)(2,1)S(1)} %collective-permute-done.60.refs_1_, bf16[192,384]{1,0:T(8,128)(2,1)S(1)} %collective-permute-done.61.refs_2_, bf16[192,384]{1,0:T(8,128)(2,1)S(1)} %collective-permute-done.62.refs_3_, ...), custom_call_target="tpu_custom_call" | custom-call | flops 3000000000 | bytes 8000000 | tf_op jit(solution)/shard_map/pallas_call | solution.py:34
  238.8 3.0 %collective-permute-done.35.refs_3_ = bf16[192,384]{1,0:T(8,128)(2,1)S(1)} collective-permute-done((bf16[192,384]{1,0:T(8,128)(2,1)S(1)}, bf16[192,384]{1,0:T(8,128)(2,1)S(1)}, u32[]{:S(2)}, u32[]{:S(2)}) %collective-permute-start.35) | collective-permute-done | bytes 147488 | tf_op jit(solution)/shard_map/ppermute | solution.py:603
  241.8 2.2 shard_map.293
  244.1 2.2 shard_map.291
  (207 shorter events, 47.5 us)
Async XLA Ops:
  2.0 7.4 %collective-permute-start.2 = (s32[1]{0:T(128)}, s32[1]{0:T(128)}, u32[]{:S(2)}, u32[]{:S(2)}) collective-permute-start(s32[1]{0:T(128)} %dynamic_slice.18), channel_id=1, source_target_pairs={{0,0},{1,1},{2,4},{3,5},{4,2},{5,3},{6,6},{7,7},{8,8},{9,9},{10,12... | collective-permute-start | bytes 20 | tf_op jit(solution)/shard_map/ppermute | solution.py:640
  5.1 7.0 %collective-permute-start = (bf16[256,768]{1,0:T(8,128)(2,1)S(1)}, bf16[256,768]{1,0:T(8,128)(2,1)S(1)}, u32[]{:S(2)}, u32[]{:S(2)}) collective-permute-start(bf16[256,768]{1,0:T(8,128)(2,1)S(1)} %get-tuple-element.220), channel_id=1, source_target_pairs={{0,0},{1,1},{2,4},{3,5},{4,2},{5,3},{6,6},{7,7},{8,8},{9,9},{10,12... | collective-permute-start | bytes 1179656 | tf_op jit(solution)/shard_map/ppermute | solution.py:623
  5.7 11.0 %collective-permute-start.1 = (bf16[256,768]{1,0:T(8,128)(2,1)S(1)}, bf16[256,768]{1,0:T(8,128)(2,1)S(1)}, u32[]{:S(2)}, u32[]{:S(2)}) collective-permute-start(bf16[256,768]{1,0:T(8,128)(2,1)S(1)} %get-tuple-element.219), channel_id=1, source_target_pairs={{0,1},{1,0},{2,5},{3,4},{4,3},{5,2},{6,7},{7,6},{8,9},{9,8},{10,13... | collective-permute-start | bytes 1179656 | tf_op jit(solution)/shard_map/ppermute | solution.py:623
  16.8 16.7 %collective-permute-start.3 = (bf16[512,768]{1,0:T(8,128)(2,1)S(1)}, bf16[512,768]{1,0:T(8,128)(2,1)S(1)}, u32[]{:S(2)}, u32[]{:S(2)}) collective-permute-start(bf16[512,768]{1,0:T(8,128)(2,1)S(1)} %constant_dynamic-update-slice_fusion.x_ref.xo_ref), channel_id=1, source_target_pairs={{0,4},{4,0},{8,12},{12,8},{16,20},{20,16},{24,28},{28,24},{1,5},{5... | collective-permute-start | bytes 2359304 | tf_op jit(solution)/shard_map/ppermute | solution.py:603
  27.9 21.0 %collective-permute-start.4 = (bf16[256,768]{1,0:T(8,128)(2,1)S(1)}, bf16[256,768]{1,0:T(8,128)(2,1)S(1)}, u32[]{:S(2)}, u32[]{:S(2)}) collective-permute-start(bf16[256,768]{1,0:T(8,128)(2,1)S(1)} %get-tuple-element.120), channel_id=1, source_target_pairs={{0,0},{1,1},{2,4},{3,5},{4,2},{5,3},{6,6},{7,7},{8,8},{9,9},{10,12... | collective-permute-start | bytes 1179656 | tf_op jit(solution)/shard_map/ppermute | solution.py:623
  28.6 20.3 %collective-permute-start.5 = (bf16[256,768]{1,0:T(8,128)(2,1)S(1)}, bf16[256,768]{1,0:T(8,128)(2,1)S(1)}, u32[]{:S(2)}, u32[]{:S(2)}) collective-permute-start(bf16[256,768]{1,0:T(8,128)(2,1)S(1)} %get-tuple-element.121), channel_id=1, source_target_pairs={{0,1},{1,0},{2,5},{3,4},{4,3},{5,2},{6,7},{7,6},{8,9},{9,8},{10,13... | collective-permute-start | bytes 1179656 | tf_op jit(solution)/shard_map/ppermute | solution.py:623
  63.3 28.9 %collective-permute-start.10 = (bf16[512,1536]{1,0:T(8,128)(2,1)S(1)}, bf16[512,1536]{1,0:T(8,128)(2,1)S(1)}, u32[]{:S(2)}, u32[]{:S(2)}) collective-permute-start(bf16[512,1536]{1,0:T(8,128)(2,1)S(1)} %get-tuple-element.131), channel_id=1, source_target_pairs={{0,4},{4,0},{8,12},{12,8},{16,20},{20,16},{24,28},{28,24},{1,5},{5... | collective-permute-start | bytes 4718600 | tf_op jit(solution)/shard_map/ppermute | solution.py:603
  66.7 25.5 %collective-permute-start.9 = (bf16[512,768]{1,0:T(8,128)(2,1)S(1)}, bf16[512,768]{1,0:T(8,128)(2,1)S(1)}, u32[]{:S(2)}, u32[]{:S(2)}) collective-permute-start(bf16[512,768]{1,0:T(8,128)(2,1)S(1)} %get-tuple-element.123.dffn_ref.lo_ref), channel_id=1, source_target_pairs={{0,4},{4,0},{8,12},{12,8},{16,20},{20,16},{24,28},{28,24},{1,5},{5... | collective-permute-start | bytes 2359304 | tf_op jit(solution)/shard_map/ppermute | solution.py:603
  70.9 10.2 %collective-permute-start.6 = (bf16[256,768]{1,0:T(8,128)(2,1)S(1)}, bf16[256,768]{1,0:T(8,128)(2,1)S(1)}, u32[]{:S(2)}, u32[]{:S(2)}) collective-permute-start(bf16[256,768]{1,0:T(8,128)(2,1)S(1)} %get-tuple-element.215), channel_id=1, source_target_pairs={{1,0},{0,1},{5,2},{4,3},{3,4},{2,5},{7,6},{6,7},{9,8},{8,9},{13,10... | collective-permute-start | bytes 1179656 | tf_op jit(solution)/shard_map/ppermute | solution.py:633
  71.6 11.9 %collective-permute-start.7 = (bf16[256,768]{1,0:T(8,128)(2,1)S(1)}, bf16[256,768]{1,0:T(8,128)(2,1)S(1)}, u32[]{:S(2)}, u32[]{:S(2)}) collective-permute-start(bf16[256,768]{1,0:T(8,128)(2,1)S(1)} %get-tuple-element.216), channel_id=1, source_target_pairs={{0,0},{1,1},{4,2},{5,3},{2,4},{3,5},{6,6},{7,7},{8,8},{9,9},{12,10... | collective-permute-start | bytes 1179656 | tf_op jit(solution)/shard_map/ppermute | solution.py:633
  72.4 34.0 %collective-permute-start.12 = (bf16[512,1536]{1,0:T(8,128)(2,1)S(1)}, bf16[512,1536]{1,0:T(8,128)(2,1)S(1)}, u32[]{:S(2)}, u32[]{:S(2)}) collective-permute-start(bf16[512,1536]{1,0:T(8,128)(2,1)S(1)} %get-tuple-element.137.pt_ref), channel_id=1, source_target_pairs={{0,4},{4,0},{8,12},{12,8},{16,20},{20,16},{24,28},{28,24},{1,5},{5... | collective-permute-start | bytes 4718600 | tf_op jit(solution)/shard_map/ppermute | solution.py:603
  81.1 52.3 %collective-permute-start.8 = (bf16[512,768]{1,0:T(8,128)(2,1)S(1)}, bf16[512,768]{1,0:T(8,128)(2,1)S(1)}, u32[]{:S(2)}, u32[]{:S(2)}) collective-permute-start(bf16[512,768]{1,0:T(8,128)(2,1)S(1)} %get-tuple-element.117.ctx_ref.c_ref.co_ref), channel_id=1, source_target_pairs={{0,4},{4,0},{8,12},{12,8},{16,20},{20,16},{24,28},{28,24},{1,5},{5... | collective-permute-start | bytes 2359304 | tf_op jit(solution)/shard_map/ppermute | solution.py:603
  83.4 23.0 %collective-permute-start.11 = (bf16[512,768]{1,0:T(8,128)(2,1)S(1)}, bf16[512,768]{1,0:T(8,128)(2,1)S(1)}, u32[]{:S(2)}, u32[]{:S(2)}) collective-permute-start(bf16[512,768]{1,0:T(8,128)(2,1)S(1)} %get-tuple-element.143.lo_ref), channel_id=1, source_target_pairs={{0,4},{4,0},{8,12},{12,8},{16,20},{20,16},{24,28},{28,24},{1,5},{5... | collective-permute-start | bytes 2359304 | tf_op jit(solution)/shard_map/ppermute | solution.py:603
  96.9 15.3 %collective-permute-start.14 = (bf16[2,2,2,96,384]{4,3,2,1,0:T(8,128)(2,1)S(1)}, bf16[2,2,2,96,384]{4,3,2,1,0:T(8,128)(2,1)S(1)}, u32[]{:S(2)}, u32[]{:S(2)}) collective-permute-start(bf16[2,2,2,96,384]{4,3,2,1,0:T(8,128)(2,1)S(1)} %get-tuple-element.151), channel_id=1, source_target_pairs={{0,16},{4,20},{8,24},{12,28},{16,0},{20,4},{24,8},{28,12},{1,17},{... | collective-permute-start | bytes 1769480 | tf_op jit(solution)/shard_map/ppermute | solution.py:603
  98.5 15.0 %collective-permute-start.13 = (bf16[2,2,2,96,384]{4,3,2,1,0:T(8,128)(2,1)S(1)}, bf16[2,2,2,96,384]{4,3,2,1,0:T(8,128)(2,1)S(1)}, u32[]{:S(2)}, u32[]{:S(2)}) collective-permute-start(bf16[2,2,2,96,384]{4,3,2,1,0:T(8,128)(2,1)S(1)} %get-tuple-element.149), channel_id=1, source_target_pairs={{0,8},{4,12},{8,0},{12,4},{16,24},{20,28},{24,16},{28,20},{1,9},{5... | collective-permute-start | bytes 1769480 | tf_op jit(solution)/shard_map/ppermute | solution.py:603
  113.6 15.2 %collective-permute-start.21 = (bf16[2,2,96,384]{3,2,1,0:T(8,128)(2,1)S(1)}, bf16[2,2,96,384]{3,2,1,0:T(8,128)(2,1)S(1)}, u32[]{:S(2)}, u32[]{:S(2)}) collective-permute-start(bf16[2,2,96,384]{3,2,1,0:T(8,128)(2,1)S(1)} %slice_bitcast_fusion.9), channel_id=1, source_target_pairs={{0,16},{4,20},{8,24},{12,28},{16,0},{20,4},{24,8},{28,12},{1,17},{... | collective-permute-start | bytes 884744 | tf_op jit(solution)/shard_map/ppermute | solution.py:603
  114.2 14.7 %collective-permute-start.22 = (bf16[2,2,96,384]{3,2,1,0:T(8,128)(2,1)S(1)}, bf16[2,2,96,384]{3,2,1,0:T(8,128)(2,1)S(1)}, u32[]{:S(2)}, u32[]{:S(2)}) collective-permute-start(bf16[2,2,96,384]{3,2,1,0:T(8,128)(2,1)S(1)} %slice_bitcast_fusion.8), channel_id=1, source_target_pairs={{0,8},{4,12},{8,0},{12,4},{16,24},{20,28},{24,16},{28,20},{1,9},{5... | collective-permute-start | bytes 884744 | tf_op jit(solution)/shard_map/ppermute | solution.py:603
  131.0 15.4 %collective-permute-start.24 = (bf16[2,2,2,96,384]{4,3,2,1,0:T(8,128)(2,1)S(1)}, bf16[2,2,2,96,384]{4,3,2,1,0:T(8,128)(2,1)S(1)}, u32[]{:S(2)}, u32[]{:S(2)}) collective-permute-start(bf16[2,2,2,96,384]{4,3,2,1,0:T(8,128)(2,1)S(1)} %get-tuple-element.172), channel_id=1, source_target_pairs={{0,16},{4,20},{8,24},{12,28},{16,0},{20,4},{24,8},{28,12},{1,17},{... | collective-permute-start | bytes 1769480 | tf_op jit(solution)/shard_map/ppermute | solution.py:603
  132.6 15.1 %collective-permute-start.23 = (bf16[2,2,2,96,384]{4,3,2,1,0:T(8,128)(2,1)S(1)}, bf16[2,2,2,96,384]{4,3,2,1,0:T(8,128)(2,1)S(1)}, u32[]{:S(2)}, u32[]{:S(2)}) collective-permute-start(bf16[2,2,2,96,384]{4,3,2,1,0:T(8,128)(2,1)S(1)} %get-tuple-element.170), channel_id=1, source_target_pairs={{0,8},{4,12},{8,0},{12,4},{16,24},{20,28},{24,16},{28,20},{1,9},{5... | collective-permute-start | bytes 1769480 | tf_op jit(solution)/shard_map/ppermute | solution.py:603
  148.6 23.4 %collective-permute-start.58 = (bf16[2,2,96,384]{3,2,0,1:T(8,128)(2,1)}, bf16[2,2,96,384]{3,2,0,1:T(8,128)(2,1)}, u32[]{:S(2)}, u32[]{:S(2)}) collective-permute-start(bf16[2,2,96,384]{3,2,0,1:T(8,128)(2,1)} %slice_bitcast_fusion.5), channel_id=1, source_target_pairs={{0,1},{1,0},{2,3},{3,2},{4,5},{5,4},{6,7},{7,6},{8,9},{9,8},{10,11... | collective-permute-start | bytes 884744 | tf_op jit(solution)/shard_map/ppermute | solution.py:606
  149.3 24.4 %collective-permute-start.47 = (bf16[2,2,96,384]{3,2,1,0:T(8,128)(2,1)}, bf16[2,2,96,384]{3,2,1,0:T(8,128)(2,1)}, u32[]{:S(2)}, u32[]{:S(2)}) collective-permute-start(bf16[2,2,96,384]{3,2,1,0:T(8,128)(2,1)} %slice_bitcast_fusion.7), channel_id=1, source_target_pairs={{0,16},{4,20},{8,24},{12,28},{16,0},{20,4},{24,8},{28,12},{1,17},{... | collective-permute-start | bytes 884744 | tf_op jit(solution)/shard_map/ppermute | solution.py:603
  161.8 6.3 %collective-permute-start.45 = (f32[12,768]{1,0:T(8,128)S(1)}, f32[12,768]{1,0:T(8,128)S(1)}, u32[]{:S(2)}, u32[]{:S(2)}) collective-permute-start(f32[12,768]{1,0:T(8,128)S(1)} %add_add_fusion.a_ref), channel_id=1, source_target_pairs={{0,2},{1,3},{2,0},{3,1},{4,6},{5,7},{6,4},{7,5},{8,10},{9,11},{10,... | collective-permute-start | bytes 110600 | tf_op jit(solution)/shard_map/ppermute | solution.py:606
  165.5 10.9 %collective-permute-start.48 = (bf16[2,2,96,384]{3,2,1,0:T(8,128)(2,1)}, bf16[2,2,96,384]{3,2,1,0:T(8,128)(2,1)}, u32[]{:S(2)}, u32[]{:S(2)}) collective-permute-start(bf16[2,2,96,384]{3,2,1,0:T(8,128)(2,1)} %slice_bitcast_fusion.6), channel_id=1, source_target_pairs={{0,8},{4,12},{8,0},{12,4},{16,24},{20,28},{24,16},{28,20},{1,9},{5... | collective-permute-start | bytes 884744 | tf_op jit(solution)/shard_map/ppermute | solution.py:603
  168.0 17.9 %collective-permute-start.27 = (bf16[2,2,2,96,384]{4,3,2,1,0:T(8,128)(2,1)S(1)}, bf16[2,2,2,96,384]{4,3,2,1,0:T(8,128)(2,1)}, u32[]{:S(2)}, u32[]{:S(2)}) collective-permute-start(bf16[2,2,2,96,384]{4,3,2,1,0:T(8,128)(2,1)S(1)} %get-tuple-element.177), channel_id=1, source_target_pairs={{0,8},{4,12},{8,0},{12,4},{16,24},{20,28},{24,16},{28,20},{1,9},{5... | collective-permute-start | bytes 1769480 | tf_op jit(solution)/shard_map/ppermute | solution.py:603
  169.3 18.5 %collective-permute-start.29 = (bf16[2,2,2,96,384]{4,3,2,1,0:T(8,128)(2,1)S(1)}, bf16[2,2,2,96,384]{4,3,2,1,0:T(8,128)(2,1)}, u32[]{:S(2)}, u32[]{:S(2)}) collective-permute-start(bf16[2,2,2,96,384]{4,3,2,1,0:T(8,128)(2,1)S(1)} %get-tuple-element.179), channel_id=1, source_target_pairs={{0,16},{4,20},{8,24},{12,28},{16,0},{20,4},{24,8},{28,12},{1,17},{... | collective-permute-start | bytes 1769480 | tf_op jit(solution)/shard_map/ppermute | solution.py:603
  172.0 44.0 %collective-permute-start.25 = (bf16[256,768]{1,0:T(8,128)(2,1)}, bf16[256,768]{1,0:T(8,128)(2,1)S(1)}, u32[]{:S(2)}, u32[]{:S(2)}) collective-permute-start(bf16[256,768]{1,0:T(8,128)(2,1)} %get-tuple-element.209), channel_id=1, source_target_pairs={{1,0},{0,1},{5,2},{4,3},{3,4},{2,5},{7,6},{6,7},{9,8},{8,9},{13,10... | collective-permute-start | bytes 1179656 | tf_op jit(solution)/shard_map/ppermute | solution.py:633
  173.7 42.9 %collective-permute-start.26 = (bf16[256,768]{1,0:T(8,128)(2,1)}, bf16[256,768]{1,0:T(8,128)(2,1)S(1)}, u32[]{:S(2)}, u32[]{:S(2)}) collective-permute-start(bf16[256,768]{1,0:T(8,128)(2,1)} %get-tuple-element.210), channel_id=1, source_target_pairs={{0,0},{1,1},{4,2},{5,3},{2,4},{3,5},{6,6},{7,7},{8,8},{9,9},{12,10... | collective-permute-start | bytes 1179656 | tf_op jit(solution)/shard_map/ppermute | solution.py:633
  176.4 31.0 %collective-permute-start.59 = (bf16[2,96,384]{2,1,0:T(8,128)(2,1)S(1)}, bf16[2,96,384]{2,1,0:T(8,128)(2,1)S(1)}, u32[]{:S(2)}, u32[]{:S(2)}) collective-permute-start(bf16[2,96,384]{2,1,0:T(8,128)(2,1)S(1)} %slice_bitcast_fusion.10), channel_id=1, source_target_pairs={{0,2},{1,3},{2,0},{3,1},{4,6},{5,7},{6,4},{7,5},{8,10},{9,11},{10,... | collective-permute-start | bytes 442376 | tf_op jit(solution)/shard_map/ppermute | solution.py:606
  186.0 14.1 %collective-permute-start.49 = (bf16[2,2,96,384]{3,2,0,1:T(8,128)(2,1)S(1)}, bf16[2,2,96,384]{3,2,0,1:T(8,128)(2,1)S(1)}, u32[]{:S(2)}, u32[]{:S(2)}) collective-permute-start(bf16[2,2,96,384]{3,2,0,1:T(8,128)(2,1)S(1)} %fusion.20), channel_id=1, source_target_pairs={{0,1},{1,0},{2,3},{3,2},{4,5},{5,4},{6,7},{7,6},{8,9},{9,8},{10,11... | collective-permute-start | bytes 884744 | tf_op jit(solution)/shard_map/ppermute | solution.py:606
  187.8 13.0 %collective-permute-start.28 = (bf16[2,2,96,384]{3,2,1,0:T(8,128)(2,1)S(1)}, bf16[2,2,96,384]{3,2,1,0:T(8,128)(2,1)S(1)}, u32[]{:S(2)}, u32[]{:S(2)}) collective-permute-start(bf16[2,2,96,384]{3,2,1,0:T(8,128)(2,1)S(1)} %slice_bitcast_fusion.3), channel_id=1, source_target_pairs={{0,16},{4,20},{8,24},{12,28},{16,0},{20,4},{24,8},{28,12},{1,17},{... | collective-permute-start | bytes 884744 | tf_op jit(solution)/shard_map/ppermute | solution.py:603
  200.0 6.7 %collective-permute-start.30 = (bf16[2,2,96,384]{3,2,1,0:T(8,128)(2,1)S(1)}, bf16[2,2,96,384]{3,2,1,0:T(8,128)(2,1)S(1)}, u32[]{:S(2)}, u32[]{:S(2)}) collective-permute-start(bf16[2,2,96,384]{3,2,1,0:T(8,128)(2,1)S(1)} %slice_bitcast_fusion.1), channel_id=1, source_target_pairs={{0,8},{4,12},{8,0},{12,4},{16,24},{20,28},{24,16},{28,20},{1,9},{5... | collective-permute-start | bytes 884744 | tf_op jit(solution)/shard_map/ppermute | solution.py:603
  200.8 7.9 %collective-permute-start.50 = (bf16[2,96,384]{2,1,0:T(8,128)(2,1)S(1)}, bf16[2,96,384]{2,1,0:T(8,128)(2,1)S(1)}, u32[]{:S(2)}, u32[]{:S(2)}) collective-permute-start(bf16[2,96,384]{2,1,0:T(8,128)(2,1)S(1)} %slice_bitcast_fusion.12), channel_id=1, source_target_pairs={{0,2},{1,3},{2,0},{3,1},{4,6},{5,7},{6,4},{7,5},{8,10},{9,11},{10,... | collective-permute-start | bytes 442376 | tf_op jit(solution)/shard_map/ppermute | solution.py:606
  206.9 6.8 %collective-permute-start.31 = (bf16[2,2,96,384]{3,2,0,1:T(8,128)(2,1)S(1)}, bf16[2,2,96,384]{3,2,0,1:T(8,128)(2,1)S(1)}, u32[]{:S(2)}, u32[]{:S(2)}) collective-permute-start(bf16[2,2,96,384]{3,2,0,1:T(8,128)(2,1)S(1)} %fusion.21), channel_id=1, source_target_pairs={{0,1},{1,0},{2,3},{3,2},{4,5},{5,4},{6,7},{7,6},{8,9},{9,8},{10,11... | collective-permute-start | bytes 884744 | tf_op jit(solution)/shard_map/ppermute | solution.py:606
  207.5 8.6 %collective-permute-start.60 = (bf16[192,384]{1,0:T(8,128)(2,1)S(1)}, bf16[192,384]{1,0:T(8,128)(2,1)S(1)}, u32[]{:S(2)}, u32[]{:S(2)}) collective-permute-start(bf16[192,384]{1,0:T(8,128)(2,1)S(1)} %bitcast.139), channel_id=1, source_target_pairs={{0,16},{4,20},{8,24},{12,28},{16,0},{20,4},{24,8},{28,12},{1,17},{... | collective-permute-start | bytes 442376 | tf_op jit(solution)/shard_map/ppermute | solution.py:603
  208.7 7.8 %collective-permute-start.61 = (bf16[192,384]{1,0:T(8,128)(2,1)S(1)}, bf16[192,384]{1,0:T(8,128)(2,1)S(1)}, u32[]{:S(2)}, u32[]{:S(2)}) collective-permute-start(bf16[192,384]{1,0:T(8,128)(2,1)S(1)} %bitcast.140), channel_id=1, source_target_pairs={{0,8},{4,12},{8,0},{12,4},{16,24},{20,28},{24,16},{28,20},{1,9},{5... | collective-permute-start | bytes 442376 | tf_op jit(solution)/shard_map/ppermute | solution.py:603
  216.5 6.5 %collective-permute-start.65 = (bf16[192,384]{1,0:T(8,128)(2,1)S(1)}, bf16[192,384]{1,0:T(8,128)(2,1)S(1)}, u32[]{:S(2)}, u32[]{:S(2)}) collective-permute-start(bf16[192,384]{1,0:T(8,128)(2,1)S(1)} %collective-permute-done.61.refs_2_), channel_id=1, source_target_pairs={{0,4},{4,0},{8,12},{12,8},{16,20},{20,16},{24,28},{28,24},{1,5},{5... | collective-permute-start | bytes 442376 | tf_op jit(solution)/shard_map/ppermute | solution.py:603
  216.6 7.3 %collective-permute-start.51 = (bf16[192,384]{1,0:T(8,128)(2,1)S(1)}, bf16[192,384]{1,0:T(8,128)(2,1)S(1)}, u32[]{:S(2)}, u32[]{:S(2)}) collective-permute-start(bf16[192,384]{1,0:T(8,128)(2,1)S(1)} %bitcast.134), channel_id=1, source_target_pairs={{0,16},{4,20},{8,24},{12,28},{16,0},{20,4},{24,8},{28,12},{1,17},{... | collective-permute-start | bytes 442376 | tf_op jit(solution)/shard_map/ppermute | solution.py:603
  219.7 8.0 %collective-permute-start.32 = (bf16[2,96,384]{2,1,0:T(8,128)(2,1)S(1)}, bf16[2,96,384]{2,1,0:T(8,128)(2,1)S(1)}, u32[]{:S(2)}, u32[]{:S(2)}) collective-permute-start(bf16[2,96,384]{2,1,0:T(8,128)(2,1)S(1)} %slice_bitcast_fusion.14), channel_id=1, source_target_pairs={{0,2},{1,3},{2,0},{3,1},{4,6},{5,7},{6,4},{7,5},{8,10},{9,11},{10,... | collective-permute-start | bytes 442376 | tf_op jit(solution)/shard_map/ppermute | solution.py:606
  221.0 10.2 %collective-permute-start.66 = (bf16[192,384]{1,0:T(8,128)(2,1)S(1)}, bf16[192,384]{1,0:T(8,128)(2,1)S(1)}, u32[]{:S(2)}, u32[]{:S(2)}) collective-permute-start(bf16[192,384]{1,0:T(8,128)(2,1)S(1)} %collective-permute-done.62.refs_3_), channel_id=1, source_target_pairs={{0,4},{4,0},{8,12},{12,8},{16,20},{20,16},{24,28},{28,24},{1,5},{5... | collective-permute-start | bytes 442376 | tf_op jit(solution)/shard_map/ppermute | solution.py:603
  221.0 6.8 %collective-permute-start.52 = (bf16[192,384]{1,0:T(8,128)(2,1)S(1)}, bf16[192,384]{1,0:T(8,128)(2,1)S(1)}, u32[]{:S(2)}, u32[]{:S(2)}) collective-permute-start(bf16[192,384]{1,0:T(8,128)(2,1)S(1)} %bitcast.135), channel_id=1, source_target_pairs={{0,8},{4,12},{8,0},{12,4},{16,24},{20,28},{24,16},{28,20},{1,9},{5... | collective-permute-start | bytes 442376 | tf_op jit(solution)/shard_map/ppermute | solution.py:603
  223.0 8.2 %collective-permute-start.53 = (bf16[192,384]{1,0:T(8,128)(2,1)S(1)}, bf16[192,384]{1,0:T(8,128)(2,1)S(1)}, u32[]{:S(2)}, u32[]{:S(2)}) collective-permute-start(bf16[192,384]{1,0:T(8,128)(2,1)S(1)} %bitcast.136), channel_id=1, source_target_pairs={{0,24},{4,28},{8,16},{12,20},{16,8},{20,12},{24,0},{28,4},{1,25},{... | collective-permute-start | bytes 442376 | tf_op jit(solution)/shard_map/ppermute | solution.py:603
  223.9 8.2 %collective-permute-start.54 = (bf16[192,384]{1,0:T(8,128)(2,1)S(1)}, bf16[192,384]{1,0:T(8,128)(2,1)S(1)}, u32[]{:S(2)}, u32[]{:S(2)}) collective-permute-start(bf16[192,384]{1,0:T(8,128)(2,1)S(1)} %bitcast.137), channel_id=1, source_target_pairs={{0,4},{4,0},{8,12},{12,8},{16,20},{20,16},{24,28},{28,24},{1,5},{5... | collective-permute-start | bytes 442376 | tf_op jit(solution)/shard_map/ppermute | solution.py:603
  227.8 9.7 %collective-permute-start.56 = (bf16[192,384]{1,0:T(8,128)(2,1)S(1)}, bf16[192,384]{1,0:T(8,128)(2,1)S(1)}, u32[]{:S(2)}, u32[]{:S(2)}) collective-permute-start(bf16[192,384]{1,0:T(8,128)(2,1)S(1)} %collective-permute-done.52.refs_2_), channel_id=1, source_target_pairs={{0,4},{4,0},{8,12},{12,8},{16,20},{20,16},{24,28},{28,24},{1,5},{5... | collective-permute-start | bytes 442376 | tf_op jit(solution)/shard_map/ppermute | solution.py:603
  231.2 10.6 %collective-permute-start.57 = (bf16[192,384]{1,0:T(8,128)(2,1)S(1)}, bf16[192,384]{1,0:T(8,128)(2,1)S(1)}, u32[]{:S(2)}, u32[]{:S(2)}) collective-permute-start(bf16[192,384]{1,0:T(8,128)(2,1)S(1)} %collective-permute-done.53.refs_3_), channel_id=1, source_target_pairs={{0,4},{4,0},{8,12},{12,8},{16,20},{20,16},{24,28},{28,24},{1,5},{5... | collective-permute-start | bytes 442376 | tf_op jit(solution)/shard_map/ppermute | solution.py:603
  232.1 6.7 %collective-permute-start.34 = (bf16[192,384]{1,0:T(8,128)(2,1)S(1)}, bf16[192,384]{1,0:T(8,128)(2,1)S(1)}, u32[]{:S(2)}, u32[]{:S(2)}) collective-permute-start(bf16[192,384]{1,0:T(8,128)(2,1)S(1)} %bitcast.145), channel_id=1, source_target_pairs={{0,8},{4,12},{8,0},{12,4},{16,24},{20,28},{24,16},{28,20},{1,9},{5... | collective-permute-start | bytes 442376 | tf_op jit(solution)/shard_map/ppermute | solution.py:603
  233.8 8.0 %collective-permute-start.35 = (bf16[192,384]{1,0:T(8,128)(2,1)S(1)}, bf16[192,384]{1,0:T(8,128)(2,1)S(1)}, u32[]{:S(2)}, u32[]{:S(2)}) collective-permute-start(bf16[192,384]{1,0:T(8,128)(2,1)S(1)} %bitcast.146), channel_id=1, source_target_pairs={{0,24},{4,28},{8,16},{12,20},{16,8},{20,12},{24,0},{28,4},{1,25},{... | collective-permute-start | bytes 442376 | tf_op jit(solution)/shard_map/ppermute | solution.py:603
  237.5 6.6 %collective-permute-start.36 = (bf16[192,384]{1,0:T(8,128)(2,1)S(1)}, bf16[192,384]{1,0:T(8,128)(2,1)S(1)}, u32[]{:S(2)}, u32[]{:S(2)}) collective-permute-start(bf16[192,384]{1,0:T(8,128)(2,1)S(1)} %bitcast.147), channel_id=1, source_target_pairs={{0,4},{4,0},{8,12},{12,8},{16,20},{20,16},{24,28},{28,24},{1,5},{5... | collective-permute-start | bytes 442376 | tf_op jit(solution)/shard_map/ppermute | solution.py:603
  237.5 6.6 %collective-permute-start.37 = (bf16[192,384]{1,0:T(8,128)(2,1)S(1)}, bf16[192,384]{1,0:T(8,128)(2,1)S(1)}, u32[]{:S(2)}, u32[]{:S(2)}) collective-permute-start(bf16[192,384]{1,0:T(8,128)(2,1)S(1)} %collective-permute-done.33.refs_1_), channel_id=1, source_target_pairs={{0,4},{4,0},{8,12},{12,8},{16,20},{20,16},{24,28},{28,24},{1,5},{5... | collective-permute-start | bytes 442376 | tf_op jit(solution)/shard_map/ppermute | solution.py:603
  (39 other events, 328.3 us)

commit v2 on v1

--- a/solution.py
+++ b/solution.py
@@ -223,7 +223,7 @@
 def mid_kernel(
     me, x_ref, ctx_ref, wo_ref, bo_ref, ga_ref, sa_ref, wu0, wu1, wu2, wu3, bu0, bu1, bu2, bu3,
     wd0, wd1, wd2, wd3, bd_ref, gf_ref, sf_ref, g0_ref, g1_ref,
-    y_ref, n_ref, r_ref, am_ref, at_ref, dm_ref, dt_ref, out_ref, dtwo_ref, dffn_ref, vec_ref,
+    y_ref, n_ref, r_ref, am_ref, at_ref, dm_ref, dt_ref, out0, out1, dtwo_ref, dffn_ref, vec_ref,
     acc, grad,
 ):
     j = pl.program_id(0)
@@ -240,7 +240,7 @@
             r_ref[at] = rstd
             y_ref[at] = (normed * ga_ref[...] + sa_ref[...]).astype(bf16)
 
-        by_rows(rows, CHUNK // 2, first)
+        by_rows(rows, CHUNK, first)
 
     y = y_ref[...]
     part = None
@@ -270,7 +270,12 @@
 
         def second(at):
             normed, rstd = normalize(y_ref[at].astype(f32) + (acc[at] + bd_ref[...]))
-            out_ref[at] = (normed * gf_ref[...] + sf_ref[...]).astype(bf16)
+            out = (normed * gf_ref[...] + sf_ref[...]).astype(bf16)
+            for k, out_ref in ((0, out0), (1, out1)):
+                @pl.when(at.start == k * part_len)
+                def _():
+                    out_ref[...] = out
+
             g = grad[at].astype(f32)
             d_two = norm_back(g * gf_ref[...], normed, rstd)
             dtwo_ref[at] = d_two
@@ -280,7 +285,7 @@
             vec_ref[1:2] += jnp.sum(g, 0, keepdims=True)
             vec_ref[2:3] += jnp.sum(d_ffn.astype(f32), 0, keepdims=True)
 
-        by_rows(rows, CHUNK, second)
+        by_rows(rows, part_len, second)
 
 
 def mid(me, x, ctx, wo, bo, ga, sa, wu, bu, wd, bd, gf, sf, g0, g1):
@@ -296,8 +301,9 @@
         [full, full, whole(wo), whole(bo), whole(ga), whole(sa)] + quarters(wu, 1, cut)
         + quarters(bu, 1, cut) + quarters(wd, 0, cut) + [whole(bd), whole(gf), whole(sf), whole(g0), whole(g1)],
         [shape(rows, width), shape(rows, width, dtype=f32), rstd] + [shape(rows, ff // 2)] * 4
-        + [shape(rows, width), shape(rows, width, dtype=f32), shape(rows, width), vec],
-        [full, full, whole(rstd)] + [col] * 4 + [full, full, full, whole(vec)],
+        + [shape(rows // 2, width)] * 2
+        + [shape(rows, width, dtype=f32), shape(rows, width), vec],
+        [full, full, whole(rstd)] + [col] * 4 + [whole(g0)] * 2 + [full, full, whole(vec)],
         [pltpu.VMEM((rows, width), f32), pltpu.VMEM((rows, width), bf16)],
         me, x, ctx, wo, bo, ga, sa, *[wu] * 4, *[bu] * 4, *[wd] * 4, bd, gf, sf, g0, g1,
         micros=18, mib=26,
@@ -502,11 +508,14 @@
     )
 
 
-def tok_kernel(me, q0, q1, k0, k1, v0, v1, wq_ref, wk_ref, wv_ref, done_ref, out_ref):
+def tok_kernel(me, q0, q1, k0, k1, v0, v1, wq_ref, wk_ref, wv_ref, done_ref, out0, out1):
     total = done_ref[...]
     for first, second, w_ref in ((q0, q1, wq_ref), (k0, k1, wk_ref), (v0, v1, wv_ref)):
         total = total + mm(jnp.concatenate([first[...], second[...]], 1), w_ref[...], NT)
-    out_ref[...] = total.astype(bf16)
+    total = total.astype(bf16)
+    half = out0.shape[0]
+    out0[...] = total[:half]
+    out1[...] = total[half:]
 
 
 def tok(me, parts, w, done):
@@ -514,7 +523,7 @@
     thirds = [pl.BlockSpec((width, width), lambda j, s, t=t: (0, t)) for t in range(3)]
     return call(
         tok_kernel, (1,), [whole(a) for a in parts] + thirds + [whole(done)],
-        shape(rows, width), pl.BlockSpec((rows, width), lambda j, s: (0, 0)), [],
+        [shape(rows // 2, width)] * 2, [pl.BlockSpec((rows // 2, width), lambda j, s: (0, 0))] * 2, [],
         me, *parts, w, w, w, done, micros=5,
     )
 
@@ -626,10 +635,9 @@
     def gather_block(arr):
         return send_block([lax.dynamic_index_in_dim(arr, r ^ odd, 0, False) for r in range(2)])
 
-    def return_block(arr):
+    def return_block(parts):
         back = []
-        for r in range(2):
-            part = arr[r * part_len : (r + 1) * part_len]
+        for r, part in enumerate(parts):
             back.append(lax.ppermute(part, ("dp", "seq"), [(b, a) for a, b in ways[r]]))
         return back
 
@@ -662,9 +670,9 @@
     w_hbm = pltpu.with_memory_space_constraint(w_qkv, pltpu.HBM)
     q, k, v = qkv(info, x, x_far, w_hbm, far_flag, biases)
     ctx, probs = attn_fwd(info, q, k, v)
-    probs = pltpu.with_memory_space_constraint(probs, pltpu.HBM)
+
     ctx_far = other(ctx)
-    y, normed, rstd, act_m, act_t, slope_m, slope_t, out, d_two, d_ffn, vec_two = mid(
+    y, normed, rstd, act_m, act_t, slope_m, slope_t, out0, out1, d_two, d_ffn, vec_two = mid(
         me, x, ctx, w_out, bias_out[None], gain_attn[None], shift_attn[None], w_up, bias_up[None],
         w_down, bias_down[None], gain_ffn[None], shift_ffn[None], *grad,
     )
@@ -707,10 +715,11 @@
     y_far = other(y)
     pre_m, pre_t, vec_up = back_one(me, d_ffn, w_down, slope_m, slope_t)
     pre_far = other(pre_t)
-    output = return_block(tie(out, pre_m))
+    output = return_block((out0, out1))
     down = grad_down(me, d_ffn, d_ffn_far, act_m, act_far)
-    pre_m, down = tie((pre_m, down))
+    up = grad_up(me, y, y_far, pre_m, pre_far)
     down = halve_first(down)
+    up = halve_first(up)
     d_one, d_attn, d_ctx, vec_one = back_two(
         me, pre_m, pre_t, w_up, d_two, normed, rstd, gain_attn[None], w_out
     )
@@ -718,12 +727,10 @@
     def mine(pair):
         return jnp.where(second, pair[1], pair[0])
 
-    attn_far = other(jnp.where(second, d_attn[:, :half], d_attn[:, half:]))
-    y, d_ctx = tie((y, d_ctx))
-    up = grad_up(me, y, y_far, pre_m, pre_far)
-    d_ctx, up, down = tie((d_ctx, up, down))
-    up = halve_first(up)
+    d_mine = (d_attn[:, :half], d_attn[:, half:])
+    attn_far = other(mine(d_mine[::-1]))
     down = halve_second(down)
+    up = halve_second(up)
     heads_far = [far[:, :half], far[:, half:]]
     pairs = heads // 4
     qs, ks, vs, k_gots, v_gots, vecs = [], [], [], [], [], []
@@ -736,6 +743,7 @@
         k_gots.append(other(d_k))
         v_gots.append(other(d_v))
     q_far = other(jnp.where(second, qs[0], qs[1]))
+    down = halve_seq_first(down)
     k_own = [jnp.where(f, g, u) for f, g, u in zip(heads_far, k_gots, ks)]
     k_oth = [jnp.where(f, u, g) for f, g, u in zip(heads_far, k_gots, ks)]
     v_own = [jnp.where(f, g, u) for f, g, u in zip(heads_far, v_gots, vs)]
@@ -743,12 +751,9 @@
 
     rest = grad_rest(
         me, x, x_far, ctx, ctx_far, mine(qs), q_far, mine(k_own), mine(k_oth), mine(v_own),
-        mine(v_oth), mine((d_attn[:, :half], d_attn[:, half:])), attn_far,
-    )
-    rest, qs, vecs, down, up = tie((rest, qs, vecs, down, up))
+        mine(v_oth), mine(d_mine), attn_far,
+    )
     rest = halve_first(rest)
-    up = halve_second(up)
-    down = halve_seq_first(down)
     d_tok = tok(me, qs + k_own + v_own, w_qkv, d_one)
     d_tok = return_block(d_tok)
     vec = jnp.concatenate(

time: 247 us -> 264 us (1.069)
  waiting for transfers between devices: 63.6 us -> 83.4 us
  local copies, waits for them, and re-layouts: 6.47 us -> 9.9 us
  starting transfers between devices: 85.1 us -> 81.9 us
    ppermute x9, waiting for transfers between devices: 19 us -> 35.3 us  [over_seq(): return lax.ppermute(arr, 'seq', [(i, i ^ bit) for i in range(seq)])]
    ppermute x49, waiting for transfers between devices: 34.1 us -> 43.4 us  [over_dp(): return lax.ppermute(arr, 'dp', [(i, i ^ bit) for i in range(dp)])]
    unnamed x41 -> x69, local copies, waits for them, and re-layouts: 0.13 us -> 6.71 us
    ppermute x4, waiting for transfers between devices: 5.78 us -> 0.01 us  [return_block(): back.append(lax.ppermute(part, ('dp', 'seq'), [(b, a) for a, b in ways[r]]))]
    ppermute x49, starting transfers between devices: 59.4 us -> 53.6 us  [over_dp(): return lax.ppermute(arr, 'dp', [(i, i ^ bit) for i in range(dp)])]
    ppermute x9, starting transfers between devices: 10.8 us -> 15.5 us  [over_seq(): return lax.ppermute(arr, 'seq', [(i, i ^ bit) for i in range(seq)])]
  transfers between devices with their start and end apart: 67 -> 67, of which waited for: 22 -> 24; matrix products, arithmetic and copies ran while one was open for 6% -> 4% of each run, Pallas kernels for 24% -> 15%
where the time goes in v2:
time: 264 us
  waiting for transfers between devices  83.4 us (32%)
  starting transfers between devices  81.9 us (31%)
  Pallas kernels  76 us (29%)
  local copies, waits for them, and re-layouts  9.9 us (4%)
  other arithmetic  8.61 us (3%)
  between operations  4.01 us (2%)
    pallas_call x15, Pallas kernels, call(): pl.pallas_call(kernel, grid_spec=pltpu.PrefetchScalarGridSpec(num_scalar_...  76 us
    ppermute x49, starting transfers between devices, over_dp(): return lax.ppermute(arr, 'dp', [(i, i ^ bit) for i in range(dp)])  53.6 us
    ppermute x49, waiting for transfers between devices, over_dp(): return lax.ppermute(arr, 'dp', [(i, i ^ bit) for i in range(dp)])  43.4 us
    ppermute x9, waiting for transfers between devices, over_seq(): return lax.ppermute(arr, 'seq', [(i, i ^ bit) for i in range(seq)])  35.3 us
    ppermute x9, starting transfers between devices, over_seq(): return lax.ppermute(arr, 'seq', [(i, i ^ bit) for i in range(seq)])  15.5 us
    ppermute x4, starting transfers between devices, send_block(): out.append(lax.ppermute(part, ('dp', 'seq'), ways[r]))  9.33 us
    unnamed x69, local copies, waits for them, and re-layouts  6.71 us
  transfers between devices with their start and end apart: 67, of which 24 were waited for; matrix products, arithmetic and copies ran while one was open for 4% of the time, Pallas kernels for 15%

profile of v2, /device:TPU:0, one launch (start us, length us, event | category | flops | bytes accessed | tf_op | source)
XLA Modules:
  0.0 263.8 jit_solution(447591369784863312)
XLA Ops:
  2.0 1.8 collective-permute-start.2
  5.7 3.1 %collective-permute-start.1 = (bf16[256,768]{1,0:T(8,128)(2,1)S(1)}, bf16[256,768]{1,0:T(8,128)(2,1)S(1)}, u32[]{:S(2)}, u32[]{:S(2)}) collective-permute-start(bf16[256,768]{1,0:T(8,128)(2,1)S(1)} %get-tuple-element.169), channel_id=1, source_target_pairs={{0,1},{1,0},{2,5},{3,4},{4,3},{5,2},{6,7},{7,6},{8,9},{9,8},{10,13... | collective-permute-start | bytes 1179656 | tf_op jit(solution)/shard_map/ppermute | solution.py:632
  11.9 4.7 %collective-permute-done.1 = bf16[256,768]{1,0:T(8,128)(2,1)S(1)} collective-permute-done((bf16[256,768]{1,0:T(8,128)(2,1)S(1)}, bf16[256,768]{1,0:T(8,128)(2,1)S(1)}, u32[]{:S(2)}, u32[]{:S(2)}) %collective-permute-start.1) | collective-permute-done | bytes 393248 | tf_op jit(solution)/shard_map/ppermute | solution.py:632
  16.7 11.1 %collective-permute-start.3 = (bf16[512,768]{1,0:T(8,128)(2,1)S(1)}, bf16[512,768]{1,0:T(8,128)(2,1)S(1)}, u32[]{:S(2)}, u32[]{:S(2)}) collective-permute-start(bf16[512,768]{1,0:T(8,128)(2,1)S(1)} %constant_dynamic-update-slice_fusion.x_ref.xo_ref), channel_id=1, source_target_pairs={{0,4},{4,0},{8,12},{12,8},{16,20},{20,16},{24,28},{28,24},{1,5},{5... | collective-permute-start | bytes 2359304 | tf_op jit(solution)/shard_map/ppermute | solution.py:612
  28.6 4.8 %collective-permute-start.5 = (bf16[256,768]{1,0:T(8,128)(2,1)S(1)}, bf16[256,768]{1,0:T(8,128)(2,1)S(1)}, u32[]{:S(2)}, u32[]{:S(2)}) collective-permute-start(bf16[256,768]{1,0:T(8,128)(2,1)S(1)} %get-tuple-element.98), channel_id=1, source_target_pairs={{0,1},{1,0},{2,5},{3,4},{4,3},{5,2},{6,7},{7,6},{8,9},{9,8},{10,13... | collective-permute-start | bytes 1179656 | tf_op jit(solution)/shard_map/ppermute | solution.py:632
  33.5 6.4 %shard_map.280 = (bf16[512,768]{1,0:T(8,128)(2,1)S(1)}, bf16[512,768]{1,0:T(8,128)(2,1)S(1)}, bf16[512,768]{1,0:T(8,128)(2,1)S(1)}) custom-call(s32[16]{0:T(128)S(1)} %concatenate.12.info, bf16[512,768]{1,0:T(8,128)(2,1)S(1)} %constant_dynamic-update-slice_fusion.x_ref.xo_ref, bf16[512,768]{1,0:T(8,128)(2,1)S(1)} %collective-permute-done.3.xf_ref.xp_ref, ...), custom_call_target="tpu_custom_call" | custom-call | flops 5000000000 | bytes 8000000 | tf_op jit(solution)/shard_map/pallas_call | solution.py:34
  39.9 9.0 %shard_map.281 = (bf16[512,768]{1,0:T(8,128)(2,1)S(1)}, bf16[12,512,512]{2,1,0:T(8,128)(2,1)}) custom-call(s32[16]{0:T(128)S(1)} %concatenate.12.info, bf16[512,768]{1,0:T(8,128)(2,1)S(1)} %get-tuple-element.91.q_ref, bf16[512,768]{1,0:T(8,128)(2,1)S(1)} %get-tuple-element.92.k_ref, bf16[512,768]{1,0:T(8,128)(2,1)S(1)} %get-tuple-element.93.v_ref), custom_call_target="tpu_custom_call" | custom-call | flops 8000000000 | bytes 8000000 | tf_op jit(solution)/shard_map/pallas_call | solution.py:34
  49.1 14.8 %shard_map.282 = (bf16[512,768]{1,0:T(8,128)(2,1)S(1)}, f32[512,768]{1,0:T(8,128)S(1)}, f32[512,1]{1,0:T(8,128)S(1)}, bf16[512,1536]{1,0:T(8,128)(2,1)S(1)}, bf1...) custom-call(s32[4]{0:T(128)S(1)} %pad_add_fusion.me, ...), custom_call_target="tpu_custom_call" | custom-call | flops 17999998976 | bytes 8000000 | tf_op jit(solution)/shard_map/pallas_call | solution.py:34
  63.9 4.0 %shard_map.283 = (bf16[512,1536]{1,0:T(8,128)(2,1)S(1)}, bf16[512,1536]{1,0:T(8,128)(2,1)S(1)}, f32[4,768]{1,0:T(4,128)S(1)}) custom-call(s32[4]{0:T(128)S(1)} %pad_add_fusion.me, bf16[512,768]{1,0:T(8,128)(2,1)S(1)} %get-tuple-element.101.dffn_ref.lo_ref, bf16[3072,768]{1,0:T(8,128)(2,1)S(1)} %bitcast.143, bf16[3072,768]{1,0:T(8,128)(2,1)S(1)} %bitcast.143, ...), custom_call_target="tpu_custom_call" | custom-call | flops 6000000000 | bytes 8000000 | tf_op jit(solution)/shard_map/pallas_call | solution.py:34
  68.0 6.6 %shard_map.284 = (f32[512,768]{1,0:T(8,128)S(1)}, bf16[512,768]{1,0:T(8,128)(2,1)S(1)}, bf16[512,768]{1,0:T(8,128)(2,1)S(1)}, f32[3,768]{1,0:T(4,128)S(1)}) custom-call(s32[4]{0:T(128)S(1)} %pad_add_fusion.me, bf16[512,1536]{1,0:T(8,128)(2,1)S(1)} %get-tuple-element.104.pm_ref.ro_ref, bf16[512,1536]{1,0:T(8,128)(2,1)S(1)} %get-tuple-element.105.pt_ref, ...), custom_call_target="tpu_custom_call" | custom-call | flops 8000000000 | bytes 8000000 | tf_op jit(solution)/shard_map/pallas_call | solution.py:34
  75.8 4.9 %shard_map.286 = (bf16[512,384]{1,0:T(8,128)(2,1)S(1)}, bf16[512,384]{1,0:T(8,128)(2,1)S(1)}, bf16[512,384]{1,0:T(8,128)(2,1)S(1)}, f32[2,384]{1,0:T(2,128)S(1)}) custom-call(s32[16]{0:T(128)S(1)} %concatenate.12.info, bf16[512,768]{1,0:T(8,128)(2,1)S(1)} %get-tuple-element.91.q_ref, bf16[512,768]{1,0:T(8,128)(2,1)S(1)} %get-tuple-element.92.k_ref, ...), custom_call_target="tpu_custom_call" | custom-call | flops 6000000000 | bytes 8000000 | tf_op jit(solution)/shard_map/pallas_call | solution.py:34
  80.8 4.9 %shard_map.285 = (bf16[512,384]{1,0:T(8,128)(2,1)S(1)}, bf16[512,384]{1,0:T(8,128)(2,1)S(1)}, bf16[512,384]{1,0:T(8,128)(2,1)S(1)}, f32[2,384]{1,0:T(2,128)S(1)}) custom-call(s32[16]{0:T(128)S(1)} %concatenate.12.info, bf16[512,768]{1,0:T(8,128)(2,1)S(1)} %get-tuple-element.91.q_ref, bf16[512,768]{1,0:T(8,128)(2,1)S(1)} %get-tuple-element.92.k_ref, ...), custom_call_target="tpu_custom_call" | custom-call | flops 6000000000 | bytes 8000000 | tf_op jit(solution)/shard_map/pallas_call | solution.py:34
  85.8 3.4 %collective-permute-start.30 = (f32[12,768]{1,0:T(8,128)S(1)}, f32[12,768]{1,0:T(8,128)S(1)}, u32[]{:S(2)}, u32[]{:S(2)}) collective-permute-start(f32[12,768]{1,0:T(8,128)S(1)} %pad_maximum_fusion.3), channel_id=1, source_target_pairs={{0,4},{4,0},{8,12},{12,8},{16,20},{20,16},{24,28},{28,24},{1,5},{5... | collective-permute-start | bytes 110600 | tf_op jit(solution)/shard_map/ppermute | solution.py:612
  94.2 1.8 collective-permute-done.32
  96.0 2.1 collective-permute-done.33
  99.9 1.8 collective-permute-start.35
  104.6 4.1 %shard_map.288 = (bf16[2,2,2,96,384]{4,3,2,1,0:T(8,128)(2,1)S(1)}, bf16[2,2,2,96,384]{4,3,2,1,0:T(8,128)(2,1)}, bf16[2,2,2,96,384]{4,3,2,1,0:T(8,128)(2,1)S(1)}, bf16[2,2,2,96,384]{4,3,2,1,0:T(8,128)(2,1)S(1)}) custom-call(s32[4]{0:T(128)S(1)} %pad_add_fusion.me, bf16[512,768]{1,0:T(8,128)(2,1)S(1)} %constant_dynamic-update-slice_fusion.x_ref.xo_ref, ...), custom_call_target="tpu_custom_call" | custom-call | flops 6000000000 | bytes 8000000 | tf_op jit(solution)/shard_map/pallas_call | solution.py:34
  114.4 2.0 copy-done.2
  117.8 2.6 shard_map.287
  120.4 3.6 %collective-permute-done.17 = bf16[2,2,2,96,384]{4,3,2,1,0:T(8,128)(2,1)} collective-permute-done((bf16[2,2,2,96,384]{4,3,2,1,0:T(8,128)(2,1)}, bf16[2,2,2,96,384]{4,3,2,1,0:T(8,128)(2,1)}, u32[]{:S(2)}, u32[]{:S(2)}) %collective-permute-start.17) | collective-permute-done | bytes 589856 | tf_op jit(solution)/shard_map/ppermute | solution.py:612
  127.9 1.9 collective-permute-start.38
  130.3 2.1 maximum_select_fusion
  132.5 3.4 %collective-permute-done.18 = bf16[2,2,96,384]{3,2,1,0:T(8,128)(2,1)S(1)} collective-permute-done((bf16[2,2,96,384]{3,2,1,0:T(8,128)(2,1)S(1)}, bf16[2,2,96,384]{3,2,1,0:T(8,128)(2,1)S(1)}, u32[]{:S(2)}, u32[]{:S(2)}) %collective-permute-start.18) | collective-permute-done | bytes 294944 | tf_op jit(solution)/shard_map/ppermute | solution.py:612
  135.9 3.9 %collective-permute-start.37 = (bf16[512,768]{1,0:T(8,128)(2,1)S(1)}, bf16[512,768]{1,0:T(8,128)(2,1)S(1)}, u32[]{:S(2)}, u32[]{:S(2)}) collective-permute-start(bf16[512,768]{1,0:T(8,128)(2,1)S(1)} %copy-done.9), channel_id=1, source_target_pairs={{0,4},{4,0},{8,12},{12,8},{16,20},{20,16},{24,28},{28,24},{1,5},{5... | collective-permute-start | bytes 2359304 | tf_op jit(solution)/shard_map/ppermute | solution.py:612
  140.8 2.1 collective-permute-start.21
  142.9 5.8 %shard_map.293 = (bf16[2,2,2,96,384]{4,3,2,1,0:T(8,128)(2,1)S(1)}, bf16[2,2,2,96,384]{4,3,2,1,0:T(8,128)(2,1)S(1)}, bf16[2,2,2,96,384]{4,3,2,1,0:T(8,128)(2,1)S(1)}, bf16[2,2,2,96,384]{4,3,2,1,0:T(8,128)(2,1)S(1)}) custom-call(s32[4]{0:T(128)S(1)} %pad_add_fusion.me, bf16[512,768]{1,0:T(8,128)(2,1)S(1)} %get-tuple-element.101.dffn_ref.lo_ref, ...), custom_call_target="tpu_custom_call" | custom-call | flops 6000000000 | bytes 8000000 | tf_op jit(solution)/shard_map/pallas_call | solution.py:34
  148.7 8.4 %collective-permute-done.21 = bf16[2,2,96,384]{3,2,0,1:T(8,128)(2,1)S(1)} collective-permute-done((bf16[2,2,96,384]{3,2,0,1:T(8,128)(2,1)S(1)}, bf16[2,2,96,384]{3,2,0,1:T(8,128)(2,1)S(1)}, u32[]{:S(2)}, u32[]{:S(2)}) %collective-permute-start.21) | collective-permute-done | bytes 294944 | tf_op jit(solution)/shard_map/ppermute | solution.py:615
  157.1 2.5 collective-permute-start.54
  161.2 4.8 %collective-permute-start.22 = (bf16[2,96,384]{2,1,0:T(8,128)(2,1)S(1)}, bf16[2,96,384]{2,1,0:T(8,128)(2,1)S(1)}, u32[]{:S(2)}, u32[]{:S(2)}) collective-permute-start(bf16[2,96,384]{2,1,0:T(8,128)(2,1)S(1)} %slice_bitcast_fusion.16), channel_id=1, source_target_pairs={{0,2},{1,3},{2,0},{3,1},{4,6},{5,7},{6,4},{7,5},{8,10},{9,11},{10,... | collective-permute-start | bytes 442376 | tf_op jit(solution)/shard_map/ppermute | solution.py:615
  166.0 4.4 %shard_map.291 = (bf16[2,2,2,96,384]{4,3,2,1,0:T(8,128)(2,1)S(1)}, bf16[2,2,2,96,384]{4,3,2,1,0:T(8,128)(2,1)S(1)}, bf16[2,2,2,96,384]{4,3,2,1,0:T(8,128)(2,1)S(1)}, bf16[2,2,2,96,384]{4,3,2,1,0:T(8,128)(2,1)S(1)}) custom-call(s32[4]{0:T(128)S(1)} %pad_add_fusion.me, bf16[512,768]{1,0:T(8,128)(2,1)S(1)} %copy-done.9, ...), custom_call_target="tpu_custom_call" | custom-call | flops 6000000000 | bytes 8000000 | tf_op jit(solution)/shard_map/pallas_call | solution.py:34
  170.4 3.2 %collective-permute-done.22 = bf16[2,96,384]{2,1,0:T(8,128)(2,1)S(1)} collective-permute-done((bf16[2,96,384]{2,1,0:T(8,128)(2,1)S(1)}, bf16[2,96,384]{2,1,0:T(8,128)(2,1)S(1)}, u32[]{:S(2)}, u32[]{:S(2)}) %collective-permute-start.22) | collective-permute-done | bytes 147488 | tf_op jit(solution)/shard_map/ppermute | solution.py:615
  175.0 1.7 collective-permute-start.23
  177.0 11.9 %collective-permute-done.39 = bf16[2,2,2,96,384]{4,3,2,1,0:T(8,128)(2,1)S(1)} collective-permute-done((bf16[2,2,2,96,384]{4,3,2,1,0:T(8,128)(2,1)S(1)}, bf16[2,2,2,96,384]{4,3,2,1,0:T(8,128)(2,1)S(1)}, u32[]{:S(2)}, u32[]{:S(2)}) %collective-permute-start.39) | collective-permute-done | bytes 589856 | tf_op jit(solution)/shard_map/ppermute | solution.py:612
  192.1 6.9 %collective-permute-done.55 = bf16[2,2,96,384]{3,2,1,0:T(8,128)(2,1)S(1)} collective-permute-done((bf16[2,2,96,384]{3,2,1,0:T(8,128)(2,1)S(1)}, bf16[2,2,96,384]{3,2,1,0:T(8,128)(2,1)S(1)}, u32[]{:S(2)}, u32[]{:S(2)}) %collective-permute-start.55) | collective-permute-done | bytes 294944 | tf_op jit(solution)/shard_map/ppermute | solution.py:612
  199.8 2.0 collective-permute-start.42
  202.0 4.9 %collective-permute-done.40 = bf16[2,2,96,384]{3,2,1,0:T(8,128)(2,1)S(1)} collective-permute-done((bf16[2,2,96,384]{3,2,1,0:T(8,128)(2,1)S(1)}, bf16[2,2,96,384]{3,2,1,0:T(8,128)(2,1)S(1)}, u32[]{:S(2)}, u32[]{:S(2)}) %collective-permute-start.40) | collective-permute-done | bytes 294944 | tf_op jit(solution)/shard_map/ppermute | solution.py:612
  209.1 7.0 %collective-permute-done.58 = bf16[2,2,96,384]{3,2,0,1:T(8,128)(2,1)S(1)} collective-permute-done((bf16[2,2,96,384]{3,2,0,1:T(8,128)(2,1)S(1)}, bf16[2,2,96,384]{3,2,0,1:T(8,128)(2,1)S(1)}, u32[]{:S(2)}, u32[]{:S(2)}) %collective-permute-start.58) | collective-permute-done | bytes 294944 | tf_op jit(solution)/shard_map/ppermute | solution.py:615
  216.3 6.7 %collective-permute-done.43 = bf16[2,2,96,384]{3,2,0,1:T(8,128)(2,1)S(1)} collective-permute-done((bf16[2,2,96,384]{3,2,0,1:T(8,128)(2,1)S(1)}, bf16[2,2,96,384]{3,2,0,1:T(8,128)(2,1)S(1)}, u32[]{:S(2)}, u32[]{:S(2)}) %collective-permute-start.43) | collective-permute-done | bytes 294944 | tf_op jit(solution)/shard_map/ppermute | solution.py:615
  223.0 4.5 %collective-permute-start.59 = (bf16[2,96,384]{2,1,0:T(8,128)(2,1)S(1)}, bf16[2,96,384]{2,1,0:T(8,128)(2,1)S(1)}, u32[]{:S(2)}, u32[]{:S(2)}) collective-permute-start(bf16[2,96,384]{2,1,0:T(8,128)(2,1)S(1)} %slice_bitcast_fusion.12), channel_id=1, source_target_pairs={{0,2},{1,3},{2,0},{3,1},{4,6},{5,7},{6,4},{7,5},{8,10},{9,11},{10,... | collective-permute-start | bytes 442376 | tf_op jit(solution)/shard_map/ppermute | solution.py:615
  227.5 2.5 collective-permute-start.25
  230.0 4.1 %collective-permute-done.59 = bf16[2,96,384]{2,1,0:T(8,128)(2,1)S(1)} collective-permute-done((bf16[2,96,384]{2,1,0:T(8,128)(2,1)S(1)}, bf16[2,96,384]{2,1,0:T(8,128)(2,1)S(1)}, u32[]{:S(2)}, u32[]{:S(2)}) %collective-permute-start.59) | collective-permute-done | bytes 147488 | tf_op jit(solution)/shard_map/ppermute | solution.py:615
  234.9 5.9 %collective-permute-done.44 = bf16[2,96,384]{2,1,0:T(8,128)(2,1)S(1)} collective-permute-done((bf16[2,96,384]{2,1,0:T(8,128)(2,1)S(1)}, bf16[2,96,384]{2,1,0:T(8,128)(2,1)S(1)}, u32[]{:S(2)}, u32[]{:S(2)}) %collective-permute-start.44) | collective-permute-done | bytes 147488 | tf_op jit(solution)/shard_map/ppermute | solution.py:615
  240.8 2.1 collective-permute-start.60
  244.5 2.0 collective-permute-start.45
  250.6 1.7 collective-permute-done.62.refs_3_
  254.1 2.2 shard_map.289
  258.8 2.8 %shard_map.294 = f32[768,768]{1,0:T(8,128)} custom-call(s32[4]{0:T(128)S(1)} %pad_add_fusion.me, bf16[192,384]{1,0:T(8,128)(2,1)S(1)} %bitcast.153, bf16[192,384]{1,0:T(8,128)(2,1)S(1)} %collective-permute-done.60.refs_1_, bf16[192,384]{1,0:T(8,128)(2,1)S(1)} %collective-permute-done.61.refs_2_, bf16[192,384]{1,0:T(8,128)(2,1)S(1)} %collective-permute-done.62.refs_3_, ...), custom_call_target="tpu_custom_call" | custom-call | flops 3000000000 | bytes 8000000 | tf_op jit(solution)/shard_map/pallas_call | solution.py:34
  261.6 2.2 shard_map.292
  (233 shorter events, 48.4 us)
Async XLA Ops:
  2.0 7.4 %collective-permute-start.2 = (s32[1]{0:T(128)}, s32[1]{0:T(128)}, u32[]{:S(2)}, u32[]{:S(2)}) collective-permute-start(s32[1]{0:T(128)} %dynamic_slice.18), channel_id=1, source_target_pairs={{0,0},{1,1},{2,4},{3,5},{4,2},{5,3},{6,6},{7,7},{8,8},{9,9},{10,12... | collective-permute-start | bytes 20 | tf_op jit(solution)/shard_map/ppermute | solution.py:648
  5.0 6.9 %collective-permute-start = (bf16[256,768]{1,0:T(8,128)(2,1)S(1)}, bf16[256,768]{1,0:T(8,128)(2,1)S(1)}, u32[]{:S(2)}, u32[]{:S(2)}) collective-permute-start(bf16[256,768]{1,0:T(8,128)(2,1)S(1)} %get-tuple-element.170), channel_id=1, source_target_pairs={{0,0},{1,1},{2,4},{3,5},{4,2},{5,3},{6,6},{7,7},{8,8},{9,9},{10,12... | collective-permute-start | bytes 1179656 | tf_op jit(solution)/shard_map/ppermute | solution.py:632
  5.7 10.9 %collective-permute-start.1 = (bf16[256,768]{1,0:T(8,128)(2,1)S(1)}, bf16[256,768]{1,0:T(8,128)(2,1)S(1)}, u32[]{:S(2)}, u32[]{:S(2)}) collective-permute-start(bf16[256,768]{1,0:T(8,128)(2,1)S(1)} %get-tuple-element.169), channel_id=1, source_target_pairs={{0,1},{1,0},{2,5},{3,4},{4,3},{5,2},{6,7},{7,6},{8,9},{9,8},{10,13... | collective-permute-start | bytes 1179656 | tf_op jit(solution)/shard_map/ppermute | solution.py:632
  16.7 16.8 %collective-permute-start.3 = (bf16[512,768]{1,0:T(8,128)(2,1)S(1)}, bf16[512,768]{1,0:T(8,128)(2,1)S(1)}, u32[]{:S(2)}, u32[]{:S(2)}) collective-permute-start(bf16[512,768]{1,0:T(8,128)(2,1)S(1)} %constant_dynamic-update-slice_fusion.x_ref.xo_ref), channel_id=1, source_target_pairs={{0,4},{4,0},{8,12},{12,8},{16,20},{20,16},{24,28},{28,24},{1,5},{5... | collective-permute-start | bytes 2359304 | tf_op jit(solution)/shard_map/ppermute | solution.py:612
  27.9 21.0 %collective-permute-start.4 = (bf16[256,768]{1,0:T(8,128)(2,1)S(1)}, bf16[256,768]{1,0:T(8,128)(2,1)S(1)}, u32[]{:S(2)}, u32[]{:S(2)}) collective-permute-start(bf16[256,768]{1,0:T(8,128)(2,1)S(1)} %get-tuple-element.97), channel_id=1, source_target_pairs={{0,0},{1,1},{2,4},{3,5},{4,2},{5,3},{6,6},{7,7},{8,8},{9,9},{10,12... | collective-permute-start | bytes 1179656 | tf_op jit(solution)/shard_map/ppermute | solution.py:632
  28.6 20.4 %collective-permute-start.5 = (bf16[256,768]{1,0:T(8,128)(2,1)S(1)}, bf16[256,768]{1,0:T(8,128)(2,1)S(1)}, u32[]{:S(2)}, u32[]{:S(2)}) collective-permute-start(bf16[256,768]{1,0:T(8,128)(2,1)S(1)} %get-tuple-element.98), channel_id=1, source_target_pairs={{0,1},{1,0},{2,5},{3,4},{4,3},{5,2},{6,7},{7,6},{8,9},{9,8},{10,13... | collective-permute-start | bytes 1179656 | tf_op jit(solution)/shard_map/ppermute | solution.py:632
  89.2 9.0 %collective-permute-start.11 = (bf16[512,384]{1,0:T(8,128)(2,1)S(1)}, bf16[512,384]{1,0:T(8,128)(2,1)S(1)}, u32[]{:S(2)}, u32[]{:S(2)}) collective-permute-start(bf16[512,384]{1,0:T(8,128)(2,1)S(1)} %get-tuple-element.116), channel_id=1, source_target_pairs={{0,4},{4,0},{8,12},{12,8},{16,20},{20,16},{24,28},{28,24},{1,5},{5... | collective-permute-start | bytes 1179656 | tf_op jit(solution)/shard_map/ppermute | solution.py:612
  89.3 9.5 %collective-permute-start.9 = (bf16[512,384]{1,0:T(8,128)(2,1)S(1)}, bf16[512,384]{1,0:T(8,128)(2,1)S(1)}, u32[]{:S(2)}, u32[]{:S(2)}) collective-permute-start(bf16[512,384]{1,0:T(8,128)(2,1)S(1)} %get-tuple-element.114), channel_id=1, source_target_pairs={{0,4},{4,0},{8,12},{12,8},{16,20},{20,16},{24,28},{28,24},{1,5},{5... | collective-permute-start | bytes 1179656 | tf_op jit(solution)/shard_map/ppermute | solution.py:612
  94.2 10.4 %collective-permute-start.14 = (bf16[512,768]{1,0:T(8,128)(2,1)S(1)}, bf16[512,768]{1,0:T(8,128)(2,1)S(1)}, u32[]{:S(2)}, u32[]{:S(2)}) collective-permute-start(bf16[512,768]{1,0:T(8,128)(2,1)S(1)} %get-tuple-element.94.ctx_ref.c_ref.co_ref), channel_id=1, source_target_pairs={{0,4},{4,0},{8,12},{12,8},{16,20},{20,16},{24,28},{28,24},{1,5},{5... | collective-permute-start | bytes 2359304 | tf_op jit(solution)/shard_map/ppermute | solution.py:612
  98.9 10.5 %collective-permute-start.34 = (f32[12,768]{1,0:T(8,128)S(1)}, f32[12,768]{1,0:T(8,128)S(1)}, u32[]{:S(2)}, u32[]{:S(2)}) collective-permute-start(f32[12,768]{1,0:T(8,128)S(1)} %add_add_fusion.a_ref), channel_id=1, source_target_pairs={{0,1},{1,0},{2,3},{3,2},{4,5},{5,4},{6,7},{7,6},{8,9},{9,8},{10,11... | collective-permute-start | bytes 110600 | tf_op jit(solution)/shard_map/ppermute | solution.py:615
  99.9 10.0 %collective-permute-start.35 = (f32[12,768]{1,0:T(8,128)S(1)}, f32[12,768]{1,0:T(8,128)S(1)}, u32[]{:S(2)}, u32[]{:S(2)}) collective-permute-start(f32[12,768]{1,0:T(8,128)S(1)} %add_add_fusion.a_ref), channel_id=1, source_target_pairs={{0,2},{1,3},{2,0},{3,1},{4,6},{5,7},{6,4},{7,5},{8,10},{9,11},{10,... | collective-permute-start | bytes 110600 | tf_op jit(solution)/shard_map/ppermute | solution.py:615
  102.9 6.9 %collective-permute-start.36 = (f32[12,768]{1,0:T(8,128)S(1)}, f32[12,768]{1,0:T(8,128)S(1)}, u32[]{:S(2)}, u32[]{:S(2)}) collective-permute-start(f32[12,768]{1,0:T(8,128)S(1)} %add_add_fusion.a_ref), channel_id=1, source_target_pairs={{0,3},{1,2},{2,1},{3,0},{4,7},{5,6},{6,5},{7,4},{8,11},{9,10},{10,... | collective-permute-start | bytes 110600 | tf_op jit(solution)/shard_map/ppermute | solution.py:615
  108.8 15.2 %collective-permute-start.17 = (bf16[2,2,2,96,384]{4,3,2,1,0:T(8,128)(2,1)}, bf16[2,2,2,96,384]{4,3,2,1,0:T(8,128)(2,1)}, u32[]{:S(2)}, u32[]{:S(2)}) collective-permute-start(bf16[2,2,2,96,384]{4,3,2,1,0:T(8,128)(2,1)} %get-tuple-element.123), channel_id=1, source_target_pairs={{0,8},{4,12},{8,0},{12,4},{16,24},{20,28},{24,16},{28,20},{1,9},{5... | collective-permute-start | bytes 1769480 | tf_op jit(solution)/shard_map/ppermute | solution.py:612
  109.4 30.8 %collective-permute-start.52 = (bf16[512,768]{1,0:T(8,128)(2,1)S(1)}, bf16[512,768]{1,0:T(8,128)(2,1)}, u32[]{:S(2)}, u32[]{:S(2)}) collective-permute-start(bf16[512,768]{1,0:T(8,128)(2,1)S(1)} %get-tuple-element.101.dffn_ref.lo_ref), channel_id=1, source_target_pairs={{0,4},{4,0},{8,12},{12,8},{16,20},{20,16},{24,28},{28,24},{1,5},{5... | collective-permute-start | bytes 2359304 | tf_op jit(solution)/shard_map/ppermute | solution.py:612
  109.4 31.5 %collective-permute-start.53 = (bf16[512,1536]{1,0:T(8,128)(2,1)}, bf16[512,1536]{1,0:T(8,128)(2,1)}, u32[]{:S(2)}, u32[]{:S(2)}) collective-permute-start(bf16[512,1536]{1,0:T(8,128)(2,1)} %get-tuple-element.145), channel_id=1, source_target_pairs={{0,4},{4,0},{8,12},{12,8},{16,20},{20,16},{24,28},{28,24},{1,5},{5... | collective-permute-start | bytes 4718600 | tf_op jit(solution)/shard_map/ppermute | solution.py:612
  109.9 18.0 %collective-permute-start.6 = (bf16[256,768]{1,0:T(8,128)(2,1)}, bf16[256,768]{1,0:T(8,128)(2,1)}, u32[]{:S(2)}, u32[]{:S(2)}) collective-permute-start(bf16[256,768]{1,0:T(8,128)(2,1)} %get-tuple-element.99), channel_id=1, source_target_pairs={{1,0},{0,1},{5,2},{4,3},{3,4},{2,5},{7,6},{6,7},{9,8},{8,9},{13,10... | collective-permute-start | bytes 1179656 | tf_op jit(solution)/shard_map/ppermute | solution.py:641
  111.7 15.1 %collective-permute-start.19 = (bf16[2,2,2,96,384]{4,3,2,1,0:T(8,128)(2,1)}, bf16[2,2,2,96,384]{4,3,2,1,0:T(8,128)(2,1)S(1)}, u32[]{:S(2)}, u32[]{:S(2)}) collective-permute-start(bf16[2,2,2,96,384]{4,3,2,1,0:T(8,128)(2,1)} %copy-done.10), channel_id=1, source_target_pairs={{0,16},{4,20},{8,24},{12,28},{16,0},{20,4},{24,8},{28,12},{1,17},{... | collective-permute-start | bytes 1769480 | tf_op jit(solution)/shard_map/ppermute | solution.py:612
  126.8 9.1 %collective-permute-start.18 = (bf16[2,2,96,384]{3,2,1,0:T(8,128)(2,1)S(1)}, bf16[2,2,96,384]{3,2,1,0:T(8,128)(2,1)S(1)}, u32[]{:S(2)}, u32[]{:S(2)}) collective-permute-start(bf16[2,2,96,384]{3,2,1,0:T(8,128)(2,1)S(1)} %slice_bitcast_fusion.10), channel_id=1, source_target_pairs={{0,16},{4,20},{8,24},{12,28},{16,0},{20,4},{24,8},{28,12},{1,17},{... | collective-permute-start | bytes 884744 | tf_op jit(solution)/shard_map/ppermute | solution.py:612
  127.9 33.3 %collective-permute-start.38 = (bf16[512,1536]{1,0:T(8,128)(2,1)S(1)}, bf16[512,1536]{1,0:T(8,128)(2,1)S(1)}, u32[]{:S(2)}, u32[]{:S(2)}) collective-permute-start(bf16[512,1536]{1,0:T(8,128)(2,1)S(1)} %copy-done.6), channel_id=1, source_target_pairs={{0,4},{4,0},{8,12},{12,8},{16,20},{20,16},{24,28},{28,24},{1,5},{5... | collective-permute-start | bytes 4718600 | tf_op jit(solution)/shard_map/ppermute | solution.py:612
  129.8 10.1 %collective-permute-start.20 = (bf16[2,2,96,384]{3,2,1,0:T(8,128)(2,1)S(1)}, bf16[2,2,96,384]{3,2,1,0:T(8,128)(2,1)S(1)}, u32[]{:S(2)}, u32[]{:S(2)}) collective-permute-start(bf16[2,2,96,384]{3,2,1,0:T(8,128)(2,1)S(1)} %slice_bitcast_fusion.8), channel_id=1, source_target_pairs={{0,8},{4,12},{8,0},{12,4},{16,24},{20,28},{24,16},{28,20},{1,9},{5... | collective-permute-start | bytes 884744 | tf_op jit(solution)/shard_map/ppermute | solution.py:612
  135.9 23.8 %collective-permute-start.37 = (bf16[512,768]{1,0:T(8,128)(2,1)S(1)}, bf16[512,768]{1,0:T(8,128)(2,1)S(1)}, u32[]{:S(2)}, u32[]{:S(2)}) collective-permute-start(bf16[512,768]{1,0:T(8,128)(2,1)S(1)} %copy-done.9), channel_id=1, source_target_pairs={{0,4},{4,0},{8,12},{12,8},{16,20},{20,16},{24,28},{28,24},{1,5},{5... | collective-permute-start | bytes 2359304 | tf_op jit(solution)/shard_map/ppermute | solution.py:612
  139.9 87.6 %collective-permute-start.12 = (bf16[256,768]{1,0:T(8,128)(2,1)S(1)}, bf16[256,768]{1,0:T(8,128)(2,1)S(1)}, u32[]{:S(2)}, u32[]{:S(2)}) collective-permute-start(bf16[256,768]{1,0:T(8,128)(2,1)S(1)} %get-tuple-element.118), channel_id=1, source_target_pairs={{1,0},{0,1},{5,2},{4,3},{3,4},{2,5},{7,6},{6,7},{9,8},{8,9},{13,10... | collective-permute-start | bytes 1179656 | tf_op jit(solution)/shard_map/ppermute | solution.py:641
  140.1 100.6 %collective-permute-start.13 = (bf16[256,768]{1,0:T(8,128)(2,1)S(1)}, bf16[256,768]{1,0:T(8,128)(2,1)S(1)}, u32[]{:S(2)}, u32[]{:S(2)}) collective-permute-start(bf16[256,768]{1,0:T(8,128)(2,1)S(1)} %get-tuple-element.119), channel_id=1, source_target_pairs={{0,0},{1,1},{4,2},{5,3},{2,4},{3,5},{6,6},{7,7},{8,8},{9,9},{12,10... | collective-permute-start | bytes 1179656 | tf_op jit(solution)/shard_map/ppermute | solution.py:641
  140.8 16.3 %collective-permute-start.21 = (bf16[2,2,96,384]{3,2,0,1:T(8,128)(2,1)S(1)}, bf16[2,2,96,384]{3,2,0,1:T(8,128)(2,1)S(1)}, u32[]{:S(2)}, u32[]{:S(2)}) collective-permute-start(bf16[2,2,96,384]{3,2,0,1:T(8,128)(2,1)S(1)} %fusion.24), channel_id=1, source_target_pairs={{0,1},{1,0},{2,3},{3,2},{4,5},{5,4},{6,7},{7,6},{8,9},{9,8},{10,11... | collective-permute-start | bytes 884744 | tf_op jit(solution)/shard_map/ppermute | solution.py:615
  157.1 17.3 %collective-permute-start.54 = (bf16[2,2,2,96,384]{4,3,2,1,0:T(8,128)(2,1)S(1)}, bf16[2,2,2,96,384]{4,3,2,1,0:T(8,128)(2,1)S(1)}, u32[]{:S(2)}, u32[]{:S(2)}) collective-permute-start(bf16[2,2,2,96,384]{4,3,2,1,0:T(8,128)(2,1)S(1)} %get-tuple-element.147), channel_id=1, source_target_pairs={{0,8},{4,12},{8,0},{12,4},{16,24},{20,28},{24,16},{28,20},{1,9},{5... | collective-permute-start | bytes 1769480 | tf_op jit(solution)/shard_map/ppermute | solution.py:612
  159.7 15.3 %collective-permute-start.56 = (bf16[2,2,2,96,384]{4,3,2,1,0:T(8,128)(2,1)S(1)}, bf16[2,2,2,96,384]{4,3,2,1,0:T(8,128)(2,1)S(1)}, u32[]{:S(2)}, u32[]{:S(2)}) collective-permute-start(bf16[2,2,2,96,384]{4,3,2,1,0:T(8,128)(2,1)S(1)} %get-tuple-element.149), channel_id=1, source_target_pairs={{0,16},{4,20},{8,24},{12,28},{16,0},{20,4},{24,8},{28,12},{1,17},{... | collective-permute-start | bytes 1769480 | tf_op jit(solution)/shard_map/ppermute | solution.py:612
  161.2 12.4 %collective-permute-start.22 = (bf16[2,96,384]{2,1,0:T(8,128)(2,1)S(1)}, bf16[2,96,384]{2,1,0:T(8,128)(2,1)S(1)}, u32[]{:S(2)}, u32[]{:S(2)}) collective-permute-start(bf16[2,96,384]{2,1,0:T(8,128)(2,1)S(1)} %slice_bitcast_fusion.16), channel_id=1, source_target_pairs={{0,2},{1,3},{2,0},{3,1},{4,6},{5,7},{6,4},{7,5},{8,10},{9,11},{10,... | collective-permute-start | bytes 442376 | tf_op jit(solution)/shard_map/ppermute | solution.py:615
  173.5 15.3 %collective-permute-start.39 = (bf16[2,2,2,96,384]{4,3,2,1,0:T(8,128)(2,1)S(1)}, bf16[2,2,2,96,384]{4,3,2,1,0:T(8,128)(2,1)S(1)}, u32[]{:S(2)}, u32[]{:S(2)}) collective-permute-start(bf16[2,2,2,96,384]{4,3,2,1,0:T(8,128)(2,1)S(1)} %get-tuple-element.140), channel_id=1, source_target_pairs={{0,8},{4,12},{8,0},{12,4},{16,24},{20,28},{24,16},{28,20},{1,9},{5... | collective-permute-start | bytes 1769480 | tf_op jit(solution)/shard_map/ppermute | solution.py:612
  174.4 16.3 %collective-permute-start.41 = (bf16[2,2,2,96,384]{4,3,2,1,0:T(8,128)(2,1)S(1)}, bf16[2,2,2,96,384]{4,3,2,1,0:T(8,128)(2,1)S(1)}, u32[]{:S(2)}, u32[]{:S(2)}) collective-permute-start(bf16[2,2,2,96,384]{4,3,2,1,0:T(8,128)(2,1)S(1)} %get-tuple-element.142), channel_id=1, source_target_pairs={{0,16},{4,20},{8,24},{12,28},{16,0},{20,4},{24,8},{28,12},{1,17},{... | collective-permute-start | bytes 1769480 | tf_op jit(solution)/shard_map/ppermute | solution.py:612
  175.0 59.1 %collective-permute-start.23 = (bf16[192,384]{1,0:T(8,128)(2,1)S(1)}, bf16[192,384]{1,0:T(8,128)(2,1)S(1)}, u32[]{:S(2)}, u32[]{:S(2)}) collective-permute-start(bf16[192,384]{1,0:T(8,128)(2,1)S(1)} %bitcast.144), channel_id=1, source_target_pairs={{0,16},{4,20},{8,24},{12,28},{16,0},{20,4},{24,8},{28,12},{1,17},{... | collective-permute-start | bytes 442376 | tf_op jit(solution)/shard_map/ppermute | solution.py:612
  188.9 10.1 %collective-permute-start.55 = (bf16[2,2,96,384]{3,2,1,0:T(8,128)(2,1)S(1)}, bf16[2,2,96,384]{3,2,1,0:T(8,128)(2,1)S(1)}, u32[]{:S(2)}, u32[]{:S(2)}) collective-permute-start(bf16[2,2,96,384]{3,2,1,0:T(8,128)(2,1)S(1)} %slice_bitcast_fusion.2), channel_id=1, source_target_pairs={{0,16},{4,20},{8,24},{12,28},{16,0},{20,4},{24,8},{28,12},{1,17},{... | collective-permute-start | bytes 884744 | tf_op jit(solution)/shard_map/ppermute | solution.py:612
  190.7 9.1 %collective-permute-start.57 = (bf16[2,2,96,384]{3,2,1,0:T(8,128)(2,1)S(1)}, bf16[2,2,96,384]{3,2,1,0:T(8,128)(2,1)S(1)}, u32[]{:S(2)}, u32[]{:S(2)}) collective-permute-start(bf16[2,2,96,384]{3,2,1,0:T(8,128)(2,1)S(1)} %slice_bitcast_fusion), channel_id=1, source_target_pairs={{0,8},{4,12},{8,0},{12,4},{16,24},{20,28},{24,16},{28,20},{1,9},{5... | collective-permute-start | bytes 884744 | tf_op jit(solution)/shard_map/ppermute | solution.py:612
  199.0 7.8 %collective-permute-start.40 = (bf16[2,2,96,384]{3,2,1,0:T(8,128)(2,1)S(1)}, bf16[2,2,96,384]{3,2,1,0:T(8,128)(2,1)S(1)}, u32[]{:S(2)}, u32[]{:S(2)}) collective-permute-start(bf16[2,2,96,384]{3,2,1,0:T(8,128)(2,1)S(1)} %slice_bitcast_fusion.6), channel_id=1, source_target_pairs={{0,16},{4,20},{8,24},{12,28},{16,0},{20,4},{24,8},{28,12},{1,17},{... | collective-permute-start | bytes 884744 | tf_op jit(solution)/shard_map/ppermute | solution.py:612
  199.8 9.2 %collective-permute-start.42 = (bf16[2,2,96,384]{3,2,1,0:T(8,128)(2,1)S(1)}, bf16[2,2,96,384]{3,2,1,0:T(8,128)(2,1)S(1)}, u32[]{:S(2)}, u32[]{:S(2)}) collective-permute-start(bf16[2,2,96,384]{3,2,1,0:T(8,128)(2,1)S(1)} %slice_bitcast_fusion.4), channel_id=1, source_target_pairs={{0,8},{4,12},{8,0},{12,4},{16,24},{20,28},{24,16},{28,20},{1,9},{5... | collective-permute-start | bytes 884744 | tf_op jit(solution)/shard_map/ppermute | solution.py:612
  206.9 27.4 %collective-permute-start.24 = (bf16[192,384]{1,0:T(8,128)(2,1)S(1)}, bf16[192,384]{1,0:T(8,128)(2,1)S(1)}, u32[]{:S(2)}, u32[]{:S(2)}) collective-permute-start(bf16[192,384]{1,0:T(8,128)(2,1)S(1)} %bitcast.145), channel_id=1, source_target_pairs={{0,8},{4,12},{8,0},{12,4},{16,24},{20,28},{24,16},{28,20},{1,9},{5... | collective-permute-start | bytes 442376 | tf_op jit(solution)/shard_map/ppermute | solution.py:612
  209.0 7.2 %collective-permute-start.58 = (bf16[2,2,96,384]{3,2,0,1:T(8,128)(2,1)S(1)}, bf16[2,2,96,384]{3,2,0,1:T(8,128)(2,1)S(1)}, u32[]{:S(2)}, u32[]{:S(2)}) collective-permute-start(bf16[2,2,96,384]{3,2,0,1:T(8,128)(2,1)S(1)} %fusion.22), channel_id=1, source_target_pairs={{0,1},{1,0},{2,3},{3,2},{4,5},{5,4},{6,7},{7,6},{8,9},{9,8},{10,11... | collective-permute-start | bytes 884744 | tf_op jit(solution)/shard_map/ppermute | solution.py:615
  216.2 6.8 %collective-permute-start.43 = (bf16[2,2,96,384]{3,2,0,1:T(8,128)(2,1)S(1)}, bf16[2,2,96,384]{3,2,0,1:T(8,128)(2,1)S(1)}, u32[]{:S(2)}, u32[]{:S(2)}) collective-permute-start(bf16[2,2,96,384]{3,2,0,1:T(8,128)(2,1)S(1)} %fusion.23), channel_id=1, source_target_pairs={{0,1},{1,0},{2,3},{3,2},{4,5},{5,4},{6,7},{7,6},{8,9},{9,8},{10,11... | collective-permute-start | bytes 884744 | tf_op jit(solution)/shard_map/ppermute | solution.py:615
  223.0 11.2 %collective-permute-start.59 = (bf16[2,96,384]{2,1,0:T(8,128)(2,1)S(1)}, bf16[2,96,384]{2,1,0:T(8,128)(2,1)S(1)}, u32[]{:S(2)}, u32[]{:S(2)}) collective-permute-start(bf16[2,96,384]{2,1,0:T(8,128)(2,1)S(1)} %slice_bitcast_fusion.12), channel_id=1, source_target_pairs={{0,2},{1,3},{2,0},{3,1},{4,6},{5,7},{6,4},{7,5},{8,10},{9,11},{10,... | collective-permute-start | bytes 442376 | tf_op jit(solution)/shard_map/ppermute | solution.py:615
  227.5 7.2 %collective-permute-start.25 = (bf16[192,384]{1,0:T(8,128)(2,1)S(1)}, bf16[192,384]{1,0:T(8,128)(2,1)S(1)}, u32[]{:S(2)}, u32[]{:S(2)}) collective-permute-start(bf16[192,384]{1,0:T(8,128)(2,1)S(1)} %bitcast.146), channel_id=1, source_target_pairs={{0,24},{4,28},{8,16},{12,20},{16,8},{20,12},{24,0},{28,4},{1,25},{... | collective-permute-start | bytes 442376 | tf_op jit(solution)/shard_map/ppermute | solution.py:612
  234.2 8.7 %collective-permute-start.26 = (bf16[192,384]{1,0:T(8,128)(2,1)S(1)}, bf16[192,384]{1,0:T(8,128)(2,1)S(1)}, u32[]{:S(2)}, u32[]{:S(2)}) collective-permute-start(bf16[192,384]{1,0:T(8,128)(2,1)S(1)} %bitcast.147), channel_id=1, source_target_pairs={{0,4},{4,0},{8,12},{12,8},{16,20},{20,16},{24,28},{28,24},{1,5},{5... | collective-permute-start | bytes 442376 | tf_op jit(solution)/shard_map/ppermute | solution.py:612
  234.3 9.6 %collective-permute-start.27 = (bf16[192,384]{1,0:T(8,128)(2,1)S(1)}, bf16[192,384]{1,0:T(8,128)(2,1)S(1)}, u32[]{:S(2)}, u32[]{:S(2)}) collective-permute-start(bf16[192,384]{1,0:T(8,128)(2,1)S(1)} %collective-permute-done.23.refs_1_), channel_id=1, source_target_pairs={{0,4},{4,0},{8,12},{12,8},{16,20},{20,16},{24,28},{28,24},{1,5},{5... | collective-permute-start | bytes 442376 | tf_op jit(solution)/shard_map/ppermute | solution.py:612
  234.8 9.7 %collective-permute-start.28 = (bf16[192,384]{1,0:T(8,128)(2,1)S(1)}, bf16[192,384]{1,0:T(8,128)(2,1)S(1)}, u32[]{:S(2)}, u32[]{:S(2)}) collective-permute-start(bf16[192,384]{1,0:T(8,128)(2,1)S(1)} %collective-permute-done.24.refs_2_), channel_id=1, source_target_pairs={{0,4},{4,0},{8,12},{12,8},{16,20},{20,16},{24,28},{28,24},{1,5},{5... | collective-permute-start | bytes 442376 | tf_op jit(solution)/shard_map/ppermute | solution.py:612
  240.8 7.0 %collective-permute-start.60 = (bf16[192,384]{1,0:T(8,128)(2,1)S(1)}, bf16[192,384]{1,0:T(8,128)(2,1)S(1)}, u32[]{:S(2)}, u32[]{:S(2)}) collective-permute-start(bf16[192,384]{1,0:T(8,128)(2,1)S(1)} %bitcast.149), channel_id=1, source_target_pairs={{0,16},{4,20},{8,24},{12,28},{16,0},{20,4},{24,8},{28,12},{1,17},{... | collective-permute-start | bytes 442376 | tf_op jit(solution)/shard_map/ppermute | solution.py:612
  243.9 8.4 %collective-permute-start.62 = (bf16[192,384]{1,0:T(8,128)(2,1)S(1)}, bf16[192,384]{1,0:T(8,128)(2,1)S(1)}, u32[]{:S(2)}, u32[]{:S(2)}) collective-permute-start(bf16[192,384]{1,0:T(8,128)(2,1)S(1)} %bitcast.151), channel_id=1, source_target_pairs={{0,24},{4,28},{8,16},{12,20},{16,8},{20,12},{24,0},{28,4},{1,25},{... | collective-permute-start | bytes 442376 | tf_op jit(solution)/shard_map/ppermute | solution.py:612
  244.4 7.9 %collective-permute-start.63 = (bf16[192,384]{1,0:T(8,128)(2,1)S(1)}, bf16[192,384]{1,0:T(8,128)(2,1)S(1)}, u32[]{:S(2)}, u32[]{:S(2)}) collective-permute-start(bf16[192,384]{1,0:T(8,128)(2,1)S(1)} %bitcast.152), channel_id=1, source_target_pairs={{0,4},{4,0},{8,12},{12,8},{16,20},{20,16},{24,28},{28,24},{1,5},{5... | collective-permute-start | bytes 442376 | tf_op jit(solution)/shard_map/ppermute | solution.py:612
  244.5 9.6 %collective-permute-start.45 = (bf16[192,384]{1,0:T(8,128)(2,1)S(1)}, bf16[192,384]{1,0:T(8,128)(2,1)S(1)}, u32[]{:S(2)}, u32[]{:S(2)}) collective-permute-start(bf16[192,384]{1,0:T(8,128)(2,1)S(1)} %bitcast.154), channel_id=1, source_target_pairs={{0,16},{4,20},{8,24},{12,28},{16,0},{20,4},{24,8},{28,12},{1,17},{... | collective-permute-start | bytes 442376 | tf_op jit(solution)/shard_map/ppermute | solution.py:612
  247.8 8.5 %collective-permute-start.46 = (bf16[192,384]{1,0:T(8,128)(2,1)S(1)}, bf16[192,384]{1,0:T(8,128)(2,1)S(1)}, u32[]{:S(2)}, u32[]{:S(2)}) collective-permute-start(bf16[192,384]{1,0:T(8,128)(2,1)S(1)} %bitcast.155), channel_id=1, source_target_pairs={{0,8},{4,12},{8,0},{12,4},{16,24},{20,28},{24,16},{28,20},{1,9},{5... | collective-permute-start | bytes 442376 | tf_op jit(solution)/shard_map/ppermute | solution.py:612
  249.6 8.6 %collective-permute-start.47 = (bf16[192,384]{1,0:T(8,128)(2,1)S(1)}, bf16[192,384]{1,0:T(8,128)(2,1)S(1)}, u32[]{:S(2)}, u32[]{:S(2)}) collective-permute-start(bf16[192,384]{1,0:T(8,128)(2,1)S(1)} %bitcast.156), channel_id=1, source_target_pairs={{0,24},{4,28},{8,16},{12,20},{16,8},{20,12},{24,0},{28,4},{1,25},{... | collective-permute-start | bytes 442376 | tf_op jit(solution)/shard_map/ppermute | solution.py:612
  (53 other events, 403.9 us)
